TPU v7x, 32 devices: a whole 2x2x4 slice. The times are simulated.
32 devices in a mesh: gx: 2 (over core), gy: 16 (over z, y, x).
Axes of the slice: x: 2, y: 2, z: 4, core: 2. Of those that a mesh axis runs over, the one named last changes fastest.
Arguments:
- frame_input: bfloat16 [8192, 1024], P(('gx', 'gy')), may hold values from -6 to 6
- code_embed: bfloat16 [8192, 3, 1024], P(('gx', 'gy')), may hold values from -6 to 6
- segment_ids: int32 [32, 256], P(('gx', 'gy')), may hold values from 0 to 3, never falling along the last dimension, each value on 1 to 128 neighbouring positions
- frame_cotangent: bfloat16 [8192, 1024], P(('gx', 'gy')), may hold values from -6 to 6
- code_cotangent: bfloat16 [8192, 3, 1024], P(('gx', 'gy')), may hold values from -6 to 6
- frame_prenorm: bfloat16 [1024], P(('gx', 'gy')), may hold values from 0.5 to 1.5
- frame_query: bfloat16 [1024, 1024], P(('gx', 'gy')), may hold values from -0.1875 to 0.1875
- frame_keys: bfloat16 [1024, 1024], P(('gx', 'gy')), may hold values from -0.1875 to 0.1875
- frame_values: bfloat16 [1024, 1024], P(('gx', 'gy')), may hold values from -0.1875 to 0.1875
- frame_outproj: bfloat16 [1024, 1024], P(('gx', 'gy')), may hold values from -0.75 to 0.75
- frame_midnorm: bfloat16 [1024], P(('gx', 'gy')), may hold values from 0.5 to 1.5
- frame_upproj: bfloat16 [1024, 4096], P(('gx', 'gy')), may hold values from -0.1875 to 0.1875
- frame_upbias: bfloat16 [4096], P(('gx', 'gy')), may hold values from -3 to 3
- frame_downproj: bfloat16 [4096, 1024], P(('gx', 'gy')), may hold values from -0.09375 to 0.09375
- frame_downbias: bfloat16 [1024], P(('gx', 'gy')), may hold values from -3 to 3
- code_prenorm: bfloat16 [1024], P(('gx', 'gy')), may hold values from 0.5 to 1.5
- code_query: bfloat16 [1024, 1024], P(('gx', 'gy')), may hold values from -0.1875 to 0.1875
- code_keys: bfloat16 [1024, 1024], P(('gx', 'gy')), may hold values from -0.1875 to 0.1875
- code_values: bfloat16 [1024, 1024], P(('gx', 'gy')), may hold values from -0.1875 to 0.1875
- code_outproj: bfloat16 [1024, 1024], P(('gx', 'gy')), may hold values from -0.25 to 0.25
- code_midnorm: bfloat16 [1024], P(('gx', 'gy')), may hold values from 0.5 to 1.5
- code_upproj: bfloat16 [1024, 4096], P(('gx', 'gy')), may hold values from -0.1875 to 0.1875
- code_upbias: bfloat16 [4096], P(('gx', 'gy')), may hold values from -3 to 3
- code_downproj: bfloat16 [4096, 1024], P(('gx', 'gy')), may hold values from -0.09375 to 0.09375
- code_downbias: bfloat16 [1024], P(('gx', 'gy')), may hold values from -3 to 3
Outputs:
- frame_output: bfloat16 [8192, 1024], P(('gx', 'gy'))
- code_output: bfloat16 [8192, 3, 1024], P(('gx', 'gy'))
- frame_input_grad: float32 [8192, 1024], P(('gx', 'gy'))
- code_embed_grad: float32 [8192, 3, 1024], P(('gx', 'gy'))
- frame_prenorm_grad: float32 [1024], P(('gx', 'gy'))
- frame_query_grad: float32 [1024, 1024], P(('gx', 'gy'))
- frame_keys_grad: float32 [1024, 1024], P(('gx', 'gy'))
- frame_values_grad: float32 [1024, 1024], P(('gx', 'gy'))
- frame_outproj_grad: float32 [1024, 1024], P(('gx', 'gy'))
- frame_midnorm_grad: float32 [1024], P(('gx', 'gy'))
- frame_upproj_grad: float32 [1024, 4096], P(('gx', 'gy'))
- frame_upbias_grad: float32 [4096], P(('gx', 'gy'))
- frame_downproj_grad: float32 [4096, 1024], P(('gx', 'gy'))
- frame_downbias_grad: float32 [1024], P(('gx', 'gy'))
- code_prenorm_grad: float32 [1024], P(('gx', 'gy'))
- code_query_grad: float32 [1024, 1024], P(('gx', 'gy'))
- code_keys_grad: float32 [1024, 1024], P(('gx', 'gy'))
- code_values_grad: float32 [1024, 1024], P(('gx', 'gy'))
- code_outproj_grad: float32 [1024, 1024], P(('gx', 'gy'))
- code_midnorm_grad: float32 [1024], P(('gx', 'gy'))
- code_upproj_grad: float32 [1024, 4096], P(('gx', 'gy'))
- code_upbias_grad: float32 [4096], P(('gx', 'gy'))
- code_downproj_grad: float32 [4096, 1024], P(('gx', 'gy'))
- code_downbias_grad: float32 [1024], P(('gx', 'gy'))
Inputs may be any that keep to these rules, and one draw needn't show every extreme that they name: `segment_ids`: within each row of 256 frames the ids never fall; every segment covers 1 to 128 frames and one covers exactly 128.
All inputs are finite; a program needn't handle non-finite values.
Results may differ from a plain program's by a relative error of at most 0.025.
Values may be sent and summed in bfloat16 or wider, within the bound.
No kernel may reach another device: no remote copies, remote signals or barrier semaphores. Data moves between devices by JAX's collectives and lax.ppermute only.
A program may use at most 320 MiB of HBM per device.

v0:
```python
import jax
import jax.numpy as jnp
from jax import lax
from jax.sharding import PartitionSpec as P

D = 1024
HEADS = 16
HD = 64
CB = 3


def gelu_tanh(value):
    return (
        0.5
        * value
        * (1.0 + jnp.tanh(0.7978845608028654 * (value + 0.044715 * value * value * value)))
    )


def rms_scale(value, gain_vec):
    return value * lax.rsqrt(jnp.mean(value * value, axis=-1, keepdims=True) + 1e-05) * gain_vec


def over_rows(left, right):
    return lax.dot_general(
        left, right, (((0,), (0,)), ((), ())), preferred_element_type=jnp.float32
    )


def against(left, right):
    return lax.dot_general(
        left, right, (((1,), (1,)), ((), ())), preferred_element_type=jnp.float32
    )


def flat_grads(grads):
    return tuple(
        (grad_arr.reshape(-1, 128) if grad_arr.ndim == 2 else grad_arr for grad_arr in grads)
    )


def shaped_grads(shards, grads):
    return tuple(
        (
            shard_arr.reshape(-1, grad_arr.shape[1]) if grad_arr.ndim == 2 else shard_arr
            for shard_arr, grad_arr in zip(shards, grads)
        )
    )


def masked_scores(query, key_rows, allowed):
    scores = jnp.einsum(
        "glhe,gmhe->ghlm", query, key_rows, preferred_element_type=jnp.float32
    ) * HD ** (-0.5)
    return jnp.where(allowed[:, None], scores, -1e30)


def attend(query, key_rows, value_rows, allowed):
    scores = masked_scores(query, key_rows, allowed)
    highest = jnp.max(scores, axis=-1, keepdims=True)
    expo = jnp.exp(scores - highest)
    totals = jnp.sum(expo, axis=-1, keepdims=True)
    probs = expo / totals
    log_total = highest + jnp.log(totals)
    mixed = jnp.einsum(
        "ghlm,gmhe->glhe",
        probs.astype(jnp.bfloat16),
        value_rows,
        preferred_element_type=jnp.float32,
    )
    return (mixed.astype(jnp.bfloat16), log_total)


def attend_back(query, key_rows, value_rows, allowed, log_total, grad_mixed):
    probs = jnp.exp(masked_scores(query, key_rows, allowed) - log_total)
    grad_probs = jnp.einsum(
        "glhe,gmhe->ghlm", grad_mixed, value_rows, preferred_element_type=jnp.float32
    )
    grad_values = jnp.einsum(
        "ghlm,glhe->gmhe",
        probs.astype(jnp.bfloat16),
        grad_mixed,
        preferred_element_type=jnp.float32,
    )
    inner = jnp.sum(probs * grad_probs, axis=-1, keepdims=True)
    grad_scores = (probs * (grad_probs - inner)).astype(jnp.bfloat16)
    grad_query = jnp.einsum(
        "ghlm,gmhe->glhe", grad_scores, key_rows, preferred_element_type=jnp.float32
    ) * HD ** (-0.5)
    grad_keys = jnp.einsum(
        "ghlm,glhe->gmhe", grad_scores, query, preferred_element_type=jnp.float32
    ) * HD ** (-0.5)
    return (grad_query, grad_keys, grad_values)


def block_forward(x_in, allowed, params, groups):
    prenorm, w_query, w_key, w_value, w_out, midnorm, w_up, b_up, w_down, b_down = params
    row_count = x_in.shape[0]
    span = row_count // groups
    normed = rms_scale(x_in, prenorm.astype(jnp.float32)).astype(jnp.bfloat16)
    query = (
        jnp.dot(normed, w_query, preferred_element_type=jnp.float32)
        .astype(jnp.bfloat16)
        .reshape(groups, span, HEADS, HD)
    )
    key_rows = (
        jnp.dot(normed, w_key, preferred_element_type=jnp.float32)
        .astype(jnp.bfloat16)
        .reshape(groups, span, HEADS, HD)
    )
    value_rows = (
        jnp.dot(normed, w_value, preferred_element_type=jnp.float32)
        .astype(jnp.bfloat16)
        .reshape(groups, span, HEADS, HD)
    )
    mixed_heads, log_total = attend(query, key_rows, value_rows, allowed)
    mixed = mixed_heads.reshape(row_count, D)
    hidden = x_in + jnp.dot(mixed, w_out, preferred_element_type=jnp.float32)
    normed_two = rms_scale(hidden, midnorm.astype(jnp.float32)).astype(jnp.bfloat16)
    preact = jnp.dot(normed_two, w_up, preferred_element_type=jnp.float32) + b_up.astype(
        jnp.float32
    )
    activated = gelu_tanh(preact).astype(jnp.bfloat16)
    result = hidden + (
        jnp.dot(activated, w_down, preferred_element_type=jnp.float32) + b_down.astype(jnp.float32)
    )
    saved = (
        normed,
        query,
        key_rows,
        value_rows,
        log_total,
        mixed,
        hidden,
        normed_two,
        preact,
        activated,
    )
    return (result, saved)


def block_backward(grad_y, x_in, allowed, params, saved):
    prenorm, w_query, w_key, w_value, w_out, midnorm, w_up, b_up, w_down, b_down = params
    normed, query, key_rows, value_rows, log_total, mixed, hidden, normed_two, preact, activated = (
        saved
    )
    row_count = x_in.shape[0]
    grad_branch = grad_y.astype(jnp.bfloat16)
    grad_b_down = jnp.sum(grad_branch.astype(jnp.float32), axis=0)
    grad_w_down = over_rows(activated, grad_branch)
    grad_act = against(grad_branch, w_down)
    unused_value, gelu_back = jax.vjp(gelu_tanh, preact)
    grad_pre = gelu_back(grad_act)[0].astype(jnp.bfloat16)
    grad_b_up = jnp.sum(grad_pre.astype(jnp.float32), axis=0)
    grad_w_up = over_rows(normed_two, grad_pre)
    grad_normed_two = against(grad_pre, w_up)
    unused_mid, mid_back = jax.vjp(rms_scale, hidden, midnorm.astype(jnp.float32))
    grad_hidden_part, grad_midnorm = mid_back(grad_normed_two)
    grad_hidden = grad_y + grad_hidden_part
    grad_attn = grad_hidden.astype(jnp.bfloat16)
    grad_w_out = over_rows(mixed, grad_attn)
    grad_mixed = against(grad_attn, w_out).astype(jnp.bfloat16)
    grad_query, grad_keys, grad_values = attend_back(
        query, key_rows, value_rows, allowed, log_total, grad_mixed.reshape(query.shape)
    )
    grad_query = grad_query.reshape(row_count, D).astype(jnp.bfloat16)
    grad_keys = grad_keys.reshape(row_count, D).astype(jnp.bfloat16)
    grad_values = grad_values.reshape(row_count, D).astype(jnp.bfloat16)
    grad_w_query = over_rows(normed, grad_query)
    grad_w_key = over_rows(normed, grad_keys)
    grad_w_value = over_rows(normed, grad_values)
    grad_normed = (
        against(grad_query, w_query) + against(grad_keys, w_key) + against(grad_values, w_value)
    )
    unused_pre, pre_back = jax.vjp(rms_scale, x_in, prenorm.astype(jnp.float32))
    grad_x_part, grad_prenorm = pre_back(grad_normed)
    grad_x = grad_hidden + grad_x_part
    return (
        grad_x,
        (
            grad_prenorm,
            grad_w_query,
            grad_w_key,
            grad_w_value,
            grad_w_out,
            grad_midnorm,
            grad_w_up,
            grad_b_up,
            grad_w_down,
            grad_b_down,
        ),
    )


def local(
    frame_input,
    code_embed,
    segment_ids,
    frame_cotangent,
    code_cotangent,
    frame_prenorm,
    frame_query,
    frame_keys,
    frame_values,
    frame_outproj,
    frame_midnorm,
    frame_upproj,
    frame_upbias,
    frame_downproj,
    frame_downbias,
    code_prenorm,
    code_query,
    code_keys,
    code_values,
    code_outproj,
    code_midnorm,
    code_upproj,
    code_upbias,
    code_downproj,
    code_downbias,
):
    frame_count = frame_input.shape[0]
    frame_params = (
        lax.all_gather(frame_prenorm, ("gx", "gy"), axis=0, tiled=True),
        lax.all_gather(frame_query, ("gx", "gy"), axis=0, tiled=True),
        lax.all_gather(frame_keys, ("gx", "gy"), axis=0, tiled=True),
        lax.all_gather(frame_values, ("gx", "gy"), axis=0, tiled=True),
        lax.all_gather(frame_outproj, ("gx", "gy"), axis=0, tiled=True),
        lax.all_gather(frame_midnorm, ("gx", "gy"), axis=0, tiled=True),
        lax.all_gather(frame_upproj, ("gx", "gy"), axis=0, tiled=True),
        lax.all_gather(frame_upbias, ("gx", "gy"), axis=0, tiled=True),
        lax.all_gather(frame_downproj, ("gx", "gy"), axis=0, tiled=True),
        lax.all_gather(frame_downbias, ("gx", "gy"), axis=0, tiled=True),
    )
    place = jnp.arange(frame_count)
    segment_row = segment_ids[0]
    frame_allowed = (
        (segment_row[:, None] == segment_row[None, :]) & (place[:, None] >= place[None, :])
    )[None]
    frame_x = frame_input.astype(jnp.float32)
    frame_out, frame_saved = block_forward(frame_x, frame_allowed, frame_params, 1)
    code_params = (
        lax.all_gather(code_prenorm, ("gx", "gy"), axis=0, tiled=True),
        lax.all_gather(code_query, ("gx", "gy"), axis=0, tiled=True),
        lax.all_gather(code_keys, ("gx", "gy"), axis=0, tiled=True),
        lax.all_gather(code_values, ("gx", "gy"), axis=0, tiled=True),
        lax.all_gather(code_outproj, ("gx", "gy"), axis=0, tiled=True),
        lax.all_gather(code_midnorm, ("gx", "gy"), axis=0, tiled=True),
        lax.all_gather(code_upproj, ("gx", "gy"), axis=0, tiled=True),
        lax.all_gather(code_upbias, ("gx", "gy"), axis=0, tiled=True),
        lax.all_gather(code_downproj, ("gx", "gy"), axis=0, tiled=True),
        lax.all_gather(code_downbias, ("gx", "gy"), axis=0, tiled=True),
    )
    code_in = (code_embed.astype(jnp.float32) + frame_out[:, None, :]).reshape(frame_count * CB, D)
    code_place = jnp.arange(CB)
    code_allowed = (code_place[:, None] >= code_place[None, :])[None]
    code_out, code_saved = block_forward(code_in, code_allowed, code_params, frame_count)
    code_params_back = (
        lax.all_gather(code_prenorm, ("gx", "gy"), axis=0, tiled=True),
        lax.all_gather(code_query, ("gx", "gy"), axis=0, tiled=True),
        lax.all_gather(code_keys, ("gx", "gy"), axis=0, tiled=True),
        lax.all_gather(code_values, ("gx", "gy"), axis=0, tiled=True),
        lax.all_gather(code_outproj, ("gx", "gy"), axis=0, tiled=True),
        lax.all_gather(code_midnorm, ("gx", "gy"), axis=0, tiled=True),
        lax.all_gather(code_upproj, ("gx", "gy"), axis=0, tiled=True),
        lax.all_gather(code_upbias, ("gx", "gy"), axis=0, tiled=True),
        lax.all_gather(code_downproj, ("gx", "gy"), axis=0, tiled=True),
        lax.all_gather(code_downbias, ("gx", "gy"), axis=0, tiled=True),
    )
    grad_code_in, code_grads = block_backward(
        code_cotangent.astype(jnp.float32).reshape(frame_count * CB, D),
        code_in,
        code_allowed,
        code_params_back,
        code_saved,
    )
    code_flat = flat_grads(code_grads)
    code_sums = (
        lax.psum_scatter(code_flat[0], ("gx", "gy"), scatter_dimension=0, tiled=True),
        lax.psum_scatter(code_flat[1], ("gx", "gy"), scatter_dimension=0, tiled=True),
        lax.psum_scatter(code_flat[2], ("gx", "gy"), scatter_dimension=0, tiled=True),
        lax.psum_scatter(code_flat[3], ("gx", "gy"), scatter_dimension=0, tiled=True),
        lax.psum_scatter(code_flat[4], ("gx", "gy"), scatter_dimension=0, tiled=True),
        lax.psum_scatter(code_flat[5], ("gx", "gy"), scatter_dimension=0, tiled=True),
        lax.psum_scatter(code_flat[6], ("gx", "gy"), scatter_dimension=0, tiled=True),
        lax.psum_scatter(code_flat[7], ("gx", "gy"), scatter_dimension=0, tiled=True),
        lax.psum_scatter(code_flat[8], ("gx", "gy"), scatter_dimension=0, tiled=True),
        lax.psum_scatter(code_flat[9], ("gx", "gy"), scatter_dimension=0, tiled=True),
    )
    code_shards = shaped_grads(code_sums, code_grads)
    grad_code_rows = grad_code_in.reshape(frame_count, CB, D)
    frame_grad_y = frame_cotangent.astype(jnp.float32) + jnp.sum(grad_code_rows, axis=1)
    frame_params_back = (
        lax.all_gather(frame_prenorm, ("gx", "gy"), axis=0, tiled=True),
        lax.all_gather(frame_query, ("gx", "gy"), axis=0, tiled=True),
        lax.all_gather(frame_keys, ("gx", "gy"), axis=0, tiled=True),
        lax.all_gather(frame_values, ("gx", "gy"), axis=0, tiled=True),
        lax.all_gather(frame_outproj, ("gx", "gy"), axis=0, tiled=True),
        lax.all_gather(frame_midnorm, ("gx", "gy"), axis=0, tiled=True),
        lax.all_gather(frame_upproj, ("gx", "gy"), axis=0, tiled=True),
        lax.all_gather(frame_upbias, ("gx", "gy"), axis=0, tiled=True),
        lax.all_gather(frame_downproj, ("gx", "gy"), axis=0, tiled=True),
        lax.all_gather(frame_downbias, ("gx", "gy"), axis=0, tiled=True),
    )
    grad_frame_in, frame_grads = block_backward(
        frame_grad_y, frame_x, frame_allowed, frame_params_back, frame_saved
    )
    frame_flat = flat_grads(frame_grads)
    frame_sums = (
        lax.psum_scatter(frame_flat[0], ("gx", "gy"), scatter_dimension=0, tiled=True),
        lax.psum_scatter(frame_flat[1], ("gx", "gy"), scatter_dimension=0, tiled=True),
        lax.psum_scatter(frame_flat[2], ("gx", "gy"), scatter_dimension=0, tiled=True),
        lax.psum_scatter(frame_flat[3], ("gx", "gy"), scatter_dimension=0, tiled=True),
        lax.psum_scatter(frame_flat[4], ("gx", "gy"), scatter_dimension=0, tiled=True),
        lax.psum_scatter(frame_flat[5], ("gx", "gy"), scatter_dimension=0, tiled=True),
        lax.psum_scatter(frame_flat[6], ("gx", "gy"), scatter_dimension=0, tiled=True),
        lax.psum_scatter(frame_flat[7], ("gx", "gy"), scatter_dimension=0, tiled=True),
        lax.psum_scatter(frame_flat[8], ("gx", "gy"), scatter_dimension=0, tiled=True),
        lax.psum_scatter(frame_flat[9], ("gx", "gy"), scatter_dimension=0, tiled=True),
    )
    frame_shards = shaped_grads(frame_sums, frame_grads)
    return (
        (
            frame_out.astype(jnp.bfloat16),
            code_out.reshape(frame_count, CB, D).astype(jnp.bfloat16),
            grad_frame_in,
            grad_code_rows,
        )
        + tuple(frame_shards)
        + tuple(code_shards)
    )


def solution(mesh):
    in_specs = (
        P(("gx", "gy"), None),
        P(("gx", "gy"), None, None),
        P(("gx", "gy"), None),
        P(("gx", "gy"), None),
        P(("gx", "gy"), None, None),
        P(("gx", "gy")),
        P(("gx", "gy"), None),
        P(("gx", "gy"), None),
        P(("gx", "gy"), None),
        P(("gx", "gy"), None),
        P(("gx", "gy")),
        P(("gx", "gy"), None),
        P(("gx", "gy")),
        P(("gx", "gy"), None),
        P(("gx", "gy")),
        P(("gx", "gy")),
        P(("gx", "gy"), None),
        P(("gx", "gy"), None),
        P(("gx", "gy"), None),
        P(("gx", "gy"), None),
        P(("gx", "gy")),
        P(("gx", "gy"), None),
        P(("gx", "gy")),
        P(("gx", "gy"), None),
        P(("gx", "gy")),
    )
    out_specs = (
        P(("gx", "gy"), None),
        P(("gx", "gy"), None, None),
        P(("gx", "gy"), None),
        P(("gx", "gy"), None, None),
        P(("gx", "gy")),
        P(("gx", "gy"), None),
        P(("gx", "gy"), None),
        P(("gx", "gy"), None),
        P(("gx", "gy"), None),
        P(("gx", "gy")),
        P(("gx", "gy"), None),
        P(("gx", "gy")),
        P(("gx", "gy"), None),
        P(("gx", "gy")),
        P(("gx", "gy")),
        P(("gx", "gy"), None),
        P(("gx", "gy"), None),
        P(("gx", "gy"), None),
        P(("gx", "gy"), None),
        P(("gx", "gy")),
        P(("gx", "gy"), None),
        P(("gx", "gy")),
        P(("gx", "gy"), None),
        P(("gx", "gy")),
    )
    return jax.shard_map(local, mesh=mesh, in_specs=in_specs, out_specs=out_specs, check_vma=False)
```

profile of v0, /device:TPU:0, one launch (start us, length us, event | category | flops | bytes accessed | tf_op | source)
XLA Modules:
  0.0 3604.5 jit_solution(1238141287911359872)
XLA Ops:
  20.4 42.3 %all-reduce.15 = (bf16[1024]{0:T(1024)(128)(2,1)S(1)}, bf16[1024]{0:T(1024)(128)(2,1)S(1)}, bf16[1024]{0:T(1024)(128)(2,1)S(1)}, bf16[1024]{0:T(1024)(128)(2,1)S...) all-reduce(bf16[1024]{0:T(1024)(128)(2,1)S(1)} %dynamic-update-slic, ...), channel_id=1, replica_groups=mesh['gx'=2,'gy'=16] {'gx','gy'}, use_global_device_ids=true, to_apply=%add | all-reduce | flops 6144 | bytes 24576
  62.7 66.1 %all-gather = bf16[32,1,128]{2,1,0:T(2,128)(2,1)S(1)} all-gather(bf16[1,1,128]{2,1,0:T(2,128)(2,1)} %bitcast.132), channel_id=1, replica_groups=mesh['gx'=2,'gy'=16] {'gx','gy'}, dimensions={0}, use_global_device_ids=true | all-gather | bytes 8448 | tf_op jit(solution)/shard_map/all_gather | solution.py:231
  128.9 63.2 %all-gather.1 = bf16[32,1,128]{2,1,0:T(2,128)(2,1)S(1)} all-gather(bf16[1,1,128]{2,1,0:T(2,128)(2,1)} %bitcast.133), channel_id=1, replica_groups=mesh['gx'=2,'gy'=16] {'gx','gy'}, dimensions={0}, use_global_device_ids=true | all-gather | bytes 8448 | tf_op jit(solution)/shard_map/all_gather | solution.py:250
  216.1 28.8 all-gather.21.cloned.1.call-done
  248.1 76.0 %all-gather.23.cloned.1.call-done = bf16[1024,4096]{1,0:T(8,128)(2,1)} async-done(((bf16[32,4096]{1,0:T(8,128)(2,1)}), bf16[1024,4096]{1,0:T(8,128)(2,1)}) %all-gather.23.cloned.1.call-update) | async-done | bytes 8388624 | tf_op jit(solution)/shard_map/all_gather | solution.py:230
  331.9 71.1 %all-gather.25.cloned.1.call-done = bf16[4096,1024]{1,0:T(8,128)(2,1)} async-done(((bf16[128,1024]{1,0:T(8,128)(2,1)}), bf16[4096,1024]{1,0:T(8,128)(2,1)}) %all-gather.25.cloned.1.call-update) | async-done | bytes 8388624 | tf_op jit(solution)/shard_map/all_gather | solution.py:232
  424.4 36.5 %all-gather.31.cloned.1.call-done = bf16[1024,1024]{1,0:T(8,128)(2,1)} async-done(((bf16[32,1024]{1,0:T(8,128)(2,1)}), bf16[1024,1024]{1,0:T(8,128)(2,1)}) %all-gather.31.cloned.1.call-update) | async-done | bytes 2097168 | tf_op jit(solution)/shard_map/all_gather | solution.py:245
  471.2 47.9 %all-gather.29.cloned.1.call-done = bf16[1024,1024]{1,0:T(8,128)(2,1)} async-done(((bf16[32,1024]{1,0:T(8,128)(2,1)}), bf16[1024,1024]{1,0:T(8,128)(2,1)}) %all-gather.29.cloned.1.call-update) | async-done | bytes 2097168 | tf_op jit(solution)/shard_map/all_gather | solution.py:244
  551.6 25.6 all-gather.27.cloned.1.call-done
  602.2 33.0 all-gather.33.cloned.1.call-done
  640.7 73.8 %all-gather.35.cloned.1.call-done = bf16[1024,4096]{1,0:T(8,128)(2,1)} async-done(((bf16[32,4096]{1,0:T(8,128)(2,1)}), bf16[1024,4096]{1,0:T(8,128)(2,1)}) %all-gather.35.cloned.1.call-update) | async-done | bytes 8388624 | tf_op jit(solution)/shard_map/all_gather | solution.py:249
  727.3 66.1 %all-gather.37.cloned.1.call-done = bf16[4096,1024]{1,0:T(8,128)(2,1)} async-done(((bf16[128,1024]{1,0:T(8,128)(2,1)}), bf16[4096,1024]{1,0:T(8,128)(2,1)}) %all-gather.37.cloned.1.call-update) | async-done | bytes 8388624 | tf_op jit(solution)/shard_map/all_gather | solution.py:251
  793.4 23.7 convert_reduce_fusion
  1217.4 40.7 %all-reduce.14 = (f32[1024]{0:T(1024)S(1)}, f32[1024]{0:T(1024)S(1)}, f32[4096]{0:T(1024)S(1)}, f32[1024]{0:T(1024)S(1)}, f32[1024]{0:T(1024)S(1)}, /*index=5*/f...) all-reduce(f32[1024]{0:T(1024)S(1)} %get-tuple-element.126, ...), channel_id=2, replica_groups=mesh['gx'=2,'gy'=16] {'gx','gy'}, use_global_device_ids=true, to_apply=%region_16.17.clone | all-reduce | flops 14336 | bytes 114688
  1270.4 146.8 %reduce-scatter.17.cloned.1.call-done = f32[256,128]{1,0:T(8,128)} async-done(((f32[8192,128]{1,0:T(8,128)}), f32[256,128]{1,0:T(8,128)}) %reduce-scatter.17.cloned.1.call-update) | async-done | bytes 131088 | tf_op jit(solution)/shard_map/reduce_scatter | solution.py:313
  1418.8 144.3 %reduce-scatter.19.cloned.1.call-done = f32[256,128]{1,0:T(8,128)} async-done(((f32[8192,128]{1,0:T(8,128)}), f32[256,128]{1,0:T(8,128)}) %reduce-scatter.19.cloned.1.call-update) | async-done | bytes 131088 | tf_op jit(solution)/shard_map/reduce_scatter | solution.py:314
  1564.6 146.0 %reduce-scatter.25.cloned.1.call-done = f32[256,128]{1,0:T(8,128)} async-done(((f32[8192,128]{1,0:T(8,128)}), f32[256,128]{1,0:T(8,128)}) %reduce-scatter.25.cloned.1.call-update) | async-done | bytes 131088 | tf_op jit(solution)/shard_map/reduce_scatter | solution.py:280
  1712.2 145.9 %reduce-scatter.27.cloned.1.call-done = f32[256,128]{1,0:T(8,128)} async-done(((f32[8192,128]{1,0:T(8,128)}), f32[256,128]{1,0:T(8,128)}) %reduce-scatter.27.cloned.1.call-update) | async-done | bytes 131088 | tf_op jit(solution)/shard_map/reduce_scatter | solution.py:281
  1859.7 143.5 %reduce-scatter.29.cloned.1.call-done = f32[256,128]{1,0:T(8,128)} async-done(((f32[8192,128]{1,0:T(8,128)}), f32[256,128]{1,0:T(8,128)}) %reduce-scatter.29.cloned.1.call-update) | async-done | bytes 131088 | tf_op jit(solution)/shard_map/reduce_scatter | solution.py:282
  2004.9 143.6 %reduce-scatter.31.cloned.1.call-done = f32[256,128]{1,0:T(8,128)} async-done(((f32[8192,128]{1,0:T(8,128)}), f32[256,128]{1,0:T(8,128)}) %reduce-scatter.31.cloned.1.call-update) | async-done | bytes 131088 | tf_op jit(solution)/shard_map/reduce_scatter | solution.py:283
  2150.0 358.4 %reduce-scatter.21.cloned.1.call-done = f32[1024,128]{1,0:T(8,128)} async-done(((f32[32768,128]{1,0:T(8,128)}), f32[1024,128]{1,0:T(8,128)}) %reduce-scatter.21.cloned.1.call-update) | async-done | bytes 524304 | tf_op jit(solution)/shard_map/reduce_scatter | solution.py:316
  2510.3 360.4 %reduce-scatter.23.cloned.1.call-done = f32[1024,128]{1,0:T(8,128)} async-done(((f32[32768,128]{1,0:T(8,128)}), f32[1024,128]{1,0:T(8,128)}) %reduce-scatter.23.cloned.1.call-update) | async-done | bytes 524304 | tf_op jit(solution)/shard_map/reduce_scatter | solution.py:318
  2872.6 360.4 %reduce-scatter.33.cloned.1.call-done = f32[1024,128]{1,0:T(8,128)} async-done(((f32[32768,128]{1,0:T(8,128)}), f32[1024,128]{1,0:T(8,128)}) %reduce-scatter.33.cloned.1.call-update) | async-done | bytes 524304 | tf_op jit(solution)/shard_map/reduce_scatter | solution.py:285
  3235.0 360.3 %reduce-scatter.35.cloned.1.call-done = f32[1024,128]{1,0:T(8,128)} async-done(((f32[32768,128]{1,0:T(8,128)}), f32[1024,128]{1,0:T(8,128)}) %reduce-scatter.35.cloned.1.call-update) | async-done | bytes 524304 | tf_op jit(solution)/shard_map/reduce_scatter | solution.py:287
  (392 shorter events, 584.1 us)
Async XLA Ops:
  7.2 196.9 %all-gather.15.cloned.1.call-start = ((), (), s32[]{:S(2)}) async-start(), calls=%async_computation.12 | async-start | bytes 2162688 | tf_op jit(solution)/shard_map/all_gather | solution.py:227
  7.9 198.8 %all-gather.17.cloned.1.call-start = ((), (), s32[]{:S(2)}) async-start(), calls=%async_computation.13 | async-start | bytes 2162688 | tf_op jit(solution)/shard_map/all_gather | solution.py:225
  8.7 200.8 %all-gather.19.cloned.1.call-start = ((), (), s32[]{:S(2)}) async-start(), calls=%async_computation.14 | async-start | bytes 2162688 | tf_op jit(solution)/shard_map/all_gather | solution.py:226
  9.4 235.5 %all-gather.21.cloned.1.call-start = ((), (), s32[]{:S(2)}) async-start(), calls=%async_computation.15 | async-start | bytes 2162688 | tf_op jit(solution)/shard_map/all_gather | solution.py:228
  10.0 314.1 %all-gather.23.cloned.1.call-start = ((), (), s32[]{:S(2)}) async-start(), calls=%async_computation.16 | async-start | bytes 8650752 | tf_op jit(solution)/shard_map/all_gather | solution.py:230
  10.6 392.4 %all-gather.25.cloned.1.call-start = ((), (), s32[]{:S(2)}) async-start(), calls=%async_computation.17 | async-start | bytes 8650752 | tf_op jit(solution)/shard_map/all_gather | solution.py:232
  11.1 449.8 %all-gather.31.cloned.1.call-start = ((), (), s32[]{:S(2)}) async-start(), calls=%async_computation.20 | async-start | bytes 2162688 | tf_op jit(solution)/shard_map/all_gather | solution.py:245
  11.9 507.1 %all-gather.29.cloned.1.call-start = ((), (), s32[]{:S(2)}) async-start(), calls=%async_computation.19 | async-start | bytes 2162688 | tf_op jit(solution)/shard_map/all_gather | solution.py:244
  12.6 564.6 %all-gather.27.cloned.1.call-start = ((), (), s32[]{:S(2)}) async-start(), calls=%async_computation.18 | async-start | bytes 2162688 | tf_op jit(solution)/shard_map/all_gather | solution.py:246
  13.4 621.8 %all-gather.33.cloned.1.call-start = ((), (), s32[]{:S(2)}) async-start(), calls=%async_computation.21 | async-start | bytes 2162688 | tf_op jit(solution)/shard_map/all_gather | solution.py:247
  14.0 700.5 %all-gather.35.cloned.1.call-start = ((), (), s32[]{:S(2)}) async-start(), calls=%async_computation.22 | async-start | bytes 8650752 | tf_op jit(solution)/shard_map/all_gather | solution.py:249
  14.7 778.7 %all-gather.37.cloned.1.call-start = ((), (), s32[]{:S(2)}) async-start(), calls=%async_computation.23 | async-start | bytes 8650752 | tf_op jit(solution)/shard_map/all_gather | solution.py:251
  15.3 1248.8 %reduce-scatter.13.cloned.1.call-start = ((), (), s32[]{:S(2)}) async-start(), calls=%async_computation.24 | async-start | bytes 4325376 | tf_op jit(solution)/shard_map/reduce_scatter | solution.py:311
  977.3 291.5 %reduce-scatter.15.cloned.1.call-start = ((), (), s32[]{:S(2)}) async-start(), calls=%async_computation.25 | async-start | bytes 4325376 | tf_op jit(solution)/shard_map/reduce_scatter | solution.py:312
  987.7 429.5 %reduce-scatter.17.cloned.1.call-start = ((), (), s32[]{:S(2)}) async-start(), calls=%async_computation.26 | async-start | bytes 4325376 | tf_op jit(solution)/shard_map/reduce_scatter | solution.py:313
  999.5 563.6 %reduce-scatter.19.cloned.1.call-start = ((), (), s32[]{:S(2)}) async-start(), calls=%async_computation.27 | async-start | bytes 4325376 | tf_op jit(solution)/shard_map/reduce_scatter | solution.py:314
  1008.5 702.1 %reduce-scatter.25.cloned.1.call-start = ((), (), s32[]{:S(2)}) async-start(), calls=%async_computation.30 | async-start | bytes 4325376 | tf_op jit(solution)/shard_map/reduce_scatter | solution.py:280
  1024.8 833.3 %reduce-scatter.27.cloned.1.call-start = ((), (), s32[]{:S(2)}) async-start(), calls=%async_computation.31 | async-start | bytes 4325376 | tf_op jit(solution)/shard_map/reduce_scatter | solution.py:281
  1035.6 967.7 %reduce-scatter.29.cloned.1.call-start = ((), (), s32[]{:S(2)}) async-start(), calls=%async_computation.32 | async-start | bytes 4325376 | tf_op jit(solution)/shard_map/reduce_scatter | solution.py:282
  1045.9 1102.5 %reduce-scatter.31.cloned.1.call-start = ((), (), s32[]{:S(2)}) async-start(), calls=%async_computation.33 | async-start | bytes 4325376 | tf_op jit(solution)/shard_map/reduce_scatter | solution.py:283
  1058.1 1450.3 %reduce-scatter.21.cloned.1.call-start = ((), (), s32[]{:S(2)}) async-start(), calls=%async_computation.28 | async-start | bytes 17301504 | tf_op jit(solution)/shard_map/reduce_scatter | solution.py:316
  1086.3 1784.4 %reduce-scatter.23.cloned.1.call-start = ((), (), s32[]{:S(2)}) async-start(), calls=%async_computation.29 | async-start | bytes 17301504 | tf_op jit(solution)/shard_map/reduce_scatter | solution.py:318
  1116.2 2116.9 %reduce-scatter.33.cloned.1.call-start = ((), (), s32[]{:S(2)}) async-start(), calls=%async_computation.34 | async-start | bytes 17301504 | tf_op jit(solution)/shard_map/reduce_scatter | solution.py:285
  1149.4 2445.9 %reduce-scatter.35.cloned.1.call-start = ((), (), s32[]{:S(2)}) async-start(), calls=%async_computation.35 | async-start | bytes 17301504 | tf_op jit(solution)/shard_map/reduce_scatter | solution.py:287
  (88 other events, 3080.6 us)
Sparse Core Ops, SparseCore 0:
  10.9 59.5 all-gather.14
  73.4 55.3 all-gather.16
  131.6 55.2 all-gather.18
  189.7 55.2 all-gather.20
  247.7 76.3 all-gather.22
  326.8 76.1 all-gather.24
  405.9 54.9 all-gather.30
  463.8 55.2 all-gather.28
  521.9 55.2 all-gather.26
  579.9 55.2 all-gather.32
  638.1 76.3 all-gather.34
  717.2 76.1 all-gather.36
  977.4 142.9 reduce-scatter.12
  1122.5 146.2 reduce-scatter.14
  1270.9 146.1 reduce-scatter.16
  1419.3 143.7 reduce-scatter.18
  1565.2 145.4 reduce-scatter.24
  1712.8 145.3 reduce-scatter.26
  1860.4 142.8 reduce-scatter.28
  2005.4 143.0 reduce-scatter.30
  2150.7 357.6 reduce-scatter.20
  2510.7 359.9 reduce-scatter.22
  2873.0 360.0 reduce-scatter.32
  3235.2 360.0 reduce-scatter.34
where the time goes:
time: 3620 us; the launch traced here: 3600 us
  waiting for transfers between devices  2780 us (77%)
  local copies, waits for them, and re-layouts  297 us (8%)
  matrix products  280 us (8%)
  blocking collectives  212 us (6%)
    reduce_scatter x1, waiting for transfers between devices, local(): lax.psum_scatter(code_flat[6], ('gx', 'gy'), scatter_dimension=0, tiled=T...  360 us
    reduce_scatter x1, waiting for transfers between devices, local(): lax.psum_scatter(frame_flat[8], ('gx', 'gy'), scatter_dimension=0, tiled=...  360 us
    reduce_scatter x1, waiting for transfers between devices, local(): lax.psum_scatter(code_flat[8], ('gx', 'gy'), scatter_dimension=0, tiled=T...  360 us
    reduce_scatter x1, waiting for transfers between devices, local(): lax.psum_scatter(frame_flat[6], ('gx', 'gy'), scatter_dimension=0, tiled=...  358 us
    reduce_scatter x1, waiting for transfers between devices, local(): lax.psum_scatter(frame_flat[3], ('gx', 'gy'), scatter_dimension=0, tiled=...  147 us
    reduce_scatter x1, waiting for transfers between devices, local(): lax.psum_scatter(code_flat[1], ('gx', 'gy'), scatter_dimension=0, tiled=T...  146 us
    reduce_scatter x1, waiting for transfers between devices, local(): lax.psum_scatter(code_flat[2], ('gx', 'gy'), scatter_dimension=0, tiled=T...  146 us
    reduce_scatter x1, waiting for transfers between devices, local(): lax.psum_scatter(frame_flat[4], ('gx', 'gy'), scatter_dimension=0, tiled=...  144 us
  transfers between devices with their start and end apart: 24, of which 20 were waited for; matrix products, arithmetic and copies ran while one was open for 11% of the time, Pallas kernels for 0%

commit v1 on v0

v1 whole, which is shorter than its diff:
```python
import functools

import jax
import jax.numpy as jnp
from jax import lax
from jax.sharding import PartitionSpec as P

D = 1024
HEADS = 16
HD = 64
CB = 3


def gelu_tanh(value):
    return (
        0.5
        * value
        * (1.0 + jnp.tanh(0.7978845608028654 * (value + 0.044715 * value * value * value)))
    )


def rms_scale(value, gain_vec):
    return value * lax.rsqrt(jnp.mean(value * value, axis=-1, keepdims=True) + 1e-05) * gain_vec


def over_rows(left, right):
    return lax.dot_general(
        left, right, (((0,), (0,)), ((), ())), preferred_element_type=jnp.float32
    )


def against(left, right):
    return lax.dot_general(
        left, right, (((1,), (1,)), ((), ())), preferred_element_type=jnp.float32
    )


def masked_scores(query, key_rows, allowed):
    scores = jnp.einsum(
        "glhe,gmhe->ghlm", query, key_rows, preferred_element_type=jnp.float32
    ) * HD ** (-0.5)
    return jnp.where(allowed[:, None], scores, -1e30)


def attend(query, key_rows, value_rows, allowed):
    scores = masked_scores(query, key_rows, allowed)
    highest = jnp.max(scores, axis=-1, keepdims=True)
    expo = jnp.exp(scores - highest)
    totals = jnp.sum(expo, axis=-1, keepdims=True)
    probs = expo / totals
    log_total = highest + jnp.log(totals)
    mixed = jnp.einsum(
        "ghlm,gmhe->glhe",
        probs.astype(jnp.bfloat16),
        value_rows,
        preferred_element_type=jnp.float32,
    )
    return (mixed.astype(jnp.bfloat16), log_total)


def attend_back(query, key_rows, value_rows, allowed, log_total, grad_mixed):
    probs = jnp.exp(masked_scores(query, key_rows, allowed) - log_total)
    grad_probs = jnp.einsum(
        "glhe,gmhe->ghlm", grad_mixed, value_rows, preferred_element_type=jnp.float32
    )
    grad_values = jnp.einsum(
        "ghlm,glhe->gmhe",
        probs.astype(jnp.bfloat16),
        grad_mixed,
        preferred_element_type=jnp.float32,
    )
    inner = jnp.sum(probs * grad_probs, axis=-1, keepdims=True)
    grad_scores = (probs * (grad_probs - inner)).astype(jnp.bfloat16)
    grad_query = jnp.einsum(
        "ghlm,gmhe->glhe", grad_scores, key_rows, preferred_element_type=jnp.float32
    ) * HD ** (-0.5)
    grad_keys = jnp.einsum(
        "ghlm,glhe->gmhe", grad_scores, query, preferred_element_type=jnp.float32
    ) * HD ** (-0.5)
    return (grad_query, grad_keys, grad_values)


def bit_list(sizes):
    found = []
    for axis, size in zip(("gx", "gy"), sizes):
        step = size // 2
        while step >= 1:
            found.append((axis, step, size))
            step //= 2
    return found


def gather_order(sizes, flip):
    names = bit_list(sizes)
    gx_bits = [pos for pos, item in enumerate(names) if item[0] == "gx"]
    gy_bits = [pos for pos, item in enumerate(names) if item[0] == "gy"]
    near = gy_bits[-2:]
    if flip:
        near = near[::-1]
    return gx_bits[:-1] + gy_bits[:-2] + near + gx_bits[-1:]


def swap(value, item):
    axis, step, size = item
    return lax.ppermute(value, axis, [(place, place ^ step) for place in range(size)])


def own_bit(item):
    axis, step, size = item
    return (lax.axis_index(axis) // step) % 2


def spans(done, pos, names):
    high = 2 ** sum(1 for other in done if other < pos)
    low = 2 ** sum(1 for other in done if other > pos)
    return high, low


def gather_step(state, done, pos, names):
    item = names[pos]
    high, low = spans(done, pos, names)
    group, blocks, rows, cols = state.shape
    received = swap(state, item)
    bit = own_bit(item)
    wide = jnp.zeros((group, high, 2, low, rows, cols), state.dtype)
    zero = jnp.zeros((), bit.dtype)
    mine = state.reshape(group, high, 1, low, rows, cols)
    theirs = received.reshape(group, high, 1, low, rows, cols)
    wide = lax.dynamic_update_slice(wide, mine, (zero, zero, bit, zero, zero, zero))
    wide = lax.dynamic_update_slice(wide, theirs, (zero, zero, 1 - bit, zero, zero, zero))
    return wide.reshape(group, blocks * 2, rows, cols), received


def gather_run(state, done, order, names):
    received = None
    for pos in order:
        state, received = gather_step(state, done, pos, names)
        done = done + [pos]
    return state, done, received


def scatter_run(state, order, names, last_type):
    left = sorted(order)
    for index, pos in enumerate(order):
        item = names[pos]
        left = [other for other in left if other != pos]
        high, low = spans(left, pos, names)
        blocks, rows, cols = state.shape
        view = state.reshape(high, 2, low, rows, cols)
        bit = own_bit(item)
        away = lax.dynamic_index_in_dim(view, 1 - bit, 1, keepdims=False)
        kept = lax.dynamic_index_in_dim(view, bit, 1, keepdims=False)
        received = swap(away, item)
        total = kept.astype(jnp.float32) + received.astype(jnp.float32)
        if index < len(order) - 1:
            total = total.astype(state.dtype)
        else:
            total = total.astype(last_type)
        state = total.reshape(blocks // 2, rows, cols)
    return state[0]


def gather_many(shards, sizes, flips, gate):
    names = bit_list(sizes)
    state = jnp.stack(shards)[:, None]
    if gate is not None:
        state, unused = lax.optimization_barrier((state, gate))
    orders = [gather_order(sizes, flip) for flip in (False, True)]
    shared = len(orders[0]) - 3
    state, done, received = gather_run(state, [], orders[0][:shared], names)
    token = received[:1, :1, :1, :1]
    parts = []
    start = 0
    for flip in (False, True):
        count = sum(1 for other in flips if other == flip)
        if count == 0:
            continue
        part = state[start : start + count]
        start += count
        part, part_done, unused = gather_run(part, done, orders[int(flip)][shared:], names)
        for index in range(count):
            whole = part[index]
            parts.append(whole.reshape(-1, whole.shape[-1]))
    return parts, token


def scatter_one(grad, sizes, flip):
    names = bit_list(sizes)
    count = 2 ** len(names)
    order = gather_order(sizes, flip)[::-1]
    return scatter_run(
        grad.reshape(count, grad.shape[0] // count, grad.shape[1]), order, names, jnp.float32
    )


def block_forward(x_in, allowed, gains, weights, groups):
    prenorm, midnorm, b_up, b_down = gains
    w_query, w_key, w_value, w_out, w_up, w_down = weights
    row_count = x_in.shape[0]
    span = row_count // groups
    normed = rms_scale(x_in, prenorm).astype(jnp.bfloat16)
    query = (
        jnp.dot(normed, w_query, preferred_element_type=jnp.float32)
        .astype(jnp.bfloat16)
        .reshape(groups, span, HEADS, HD)
    )
    key_rows = (
        jnp.dot(normed, w_key, preferred_element_type=jnp.float32)
        .astype(jnp.bfloat16)
        .reshape(groups, span, HEADS, HD)
    )
    value_rows = (
        jnp.dot(normed, w_value, preferred_element_type=jnp.float32)
        .astype(jnp.bfloat16)
        .reshape(groups, span, HEADS, HD)
    )
    mixed_heads, log_total = attend(query, key_rows, value_rows, allowed)
    mixed = mixed_heads.reshape(row_count, D)
    hidden = x_in + jnp.dot(mixed, w_out, preferred_element_type=jnp.float32)
    normed_two = rms_scale(hidden, midnorm).astype(jnp.bfloat16)
    preact = jnp.dot(normed_two, w_up, preferred_element_type=jnp.float32) + b_up
    activated = gelu_tanh(preact).astype(jnp.bfloat16)
    result = hidden + (jnp.dot(activated, w_down, preferred_element_type=jnp.float32) + b_down)
    saved = (
        normed,
        query,
        key_rows,
        value_rows,
        log_total,
        mixed,
        hidden,
        normed_two,
        preact,
        activated,
    )
    return (result, saved)


def block_backward(grad_y, x_in, allowed, gains, weights, saved, sizes):
    prenorm, midnorm, b_up, b_down = gains
    w_query, w_key, w_value, w_out, w_up, w_down = weights
    normed, query, key_rows, value_rows, log_total, mixed, hidden, normed_two, preact, activated = (
        saved
    )
    row_count = x_in.shape[0]
    low = jnp.bfloat16
    grad_branch = grad_y.astype(jnp.bfloat16)
    grad_b_down = jnp.sum(grad_branch.astype(jnp.float32), axis=0)
    shard_down = scatter_one(over_rows(activated, grad_branch).astype(low), sizes, True)
    grad_act = against(grad_branch, w_down)
    unused_value, gelu_back = jax.vjp(gelu_tanh, preact)
    grad_pre = gelu_back(grad_act)[0].astype(jnp.bfloat16)
    grad_b_up = jnp.sum(grad_pre.astype(jnp.float32), axis=0)
    shard_up = scatter_one(over_rows(normed_two, grad_pre).astype(low), sizes, False)
    grad_normed_two = against(grad_pre, w_up)
    unused_mid, mid_back = jax.vjp(rms_scale, hidden, midnorm)
    grad_hidden_part, grad_midnorm = mid_back(grad_normed_two)
    grad_hidden = grad_y + grad_hidden_part
    grad_attn = grad_hidden.astype(jnp.bfloat16)
    grad_w_out = over_rows(mixed, grad_attn)
    grad_mixed = against(grad_attn, w_out).astype(jnp.bfloat16)
    grad_query, grad_keys, grad_values = attend_back(
        query, key_rows, value_rows, allowed, log_total, grad_mixed.reshape(query.shape)
    )
    grad_query = grad_query.reshape(row_count, D).astype(jnp.bfloat16)
    grad_keys = grad_keys.reshape(row_count, D).astype(jnp.bfloat16)
    grad_values = grad_values.reshape(row_count, D).astype(jnp.bfloat16)
    pair = jnp.concatenate([grad_query, grad_keys], axis=1)
    shard_pair = scatter_one(over_rows(normed, pair).astype(low), sizes, False)
    grad_w_value = over_rows(normed, grad_values)
    other = jnp.concatenate([grad_w_value.astype(low), grad_w_out.astype(low)], axis=1)
    shard_other = scatter_one(other, sizes, True)
    grad_normed = (
        against(grad_query, w_query) + against(grad_keys, w_key) + against(grad_values, w_value)
    )
    unused_pre, pre_back = jax.vjp(rms_scale, x_in, prenorm)
    grad_x_part, grad_prenorm = pre_back(grad_normed)
    grad_x = grad_hidden + grad_x_part
    shards = (
        shard_pair[:, :D],
        shard_pair[:, D:],
        shard_other[:, :D],
        shard_other[:, D:],
        shard_up,
        shard_down,
    )
    return (grad_x, shards, (grad_prenorm, grad_midnorm, grad_b_up, grad_b_down))


def local(
    sizes,
    frame_input,
    code_embed,
    segment_ids,
    frame_cotangent,
    code_cotangent,
    frame_prenorm,
    frame_query,
    frame_keys,
    frame_values,
    frame_outproj,
    frame_midnorm,
    frame_upproj,
    frame_upbias,
    frame_downproj,
    frame_downbias,
    code_prenorm,
    code_query,
    code_keys,
    code_values,
    code_outproj,
    code_midnorm,
    code_upproj,
    code_upbias,
    code_downproj,
    code_downbias,
):
    frame_count = frame_input.shape[0]
    names = bit_list(sizes)
    devices = 2 ** len(names)
    vectors = (
        frame_prenorm,
        frame_midnorm,
        frame_upbias,
        frame_downbias,
        code_prenorm,
        code_midnorm,
        code_upbias,
        code_downbias,
    )
    widths = [vec.shape[0] for vec in vectors]
    packed = jnp.concatenate(vectors)[None, None, None, :]
    whole, unused, unused_two = gather_run(packed, [], gather_order(sizes, False), names)
    whole = whole.reshape(devices, -1).astype(jnp.float32)
    gains = []
    start = 0
    for width in widths:
        gains.append(whole[:, start : start + width].reshape(devices * width))
        start += width
    order = (False, False, True, True)
    (fq, fk, fv, fo), token = gather_many(
        [frame_query, frame_keys, frame_values, frame_outproj], sizes, order, None
    )
    (fu,), token_up = gather_many([frame_upproj], sizes, (False,), token)
    (fd,), token_down = gather_many([frame_downproj], sizes, (True,), token)
    (cq, ck, cv, co), token = gather_many(
        [code_query, code_keys, code_values, code_outproj], sizes, order, (token_up, token_down)
    )
    (cu,), unused = gather_many([code_upproj], sizes, (False,), token)
    (cd,), unused = gather_many([code_downproj], sizes, (True,), token)
    frame_weights = (fq, fk, fv, fo, fu, fd)
    code_weights = (cq, ck, cv, co, cu, cd)
    frame_gains = tuple(gains[:4])
    code_gains = tuple(gains[4:])
    place = jnp.arange(frame_count)
    segment_row = segment_ids[0]
    frame_allowed = (
        (segment_row[:, None] == segment_row[None, :]) & (place[:, None] >= place[None, :])
    )[None]
    frame_x = frame_input.astype(jnp.float32)
    frame_out, frame_saved = block_forward(frame_x, frame_allowed, frame_gains, frame_weights, 1)
    code_in = (code_embed.astype(jnp.float32) + frame_out[:, None, :]).reshape(frame_count * CB, D)
    code_place = jnp.arange(CB)
    code_allowed = (code_place[:, None] >= code_place[None, :])[None]
    code_out, code_saved = block_forward(
        code_in, code_allowed, code_gains, code_weights, frame_count
    )
    grad_code_in, code_shards, code_vectors = block_backward(
        code_cotangent.astype(jnp.float32).reshape(frame_count * CB, D),
        code_in,
        code_allowed,
        code_gains,
        code_weights,
        code_saved,
        sizes,
    )
    grad_code_rows = grad_code_in.reshape(frame_count, CB, D)
    frame_grad_y = frame_cotangent.astype(jnp.float32) + jnp.sum(grad_code_rows, axis=1)
    grad_frame_in, frame_shards, frame_vectors = block_backward(
        frame_grad_y,
        frame_x,
        frame_allowed,
        frame_gains,
        frame_weights,
        frame_saved,
        sizes,
    )
    terms = jnp.concatenate(
        [
            grad_vec.reshape(devices, -1)
            for grad_vec in tuple(frame_vectors) + tuple(code_vectors)
        ],
        axis=1,
    )[:, None, :]
    sums = scatter_run(terms, gather_order(sizes, False)[::-1], names, jnp.float32)[0]
    vector_shards = []
    start = 0
    for width in widths:
        vector_shards.append(sums[start : start + width])
        start += width

    def arranged(shards, vecs):
        query, keys, values, outproj, upproj, downproj = shards
        prenorm, midnorm, upbias, downbias = vecs
        return (
            prenorm,
            query,
            keys,
            values,
            outproj,
            midnorm,
            upproj,
            upbias,
            downproj,
            downbias,
        )

    return (
        (
            frame_out.astype(jnp.bfloat16),
            code_out.reshape(frame_count, CB, D).astype(jnp.bfloat16),
            grad_frame_in,
            grad_code_rows,
        )
        + arranged(frame_shards, vector_shards[:4])
        + arranged(code_shards, vector_shards[4:])
    )


def solution(mesh):
    in_specs = (
        P(("gx", "gy"), None),
        P(("gx", "gy"), None, None),
        P(("gx", "gy"), None),
        P(("gx", "gy"), None),
        P(("gx", "gy"), None, None),
        P(("gx", "gy")),
        P(("gx", "gy"), None),
        P(("gx", "gy"), None),
        P(("gx", "gy"), None),
        P(("gx", "gy"), None),
        P(("gx", "gy")),
        P(("gx", "gy"), None),
        P(("gx", "gy")),
        P(("gx", "gy"), None),
        P(("gx", "gy")),
        P(("gx", "gy")),
        P(("gx", "gy"), None),
        P(("gx", "gy"), None),
        P(("gx", "gy"), None),
        P(("gx", "gy"), None),
        P(("gx", "gy")),
        P(("gx", "gy"), None),
        P(("gx", "gy")),
        P(("gx", "gy"), None),
        P(("gx", "gy")),
    )
    out_specs = (
        P(("gx", "gy"), None),
        P(("gx", "gy"), None, None),
        P(("gx", "gy"), None),
        P(("gx", "gy"), None, None),
        P(("gx", "gy")),
        P(("gx", "gy"), None),
        P(("gx", "gy"), None),
        P(("gx", "gy"), None),
        P(("gx", "gy"), None),
        P(("gx", "gy")),
        P(("gx", "gy"), None),
        P(("gx", "gy")),
        P(("gx", "gy"), None),
        P(("gx", "gy")),
        P(("gx", "gy")),
        P(("gx", "gy"), None),
        P(("gx", "gy"), None),
        P(("gx", "gy"), None),
        P(("gx", "gy"), None),
        P(("gx", "gy")),
        P(("gx", "gy"), None),
        P(("gx", "gy")),
        P(("gx", "gy"), None),
        P(("gx", "gy")),
    )
    sizes = (mesh.shape["gx"], mesh.shape["gy"])
    return jax.shard_map(
        functools.partial(local, sizes), mesh=mesh, in_specs=in_specs, out_specs=out_specs, check_vma=False)
```

time: 3620 us -> 1180 us (0.33)
  waiting for transfers between devices: 2780 us -> 470 us
  blocking collectives: 212 us -> 0 us
  starting transfers between devices: 1.34 us -> 76.4 us
  other arithmetic: 18.2 us -> 67 us
  matrix products: 280 us -> 243 us
    reduce_scatter x12 -> x0, waiting for transfers between devices: 2310 us -> none  [the longest x1 360 us: local(): lax.psum_scatter(code_flat[6], ('gx', 'gy'), scatter_dimension=0, tiled=T...]
    ppermute x0 -> x86, waiting for transfers between devices: none -> 470 us  [swap(): lax.ppermute(value, axis, [(place, place ^ step) for place in range(size)])]
    all_gather x12 -> x0, waiting for transfers between devices: 459 us -> none  [the longest x1 76 us: local(): lax.all_gather(frame_upproj, ('gx', 'gy'), axis=0, tiled=True)]
    reshape x24 -> x6, local copies, waits for them, and re-layouts: 132 us -> 0.69 us  [the longest x3 0.66 us: gather_step(): return (wide.reshape(group, blocks * 2, rows, cols), received)]
    all_gather x2 -> x0, blocking collectives: 129 us -> none  [the longest x1 66.1 us: local(): lax.all_gather(frame_upbias, ('gx', 'gy'), axis=0, tiled=True)]
    unnamed x2 -> x0, blocking collectives: 83 us -> none
    ppermute x0 -> x86, starting transfers between devices: none -> 76.4 us  [swap(): lax.ppermute(value, axis, [(place, place ^ step) for place in range(size)])]
    dynamic_update_slice x0 -> x81, local copies, waits for them, and re-layouts: none -> 68.6 us  [the longest x41 39.1 us: gather_step(): lax.dynamic_update_slice(wide, theirs, (zero, zero, 1 - bit, zero, zero,...]
  transfers between devices with their start and end apart: 24 -> 86, of which waited for: 20 -> 45; matrix products, arithmetic and copies ran while one was open for 11% -> 30% of each run, Pallas kernels for 0% -> 0%
where the time goes in v1:
time: 1180 us; the launch traced here: 1170 us
  waiting for transfers between devices  470 us (40%)
  local copies, waits for them, and re-layouts  309 us (26%)
  matrix products  243 us (21%)
  starting transfers between devices  76.4 us (6%)
  other arithmetic  67 us (6%)
    ppermute x86, waiting for transfers between devices, swap(): lax.ppermute(value, axis, [(place, place ^ step) for place in range(size)])  470 us
    ppermute x86, starting transfers between devices, swap(): lax.ppermute(value, axis, [(place, place ^ step) for place in range(size)])  76.4 us
    dot_general x12, matrix products, against(): lax.dot_general(left, right, (((1,), (1,)), ((), ())), preferred_element_...  68.6 us
    dot_general x10, matrix products, over_rows(): lax.dot_general(left, right, (((0,), (0,)), ((), ())), preferred_element_...  60.6 us
    dynamic_update_slice x41, local copies, waits for them, and re-layouts, gather_step(): lax.dynamic_update_slice(wide, theirs, (zero, zero, 1 - bit, zero, zero,...  39.1 us
    convert_element_type x32, other arithmetic, scatter_run(): total = total.astype(state.dtype)  37.1 us
    dynamic_update_slice x40, local copies, waits for them, and re-layouts, gather_step(): lax.dynamic_update_slice(wide, mine, (zero, zero, bit, zero, zero, zero))  29.5 us
    squeeze x43, local copies, waits for them, and re-layouts, scatter_run(): away = lax.dynamic_index_in_dim(view, 1 - bit, 1, keepdims=False)  29.1 us
  transfers between devices with their start and end apart: 86, of which 45 were waited for; matrix products, arithmetic and copies ran while one was open for 30% of the time, Pallas kernels for 0%

profile of v1, /device:TPU:0, one launch (start us, length us, event | category | flops | bytes accessed | tf_op | source)
XLA Modules:
  0.0 1168.9 jit_solution(2937350670755166439)
XLA Ops:
  54.4 12.2 %collective-permute-done.24 = bf16[4,2,32,1024]{3,2,1,0:T(8,128)(2,1)S(1)} collective-permute-done((bf16[4,2,32,1024]{3,2,1,0:T(8,128)(2,1)S(1)}, bf16[4,2,32,1024]{3,2,1,0:T(8,128)(2,1)S(1)}, u32[]{:S(2)}, u32[]{:S(2)}) %collective-permute-start.24) | collective-permute-done | bytes 524320 | tf_op jit(solution)/shard_map/ppermute | solution.py:105
  71.1 16.9 %collective-permute-done.6 = bf16[4,2,32,1024]{3,2,1,0:T(8,128)(2,1)S(1)} collective-permute-done((bf16[4,2,32,1024]{3,2,1,0:T(8,128)(2,1)S(1)}, bf16[4,2,32,1024]{3,2,1,0:T(8,128)(2,1)S(1)}, u32[]{:S(2)}, u32[]{:S(2)}) %collective-permute-start.6) | collective-permute-done | bytes 524320 | tf_op jit(solution)/shard_map/ppermute | solution.py:105
  92.8 17.5 %collective-permute-done.13 = bf16[1,1,32,4096]{3,2,1,0:T(8,128)(2,1)S(1)} collective-permute-done((bf16[1,1,32,4096]{3,2,1,0:T(8,128)(2,1)S(1)}, bf16[1,1,32,4096]{3,2,1,0:T(8,128)(2,1)S(1)}, u32[]{:S(2)}, u32[]{:S(2)}) %collective-permute-start.13) | collective-permute-done | bytes 262176 | tf_op jit(solution)/shard_map/ppermute | solution.py:105
  146.0 16.2 %collective-permute-done.14 = bf16[1,2,32,4096]{3,2,1,0:T(8,128)(2,1)S(1)} collective-permute-done((bf16[1,2,32,4096]{3,2,1,0:T(8,128)(2,1)S(1)}, bf16[1,2,32,4096]{3,2,1,0:T(8,128)(2,1)S(1)}, u32[]{:S(2)}, u32[]{:S(2)}) %collective-permute-start.14) | collective-permute-done | bytes 524320 | tf_op jit(solution)/shard_map/ppermute | solution.py:105
  172.6 15.7 %collective-permute-done.29 = bf16[2,8,32,1024]{3,2,1,0:T(8,128)(2,1)S(1)} collective-permute-done((bf16[2,8,32,1024]{3,2,1,0:T(8,128)(2,1)S(1)}, bf16[2,8,32,1024]{3,2,1,0:T(8,128)(2,1)S(1)}, u32[]{:S(2)}, u32[]{:S(2)}) %collective-permute-start.29) | collective-permute-done | bytes 1048608 | tf_op jit(solution)/shard_map/ppermute | solution.py:105
  195.2 15.7 %collective-permute-done.11 = bf16[2,8,32,1024]{3,2,1,0:T(8,128)(2,1)S(1)} collective-permute-done((bf16[2,8,32,1024]{3,2,1,0:T(8,128)(2,1)S(1)}, bf16[2,8,32,1024]{3,2,1,0:T(8,128)(2,1)S(1)}, u32[]{:S(2)}, u32[]{:S(2)}) %collective-permute-start.11) | collective-permute-done | bytes 1048608 | tf_op jit(solution)/shard_map/ppermute | solution.py:105
  220.3 33.0 %collective-permute-done.20 = bf16[1,4,128,1024]{3,2,1,0:T(8,128)(2,1)S(1)} collective-permute-done((bf16[1,4,128,1024]{3,2,1,0:T(8,128)(2,1)S(1)}, bf16[1,4,128,1024]{3,2,1,0:T(8,128)(2,1)S(1)}, u32[]{:S(2)}, u32[]{:S(2)}) %collective-permute-start.20) | collective-permute-done | bytes 1048608 | tf_op jit(solution)/shard_map/ppermute | solution.py:105
  303.4 47.7 %collective-permute-done.16 = bf16[1,8,32,4096]{3,2,1,0:T(8,128)(2,1)} collective-permute-done((bf16[1,8,32,4096]{3,2,1,0:T(8,128)(2,1)}, bf16[1,8,32,4096]{3,2,1,0:T(8,128)(2,1)}, u32[]{:S(2)}, u32[]{:S(2)}) %collective-permute-start.16) | collective-permute-done | bytes 2097184 | tf_op jit(solution)/shard_map/ppermute | solution.py:105
  461.4 10.8 fusion.37
  509.5 12.9 %fusion.119 = f32[768,4096]{1,0:T(8,128)} fusion(bf16[1024,4096]{1,0:T(8,128)(2,1)} %bitcast.675, f32[768,1024]{1,0:T(8,128)S(1)} %get-tuple-element.241, f32[1024]{0:T(1024)S(1)} %copy-done.98, f32[768]{0:T(1024)S(1)} %fusion.112), kind=kOutput, calls=%fused_computation.395 | convolution fusion | flops 6444810240 | bytes 24124416 | tf_op jit(solution)/shard_map/dot_general | solution.py:221
  525.4 24.1 %convert_reduce_fusion = (f32[4096]{0:T(1024)}, bf16[768,4096]{1,0:T(8,128)(2,1)}) fusion(bf16[4096,1024]{1,0:T(8,128)(2,1)S(1)} %bitcast.685, bf16[768,1024]{1,0:T(8,128)(2,1)S(1)} %copy-done.74, f32[768,4096]{1,0:T(8,128)} %fusion.119, f32[4096]{0:T(1024)S(1)} %copy-done.103), kind=kOutput, calls=%fused_computation.15 | convolution fusion | flops 6527381504 | bytes 28868608 | tf_op jit(solution)/shard_map/dot_general | solution.py:33
  549.5 11.4 multiply_reduce_fusion.1
  561.0 12.2 %convolution_convert_fusion.1 = bf16[1024,4096]{1,0:T(8,128)(2,1)} fusion(bf16[768,4096]{1,0:T(8,128)(2,1)} %get-tuple-element.249, f32[768,1024]{1,0:T(8,128)S(1)} %copy-done.61, f32[1024]{0:T(1024)S(1)} %copy-done.98, f32[768]{0:T(1024)S(1)} %fusion.112), kind=kOutput, calls=%fused_computation.28 | convolution fusion | flops 6449004544 | bytes 17832960 | tf_op jit(solution)/shard_map/dot_general | solution.py:27
  573.2 14.7 %convolution_convert_fusion = bf16[4096,1024]{1,0:T(8,128)(2,1)} fusion(f32[768,1024]{1,0:T(8,128)S(1)} %copy-done.23, f32[768,4096]{1,0:T(8,128)} %fusion.119, f32[4096]{0:T(1024)S(1)} %copy-done.103), kind=kOutput, calls=%fused_computation.27 | convolution fusion | flops 6478888960 | bytes 24133632 | tf_op jit(solution)/shard_map/dot_general | solution.py:27
  743.4 12.1 %add_convert_fusion = bf16[768,1024]{1,0:T(8,128)(2,1)} fusion(f32[768,1024]{1,0:T(8,128)S(1)} %copy-done.62, bf16[4096,1024]{1,0:T(8,128)(2,1)S(1)} %bitcast.688, f32[1024]{0:T(1024)S(1)} %copy-done.109, f32[768,4096]{1,0:T(8,128)} %fusion.119, f32[4096]{0:T(1024)S(1)} %copy-done.103), kind=kOutput, calls=%fused_computation.109 | convolution fusion | flops 6476267520 | bytes 25710592 | tf_op jit(solution)/shard_map/dot_general | solution.py:223
  836.4 20.5 %collective-permute-done.52 = bf16[4,2,32,2048]{3,2,0,1:T(8,128)(2,1)S(1)} collective-permute-done((bf16[4,2,32,2048]{3,2,0,1:T(8,128)(2,1)S(1)}, bf16[4,2,32,2048]{3,2,0,1:T(8,128)(2,1)S(1)}, u32[]{:S(2)}, u32[]{:S(2)}) %collective-permute-start.52) | collective-permute-done | bytes 1048608 | tf_op jit(solution)/shard_map/ppermute | solution.py:105
  861.2 20.5 %collective-permute-done.72 = bf16[4,2,32,2048]{3,2,0,1:T(8,128)(2,1)S(1)} collective-permute-done((bf16[4,2,32,2048]{3,2,0,1:T(8,128)(2,1)S(1)}, bf16[4,2,32,2048]{3,2,0,1:T(8,128)(2,1)S(1)}, u32[]{:S(2)}, u32[]{:S(2)}) %collective-permute-start.72) | collective-permute-done | bytes 1048608 | tf_op jit(solution)/shard_map/ppermute | solution.py:105
  897.8 9.5 collective-permute-done.73
  998.9 28.2 %collective-permute-done.82 = bf16[4,2,128,1024]{3,2,1,0:T(8,128)(2,1)} collective-permute-done((bf16[4,2,128,1024]{3,2,1,0:T(8,128)(2,1)}, bf16[4,2,128,1024]{3,2,1,0:T(8,128)(2,1)}, u32[]{:S(2)}, u32[]{:S(2)}) %collective-permute-start.82) | collective-permute-done | bytes 2097184 | tf_op jit(solution)/shard_map/ppermute | solution.py:105
  1036.9 35.1 %collective-permute-done.62 = bf16[4,2,128,1024]{3,2,1,0:T(8,128)(2,1)} collective-permute-done((bf16[4,2,128,1024]{3,2,1,0:T(8,128)(2,1)}, bf16[4,2,128,1024]{3,2,1,0:T(8,128)(2,1)}, u32[]{:S(2)}, u32[]{:S(2)}) %collective-permute-start.62) | collective-permute-done | bytes 2097184 | tf_op jit(solution)/shard_map/ppermute | solution.py:105
  1080.2 19.4 %collective-permute-done.83 = bf16[4,1,128,1024]{3,2,1,0:T(8,128)(2,1)S(1)} collective-permute-done((bf16[4,1,128,1024]{3,2,1,0:T(8,128)(2,1)S(1)}, bf16[4,1,128,1024]{3,2,1,0:T(8,128)(2,1)S(1)}, u32[]{:S(2)}, u32[]{:S(2)}) %collective-permute-start.83) | collective-permute-done | bytes 1048608 | tf_op jit(solution)/shard_map/ppermute | solution.py:105
  1102.5 12.7 %collective-permute-done.63 = bf16[4,1,128,1024]{3,2,1,0:T(8,128)(2,1)S(1)} collective-permute-done((bf16[4,1,128,1024]{3,2,1,0:T(8,128)(2,1)S(1)}, bf16[4,1,128,1024]{3,2,1,0:T(8,128)(2,1)S(1)}, u32[]{:S(2)}, u32[]{:S(2)}) %collective-permute-start.63) | collective-permute-done | bytes 1048608 | tf_op jit(solution)/shard_map/ppermute | solution.py:105
  1126.9 16.6 %collective-permute-done.64 = bf16[2,1,128,1024]{3,2,0,1:T(8,128)(2,1)S(1)} collective-permute-done((bf16[2,1,128,1024]{3,2,0,1:T(8,128)(2,1)S(1)}, bf16[2,1,128,1024]{3,2,0,1:T(8,128)(2,1)S(1)}, u32[]{:S(2)}, u32[]{:S(2)}) %collective-permute-start.64) | collective-permute-done | bytes 524320 | tf_op jit(solution)/shard_map/ppermute | solution.py:105
  1153.4 11.7 collective-permute-done.65
  (776 shorter events, 717.5 us)
Async XLA Ops:
  91.2 50.6 %collective-permute-start.7 = (bf16[2,4,32,1024]{3,2,1,0:T(8,128)(2,1)S(1)}, bf16[2,4,32,1024]{3,2,1,0:T(8,128)(2,1)S(1)}, u32[]{:S(2)}, u32[]{:S(2)}) collective-permute-start(bf16[2,4,32,1024]{3,2,1,0:T(8,128)(2,1)S(1)} %bitcast.769), channel_id=1, source_target_pairs={{0,1},{1,0},{2,3},{3,2},{4,5},{5,4},{6,7},{7,6},{8,9},{9,8},{10,11... | collective-permute-start | bytes 1572872 | tf_op jit(solution)/shard_map/ppermute | solution.py:105
  115.2 54.1 %collective-permute-start.37 = (bf16[1,2,128,1024]{3,2,1,0:T(8,128)(2,1)S(1)}, bf16[1,2,128,1024]{3,2,1,0:T(8,128)(2,1)S(1)}, u32[]{:S(2)}, u32[]{:S(2)}) collective-permute-start(bf16[1,2,128,1024]{3,2,1,0:T(8,128)(2,1)S(1)} %bitcast.760), channel_id=1, source_target_pairs={{0,4},{1,5},{2,6},{3,7},{4,0},{5,1},{6,2},{7,3},{8,12},{9,13},{10,... | collective-permute-start | bytes 1572872 | tf_op jit(solution)/shard_map/ppermute | solution.py:105
  141.8 50.7 %collective-permute-start.26 = (bf16[2,8,32,1024]{3,2,1,0:T(8,128)(2,1)S(1)}, bf16[2,8,32,1024]{3,2,1,0:T(8,128)(2,1)S(1)}, u32[]{:S(2)}, u32[]{:S(2)}) collective-permute-start(bf16[2,8,32,1024]{3,2,1,0:T(8,128)(2,1)S(1)} %bitcast.723), channel_id=1, source_target_pairs={{0,2},{1,3},{2,0},{3,1},{4,6},{5,7},{6,4},{7,5},{8,10},{9,11},{10,... | collective-permute-start | bytes 3145736 | tf_op jit(solution)/shard_map/ppermute | solution.py:105
  162.8 50.5 %collective-permute-start.8 = (bf16[2,8,32,1024]{3,2,1,0:T(8,128)(2,1)S(1)}, bf16[2,8,32,1024]{3,2,1,0:T(8,128)(2,1)S(1)}, u32[]{:S(2)}, u32[]{:S(2)}) collective-permute-start(bf16[2,8,32,1024]{3,2,1,0:T(8,128)(2,1)S(1)} %bitcast.720), channel_id=1, source_target_pairs={{0,2},{1,3},{2,0},{3,1},{4,6},{5,7},{6,4},{7,5},{8,10},{9,11},{10,... | collective-permute-start | bytes 3145736 | tf_op jit(solution)/shard_map/ppermute | solution.py:105
  169.3 87.4 %collective-permute-start.33 = (bf16[1,4,32,4096]{3,2,1,0:T(8,128)(2,1)S(1)}, bf16[1,4,32,4096]{3,2,1,0:T(8,128)(2,1)S(1)}, u32[]{:S(2)}, u32[]{:S(2)}) collective-permute-start(bf16[1,4,32,4096]{3,2,1,0:T(8,128)(2,1)S(1)} %bitcast.727), channel_id=1, source_target_pairs={{0,2},{1,3},{2,0},{3,1},{4,6},{5,7},{6,4},{7,5},{8,10},{9,11},{10,... | collective-permute-start | bytes 3145736 | tf_op jit(solution)/shard_map/ppermute | solution.py:105
  188.4 66.4 %collective-permute-start.38 = (bf16[1,4,128,1024]{3,2,1,0:T(8,128)(2,1)S(1)}, bf16[1,4,128,1024]{3,2,1,0:T(8,128)(2,1)S(1)}, u32[]{:S(2)}, u32[]{:S(2)}) collective-permute-start(bf16[1,4,128,1024]{3,2,1,0:T(8,128)(2,1)S(1)} %bitcast.729), channel_id=1, source_target_pairs={{0,1},{1,0},{2,3},{3,2},{4,5},{5,4},{6,7},{7,6},{8,9},{9,8},{10,11... | collective-permute-start | bytes 3145736 | tf_op jit(solution)/shard_map/ppermute | solution.py:105
  192.5 60.8 %collective-permute-start.20 = (bf16[1,4,128,1024]{3,2,1,0:T(8,128)(2,1)S(1)}, bf16[1,4,128,1024]{3,2,1,0:T(8,128)(2,1)S(1)}, u32[]{:S(2)}, u32[]{:S(2)}) collective-permute-start(bf16[1,4,128,1024]{3,2,1,0:T(8,128)(2,1)S(1)} %bitcast.731), channel_id=1, source_target_pairs={{0,1},{1,0},{2,3},{3,2},{4,5},{5,4},{6,7},{7,6},{8,9},{9,8},{10,11... | collective-permute-start | bytes 3145736 | tf_op jit(solution)/shard_map/ppermute | solution.py:105
  213.4 139.7 %collective-permute-start.27 = (bf16[2,16,32,1024]{3,2,1,0:T(8,128)(2,1)}, bf16[2,16,32,1024]{3,2,1,0:T(8,128)(2,1)}, u32[]{:S(2)}, u32[]{:S(2)}) collective-permute-start(bf16[2,16,32,1024]{3,2,1,0:T(8,128)(2,1)} %bitcast.124), channel_id=1, source_target_pairs={{0,16},{16,0},{1,17},{17,1},{2,18},{18,2},{3,19},{19,3},{4,20},{20... | collective-permute-start | bytes 6291464 | tf_op jit(solution)/shard_map/ppermute | solution.py:105
  257.8 106.9 %collective-permute-start.34 = (bf16[1,8,32,4096]{3,2,1,0:T(8,128)(2,1)}, bf16[1,8,32,4096]{3,2,1,0:T(8,128)(2,1)}, u32[]{:S(2)}, u32[]{:S(2)}) collective-permute-start(bf16[1,8,32,4096]{3,2,1,0:T(8,128)(2,1)} %bitcast.158), channel_id=1, source_target_pairs={{0,1},{1,0},{2,3},{3,2},{4,5},{5,4},{6,7},{7,6},{8,9},{9,8},{10,11... | collective-permute-start | bytes 6291464 | tf_op jit(solution)/shard_map/ppermute | solution.py:105
  271.4 97.0 %collective-permute-start.39 = (bf16[1,8,128,1024]{3,2,1,0:T(8,128)(2,1)}, bf16[1,8,128,1024]{3,2,1,0:T(8,128)(2,1)}, u32[]{:S(2)}, u32[]{:S(2)}) collective-permute-start(bf16[1,8,128,1024]{3,2,1,0:T(8,128)(2,1)} %bitcast.180), channel_id=1, source_target_pairs={{0,2},{1,3},{2,0},{3,1},{4,6},{5,7},{6,4},{7,5},{8,10},{9,11},{10,... | collective-permute-start | bytes 6291464 | tf_op jit(solution)/shard_map/ppermute | solution.py:105
  281.9 69.2 %collective-permute-start.16 = (bf16[1,8,32,4096]{3,2,1,0:T(8,128)(2,1)}, bf16[1,8,32,4096]{3,2,1,0:T(8,128)(2,1)}, u32[]{:S(2)}, u32[]{:S(2)}) collective-permute-start(bf16[1,8,32,4096]{3,2,1,0:T(8,128)(2,1)} %bitcast.702), channel_id=1, source_target_pairs={{0,1},{1,0},{2,3},{3,2},{4,5},{5,4},{6,7},{7,6},{8,9},{9,8},{10,11... | collective-permute-start | bytes 6291464 | tf_op jit(solution)/shard_map/ppermute | solution.py:105
  299.7 64.6 %collective-permute-start.21 = (bf16[1,8,128,1024]{3,2,1,0:T(8,128)(2,1)S(1)}, bf16[1,8,128,1024]{3,2,1,0:T(8,128)(2,1)S(1)}, u32[]{:S(2)}, u32[]{:S(2)}) collective-permute-start(bf16[1,8,128,1024]{3,2,1,0:T(8,128)(2,1)S(1)} %bitcast.703), channel_id=1, source_target_pairs={{0,2},{1,3},{2,0},{3,1},{4,6},{5,7},{6,4},{7,5},{8,10},{9,11},{10,... | collective-permute-start | bytes 6291464 | tf_op jit(solution)/shard_map/ppermute | solution.py:105
  367.9 135.8 %collective-permute-start.35 = (bf16[1,16,32,4096]{3,2,1,0:T(8,128)(2,1)}, bf16[1,16,32,4096]{3,2,1,0:T(8,128)(2,1)}, u32[]{:S(2)}, u32[]{:S(2)}) collective-permute-start(bf16[1,16,32,4096]{3,2,1,0:T(8,128)(2,1)} %bitcast.161), channel_id=1, source_target_pairs={{0,16},{16,0},{1,17},{17,1},{2,18},{18,2},{3,19},{19,3},{4,20},{20... | collective-permute-start | bytes 12582920 | tf_op jit(solution)/shard_map/ppermute | solution.py:105
  371.5 150.9 %collective-permute-start.40 = (bf16[1,16,128,1024]{3,2,1,0:T(8,128)(2,1)}, bf16[1,16,128,1024]{3,2,1,0:T(8,128)(2,1)}, u32[]{:S(2)}, u32[]{:S(2)}) collective-permute-start(bf16[1,16,128,1024]{3,2,1,0:T(8,128)(2,1)} %bitcast.183), channel_id=1, source_target_pairs={{0,16},{16,0},{1,17},{17,1},{2,18},{18,2},{3,19},{19,3},{4,20},{20... | collective-permute-start | bytes 12582920 | tf_op jit(solution)/shard_map/ppermute | solution.py:105
  773.7 196.9 %collective-permute-start.81 = (bf16[1,16,128,1024]{3,2,1,0:T(8,128)(2,1)}, bf16[1,16,128,1024]{3,2,1,0:T(8,128)(2,1)}, u32[]{:S(2)}, u32[]{:S(2)}) collective-permute-start(bf16[1,16,128,1024]{3,2,1,0:T(8,128)(2,1)} %dynamic-slice_bitcast_fusion), channel_id=1, source_target_pairs={{0,16},{16,0},{1,17},{17,1},{2,18},{18,2},{3,19},{19,3},{4,20},{20... | collective-permute-start | bytes 12582920 | tf_op jit(solution)/shard_map/ppermute | solution.py:105
  774.2 204.0 %collective-permute-start.76 = (bf16[1,16,32,4096]{3,2,1,0:T(8,128)(2,1)}, bf16[1,16,32,4096]{3,2,1,0:T(8,128)(2,1)}, u32[]{:S(2)}, u32[]{:S(2)}) collective-permute-start(bf16[1,16,32,4096]{3,2,1,0:T(8,128)(2,1)} %dynamic-slice_bitcast_fusion.1), channel_id=1, source_target_pairs={{0,16},{16,0},{1,17},{17,1},{2,18},{18,2},{3,19},{19,3},{4,20},{20... | collective-permute-start | bytes 12582920 | tf_op jit(solution)/shard_map/ppermute | solution.py:105
  830.0 154.1 %collective-permute-start.61 = (bf16[1,16,128,1024]{3,2,1,0:T(8,128)(2,1)S(1)}, bf16[1,16,128,1024]{3,2,1,0:T(8,128)(2,1)}, u32[]{:S(2)}, u32[]{:S(2)}) collective-permute-start(bf16[1,16,128,1024]{3,2,1,0:T(8,128)(2,1)S(1)} %dynamic-slice_bitcast_fusion.2), channel_id=1, source_target_pairs={{0,16},{16,0},{1,17},{17,1},{2,18},{18,2},{3,19},{19,3},{4,20},{20... | collective-permute-start | bytes 12582920 | tf_op jit(solution)/shard_map/ppermute | solution.py:105
  907.3 86.3 %collective-permute-start.56 = (bf16[1,16,32,4096]{3,2,1,0:T(8,128)(2,1)}, bf16[1,16,32,4096]{3,2,1,0:T(8,128)(2,1)}, u32[]{:S(2)}, u32[]{:S(2)}) collective-permute-start(bf16[1,16,32,4096]{3,2,1,0:T(8,128)(2,1)} %dynamic-slice_bitcast_fusion.3), channel_id=1, source_target_pairs={{0,16},{16,0},{1,17},{17,1},{2,18},{18,2},{3,19},{19,3},{4,20},{20... | collective-permute-start | bytes 12582920 | tf_op jit(solution)/shard_map/ppermute | solution.py:105
  978.2 48.9 %collective-permute-start.82 = (bf16[4,2,128,1024]{3,2,1,0:T(8,128)(2,1)}, bf16[4,2,128,1024]{3,2,1,0:T(8,128)(2,1)}, u32[]{:S(2)}, u32[]{:S(2)}) collective-permute-start(bf16[4,2,128,1024]{3,2,1,0:T(8,128)(2,1)} %dynamic-slice_bitcast_fusion.4), channel_id=1, source_target_pairs={{0,2},{1,3},{2,0},{3,1},{4,6},{5,7},{6,4},{7,5},{8,10},{9,11},{10,... | collective-permute-start | bytes 6291464 | tf_op jit(solution)/shard_map/ppermute | solution.py:105
  983.4 48.9 %collective-permute-start.77 = (bf16[8,1,32,4096]{3,2,0,1:T(8,128)(2,1)}, bf16[8,1,32,4096]{3,2,0,1:T(8,128)(2,1)}, u32[]{:S(2)}, u32[]{:S(2)}) collective-permute-start(bf16[8,1,32,4096]{3,2,0,1:T(8,128)(2,1)} %dynamic-slice_bitcast_fusion.5), channel_id=1, source_target_pairs={{0,1},{1,0},{2,3},{3,2},{4,5},{5,4},{6,7},{7,6},{8,9},{9,8},{10,11... | collective-permute-start | bytes 6291464 | tf_op jit(solution)/shard_map/ppermute | solution.py:105
  992.2 79.8 %collective-permute-start.62 = (bf16[4,2,128,1024]{3,2,1,0:T(8,128)(2,1)}, bf16[4,2,128,1024]{3,2,1,0:T(8,128)(2,1)}, u32[]{:S(2)}, u32[]{:S(2)}) collective-permute-start(bf16[4,2,128,1024]{3,2,1,0:T(8,128)(2,1)} %dynamic-slice_bitcast_fusion.8), channel_id=1, source_target_pairs={{0,2},{1,3},{2,0},{3,1},{4,6},{5,7},{6,4},{7,5},{8,10},{9,11},{10,... | collective-permute-start | bytes 6291464 | tf_op jit(solution)/shard_map/ppermute | solution.py:105
  997.6 79.6 %collective-permute-start.57 = (bf16[8,1,32,4096]{3,2,0,1:T(8,128)(2,1)S(1)}, bf16[8,1,32,4096]{3,2,0,1:T(8,128)(2,1)S(1)}, u32[]{:S(2)}, u32[]{:S(2)}) collective-permute-start(bf16[8,1,32,4096]{3,2,0,1:T(8,128)(2,1)S(1)} %dynamic-slice_bitcast_fusion.9), channel_id=1, source_target_pairs={{0,1},{1,0},{2,3},{3,2},{4,5},{5,4},{6,7},{7,6},{8,9},{9,8},{10,11... | collective-permute-start | bytes 6291464 | tf_op jit(solution)/shard_map/ppermute | solution.py:105
  1029.7 69.9 %collective-permute-start.83 = (bf16[4,1,128,1024]{3,2,1,0:T(8,128)(2,1)S(1)}, bf16[4,1,128,1024]{3,2,1,0:T(8,128)(2,1)S(1)}, u32[]{:S(2)}, u32[]{:S(2)}) collective-permute-start(bf16[4,1,128,1024]{3,2,1,0:T(8,128)(2,1)S(1)} %constant_dynamic-slice_fusion.1), channel_id=1, source_target_pairs={{0,1},{1,0},{2,3},{3,2},{4,5},{5,4},{6,7},{7,6},{8,9},{9,8},{10,11... | collective-permute-start | bytes 3145736 | tf_op jit(solution)/shard_map/ppermute | solution.py:105
  1034.8 65.3 %collective-permute-start.78 = (bf16[4,1,32,4096]{3,2,0,1:T(8,128)(2,1)S(1)}, bf16[4,1,32,4096]{3,2,0,1:T(8,128)(2,1)S(1)}, u32[]{:S(2)}, u32[]{:S(2)}) collective-permute-start(bf16[4,1,32,4096]{3,2,0,1:T(8,128)(2,1)S(1)} %dynamic-slice_bitcast_fusion.12), channel_id=1, source_target_pairs={{0,2},{1,3},{2,0},{3,1},{4,6},{5,7},{6,4},{7,5},{8,10},{9,11},{10,... | collective-permute-start | bytes 3145736 | tf_op jit(solution)/shard_map/ppermute | solution.py:105
  (187 other events, 3892.1 us)

commit v2 on v0

v2 whole, which is shorter than its diff:
```python
import functools
import math

import jax
import jax.numpy as jnp
from jax import lax
from jax.experimental import pallas as pl
from jax.experimental.pallas import tpu as pltpu
from jax.sharding import PartitionSpec as P

D = 1024
HEADS = 16
HD = 64
CB = 3
LIGHT = pl.CostEstimate(flops=1, bytes_accessed=1, transcendentals=0)


def gelu_tanh(value):
    return (
        0.5
        * value
        * (1.0 + jnp.tanh(0.7978845608028654 * (value + 0.044715 * value * value * value)))
    )


def rms_scale(value, gain_vec):
    return value * lax.rsqrt(jnp.mean(value * value, axis=-1, keepdims=True) + 1e-05) * gain_vec


def over_rows(left, right):
    return lax.dot_general(
        left, right, (((0,), (0,)), ((), ())), preferred_element_type=jnp.float32
    )


def against(left, right):
    return lax.dot_general(
        left, right, (((1,), (1,)), ((), ())), preferred_element_type=jnp.float32
    )


def head_marks():
    lane = lax.broadcasted_iota(jnp.int32, (D, 128), 0) // HD
    head = lax.broadcasted_iota(jnp.int32, (D, 128), 1)
    return (lane == head).astype(jnp.bfloat16)


def head_sums(left, right, marks):
    product = left.astype(jnp.float32) * right.astype(jnp.float32)
    upper = product.astype(jnp.bfloat16)
    lower = (product - upper.astype(jnp.float32)).astype(jnp.bfloat16)
    return jnp.dot(upper, marks, preferred_element_type=jnp.float32) + jnp.dot(
        lower, marks, preferred_element_type=jnp.float32
    )


def spread(heads, marks):
    return lax.dot_general(
        heads, marks, (((1,), (1,)), ((), ())), preferred_element_type=jnp.float32
    )


def token_probs(tokens_q, tokens_k, marks):
    probs = []
    for token in range(CB):
        scores = [
            head_sums(tokens_q[token], tokens_k[other], marks) * HD ** (-0.5)
            for other in range(token + 1)
        ]
        highest = functools.reduce(jnp.maximum, scores)
        expo = [jnp.exp(score - highest) for score in scores]
        total = functools.reduce(jnp.add, expo)
        probs.append([term / total for term in expo])
    return probs


def code_attend_kernel(pair_ref, values_ref, marks_ref, out_ref):
    marks = marks_ref[...]
    query = [pair_ref[token, :, :D] for token in range(CB)]
    keys = [pair_ref[token, :, D:] for token in range(CB)]
    probs = token_probs(query, keys, marks)
    for token in range(CB):
        mixed = None
        for other in range(token + 1):
            value = values_ref[other].astype(jnp.float32)
            term = spread(probs[token][other].astype(jnp.bfloat16), marks) * value
            mixed = term if mixed is None else mixed + term
        out_ref[token] = mixed.astype(jnp.bfloat16)


def code_attend_back_kernel(
    pair_ref, values_ref, grad_ref, marks_ref, out_pair_ref, out_values_ref
):
    marks = marks_ref[...]
    query = [pair_ref[token, :, :D] for token in range(CB)]
    keys = [pair_ref[token, :, D:] for token in range(CB)]
    probs = token_probs(query, keys, marks)
    grad_scores = []
    for token in range(CB):
        grads = [
            head_sums(grad_ref[token], values_ref[other], marks)
            for other in range(token + 1)
        ]
        inner = functools.reduce(
            jnp.add, [prob * grad for prob, grad in zip(probs[token], grads)]
        )
        grad_scores.append(
            [
                (prob * (grad - inner)).astype(jnp.bfloat16)
                for prob, grad in zip(probs[token], grads)
            ]
        )
    scale = HD ** (-0.5)
    grad_keys = [None] * CB
    grad_values = [None] * CB
    for token in range(CB):
        grad_query = None
        for other in range(token + 1):
            wide = spread(grad_scores[token][other], marks)
            term = wide * keys[other].astype(jnp.float32)
            grad_query = term if grad_query is None else grad_query + term
            term = wide * query[token].astype(jnp.float32)
            grad_keys[other] = term if grad_keys[other] is None else grad_keys[other] + term
            wide = spread(probs[token][other].astype(jnp.bfloat16), marks)
            term = wide * grad_ref[token].astype(jnp.float32)
            grad_values[other] = term if grad_values[other] is None else grad_values[other] + term
        out_pair_ref[token, :, :D] = (grad_query * scale).astype(jnp.bfloat16)
    for token in range(CB):
        out_pair_ref[token, :, D:] = (grad_keys[token] * scale).astype(jnp.bfloat16)
        out_values_ref[token] = grad_values[token].astype(jnp.bfloat16)


def token_specs(step, widths):
    return [pl.BlockSpec((CB, step, width), lambda i: (0, i, 0)) for width in widths] + [
        pl.BlockSpec((D, 128), lambda i: (0, 0))
    ]


def code_attend(pair, values):
    frames = values.shape[1]
    step = math.gcd(frames, 64)
    return pl.pallas_call(
        code_attend_kernel,
        grid=(frames // step,),
        in_specs=token_specs(step, (2 * D, D)),
        out_specs=pl.BlockSpec((CB, step, D), lambda i: (0, i, 0)),
        out_shape=jax.ShapeDtypeStruct((CB, frames, D), jnp.bfloat16),
        cost_estimate=LIGHT,
        name="code_attend",
    )(pair, values, head_marks())


def code_attend_back(pair, values, grad_mixed):
    frames = values.shape[1]
    step = math.gcd(frames, 64)
    return pl.pallas_call(
        code_attend_back_kernel,
        grid=(frames // step,),
        in_specs=token_specs(step, (2 * D, D, D)),
        out_specs=[
            pl.BlockSpec((CB, step, 2 * D), lambda i: (0, i, 0)),
            pl.BlockSpec((CB, step, D), lambda i: (0, i, 0)),
        ],
        out_shape=[
            jax.ShapeDtypeStruct((CB, frames, 2 * D), jnp.bfloat16),
            jax.ShapeDtypeStruct((CB, frames, D), jnp.bfloat16),
        ],
        cost_estimate=LIGHT,
        name="code_attend_back",
    )(pair, values, grad_mixed, head_marks())


def frame_mask(column_ref, row_ref):
    frames = column_ref.shape[0]
    shape = (frames, frames)
    earlier = lax.broadcasted_iota(jnp.int32, shape, 0) >= lax.broadcasted_iota(
        jnp.int32, shape, 1
    )
    return earlier & (column_ref[...] == row_ref[...])


def frame_probs(query, keys, allowed):
    scores = against(query, keys) * HD ** (-0.5)
    scores = jnp.where(allowed, scores, -1e30)
    highest = jnp.max(scores, axis=-1, keepdims=True)
    expo = jnp.exp(scores - highest)
    return expo / jnp.sum(expo, axis=-1, keepdims=True)


def half_lanes(value, upper):
    lane = lax.broadcasted_iota(jnp.int32, value.shape, 1)
    chosen = (lane >= HD) if upper else (lane < HD)
    return jnp.where(chosen, value, jnp.zeros_like(value))


def frame_attend_kernel(query_ref, keys_ref, values_ref, column_ref, row_ref, out_ref):
    allowed = frame_mask(column_ref, row_ref)
    mixed = None
    for upper in (False, True):
        probs = frame_probs(half_lanes(query_ref[...], upper), keys_ref[...], allowed)
        term = jnp.dot(
            probs.astype(jnp.bfloat16),
            half_lanes(values_ref[...], upper),
            preferred_element_type=jnp.float32,
        )
        mixed = term if mixed is None else mixed + term
    out_ref[...] = mixed.astype(jnp.bfloat16)


def frame_attend_back_kernel(
    query_ref, keys_ref, values_ref, grad_ref, column_ref, row_ref, out_pair_ref, out_values_ref
):
    allowed = frame_mask(column_ref, row_ref)
    scale = HD ** (-0.5)
    grads = [None, None, None]
    for upper in (False, True):
        query = half_lanes(query_ref[...], upper)
        keys = half_lanes(keys_ref[...], upper)
        grad_out = half_lanes(grad_ref[...], upper)
        probs = frame_probs(query, keys, allowed)
        grad_probs = against(grad_out, values_ref[...])
        inner = jnp.sum(probs * grad_probs, axis=-1, keepdims=True)
        grad_scores = (probs * (grad_probs - inner)).astype(jnp.bfloat16)
        terms = (
            jnp.dot(grad_scores, keys, preferred_element_type=jnp.float32) * scale,
            over_rows(grad_scores, query) * scale,
            over_rows(probs.astype(jnp.bfloat16), grad_out),
        )
        grads = [term if grad is None else grad + term for grad, term in zip(grads, terms)]
    start = pl.multiple_of(pl.program_id(0) * 2 * HD, 2 * HD)
    out_pair_ref[:, pl.ds(start, 2 * HD)] = grads[0].astype(jnp.bfloat16)
    out_pair_ref[:, pl.ds(D + start, 2 * HD)] = grads[1].astype(jnp.bfloat16)
    out_values_ref[...] = grads[2].astype(jnp.bfloat16)


def pair_specs(frames, extra):
    pairs = HEADS // 2
    block = (frames, 2 * HD)
    return (
        [
            pl.BlockSpec(block, lambda j: (0, j)),
            pl.BlockSpec(block, lambda j: (0, j + pairs)),
        ]
        + [pl.BlockSpec(block, lambda j: (0, j))] * extra
        + [
            pl.BlockSpec((frames, 1), lambda j: (0, 0)),
            pl.BlockSpec((1, frames), lambda j: (0, 0)),
        ]
    )


def frame_attend(pair, values, segments):
    frames = values.shape[0]
    return pl.pallas_call(
        frame_attend_kernel,
        grid=(HEADS // 2,),
        in_specs=pair_specs(frames, 1),
        out_specs=pl.BlockSpec((frames, 2 * HD), lambda j: (0, j)),
        out_shape=jax.ShapeDtypeStruct((frames, D), jnp.bfloat16),
        cost_estimate=LIGHT,
        name="frame_attend",
    )(pair, pair, values, segments.reshape(frames, 1), segments.reshape(1, frames))


def frame_attend_back(pair, values, grad_mixed, segments):
    frames = values.shape[0]
    return pl.pallas_call(
        frame_attend_back_kernel,
        grid=(HEADS // 2,),
        in_specs=pair_specs(frames, 2),
        out_specs=[
            pl.BlockSpec((frames, 2 * D), lambda j: (0, 0)),
            pl.BlockSpec((frames, 2 * HD), lambda j: (0, j)),
        ],
        out_shape=[
            jax.ShapeDtypeStruct((frames, 2 * D), jnp.bfloat16),
            jax.ShapeDtypeStruct((frames, D), jnp.bfloat16),
        ],
        cost_estimate=LIGHT,
        name="frame_attend_back",
    )(
        pair,
        pair,
        values,
        grad_mixed,
        segments.reshape(frames, 1),
        segments.reshape(1, frames),
    )


def bit_masks(sizes):
    count = sizes[0] * sizes[1]
    masks = []
    step = count // 2
    while step >= 1:
        masks.append(step)
        step //= 2
    return masks, masks.index(sizes[1])


def swap(value, mask, sizes):
    count = sizes[0] * sizes[1]
    return lax.ppermute(value, ("gx", "gy"), [(place, place ^ mask) for place in range(count)])


def device_index(sizes):
    return lax.axis_index("gx") * sizes[1] + lax.axis_index("gy")


def far_groups(sizes):
    masks, core = bit_masks(sizes)
    far = [mask for place, mask in enumerate(masks[:-2]) if place != core]
    return [far[start : start + 2] for start in range(0, len(far), 2)]


def combined(group):
    found = []
    for index in range(2 ** len(group)):
        mask = 0
        for place, bit in enumerate(group):
            if (index >> (len(group) - 1 - place)) & 1:
                mask |= bit
        found.append(mask)
    return found


def small_index(group, sizes):
    me = device_index(sizes)
    index = jnp.zeros((), jnp.int32)
    for bit in group:
        index = index * 2 + ((me // bit) % 2).astype(jnp.int32)
    return index


def place_far_kernel(place_ref, *refs):
    for index, ref in enumerate(refs[:-1]):
        refs[-1][0, place_ref[0] ^ index] = ref[0]


def placed_far(pieces, place):
    planes, rows, cols = pieces[0].shape
    slots = len(pieces)
    return pl.pallas_call(
        place_far_kernel,
        grid_spec=pltpu.PrefetchScalarGridSpec(
            num_scalar_prefetch=1,
            grid=(planes,),
            in_specs=[pl.BlockSpec((1, rows, cols), lambda i, place_ref: (i, 0, 0))] * slots,
            out_specs=pl.BlockSpec((1, slots, rows, cols), lambda i, place_ref: (i, 0, 0, 0)),
        ),
        out_shape=jax.ShapeDtypeStruct((planes, slots, rows, cols), pieces[0].dtype),
        cost_estimate=LIGHT,
        name="place_far",
    )(place.reshape(1), *pieces)


def place_near_kernel(place_ref, *refs):
    for index, ref in enumerate(refs[:-1]):
        refs[-1][0, place_ref[1] ^ (index // 4), 0, place_ref[0] ^ (index % 4)] = ref[0]


def place_near_tail_kernel(place_ref, *refs):
    cols = refs[-2].shape[-1]
    for index, ref in enumerate(refs[:-2]):
        slot = (0, place_ref[1] ^ (index // 4), 0, place_ref[0] ^ (index % 4))
        refs[-2][slot] = ref[0, :, :cols]
        refs[-1][slot] = ref[0, :, cols:]


def placed_near(pieces, near_place, core_place, group, high, low, tail):
    rows, cols = pieces[0].shape[1:]
    widths = [cols - tail, tail] if tail else [cols]
    offset = group * high * low
    outs = pl.pallas_call(
        place_near_tail_kernel if tail else place_near_kernel,
        grid_spec=pltpu.PrefetchScalarGridSpec(
            num_scalar_prefetch=1,
            grid=(high * low,),
            in_specs=[pl.BlockSpec((1, rows, cols), lambda i, place_ref: (i + offset, 0, 0))] * 8,
            out_specs=[
                pl.BlockSpec(
                    (1, 2, 1, 4, rows, width),
                    lambda i, place_ref: (i // low, 0, i % low, 0, 0, 0),
                )
                for width in widths
            ],
        ),
        out_shape=[
            jax.ShapeDtypeStruct((high, 2, low, 4, rows, width), pieces[0].dtype)
            for width in widths
        ],
        cost_estimate=LIGHT,
        name="place_near",
    )(jnp.stack([near_place, core_place]), *pieces)
    return [out.reshape(high * 2 * low * 4 * rows, out.shape[-1]) for out in outs]


def pinned(*values):
    return lax.optimization_barrier(values)


class Gather:
    def __init__(self, shard, sizes, flip, tail=0):
        self.sizes = sizes
        self.tail = tail
        self.groups, self.rows, self.cols = shard.shape
        self.state = shard
        self.far = far_groups(sizes)
        masks, core = bit_masks(sizes)
        self.near = masks[-2:]
        self.first, self.second = (2, 1) if not flip else (1, 2)
        self.core = masks[core]
        self.high = 2**core
        self.low = 2 ** (len(masks) - core - 3)
        self.pieces = None
        self.received = None
        self.stage = -len(self.far)

    def flown(self, value, mask):
        return swap(value, mask, self.sizes)

    def send(self):
        if self.stage < 0:
            masks = combined(self.far[self.stage])
            self.received = [self.flown(self.state, mask) for mask in masks[1:]]
        elif self.stage == 0:
            mask = combined(self.near)[self.first]
            self.received = [self.flown(self.pieces[0], mask)]
        elif self.stage == 1:
            mask = combined(self.near)[self.second]
            self.received = [self.flown(self.pieces[index], mask) for index in (0, self.first)]
        else:
            self.received = [self.flown(piece, self.core) for piece in self.pieces]

    def take(self):
        if self.stage < 0:
            group = self.far[self.stage]
            wide = placed_far(
                [
                    value.reshape(-1, self.rows, self.cols)
                    for value in [self.state] + list(self.received)
                ],
                small_index(group, self.sizes),
            )
            self.state = wide.reshape(-1, self.rows, self.cols)
            if self.stage == -1:
                self.pieces = [self.state, None, None, None]
        elif self.stage == 0:
            self.pieces[self.first] = self.received[0]
        elif self.stage == 1:
            self.pieces[self.second] = self.received[0]
            self.pieces[3] = self.received[1]
        else:
            near_place = small_index(self.near, self.sizes)
            core_place = small_index([self.core], self.sizes)
            outs = [
                placed_near(
                    self.pieces + list(self.received),
                    near_place,
                    core_place,
                    group,
                    self.high,
                    self.low,
                    self.tail,
                )
                for group in range(self.groups)
            ]
            self.whole = [out[0] for out in outs]
            self.tails = [out[-1] for out in outs]
        self.received = None
        self.stage += 1


def ended(chains, *others):
    flat = [value for chain in chains for value in chain.received]
    held = list(pinned(*flat, *others))
    for chain in chains:
        count = len(chain.received)
        chain.received, held = held[:count], held[count:]
        chain.take()
    return held


def started(chains):
    for chain in chains:
        chain.send()


def half_kernel(side_ref, acts_ref, grad_ref, out_ref):
    out_ref[...] = over_rows(acts_ref[...], grad_ref[...]).astype(jnp.bfloat16)


def half_add_kernel(side_ref, acts_ref, grad_ref, add_ref, out_ref):
    total = over_rows(acts_ref[...], grad_ref[...]) + add_ref[...].astype(jnp.float32)
    out_ref[...] = total.astype(jnp.bfloat16)


def half_product(acts, grad, sizes, received):
    masks, core = bit_masks(sizes)
    rows, inner = acts.shape
    cols = grad.shape[1]
    segment = inner // (2 * 2**core)
    tile = math.gcd(segment, 512)
    parts = segment // tile
    wide = math.gcd(cols, 1024)
    side = small_index([masks[core]], sizes)
    if received is None:
        side = 1 - side

    def acts_at(i, j, side_ref):
        return (0, (i // parts) * 2 * parts + side_ref[0] * parts + i % parts)

    specs = [
        pl.BlockSpec((rows, tile), acts_at),
        pl.BlockSpec((rows, wide), lambda i, j, side_ref: (0, j)),
    ]
    out_spec = pl.BlockSpec((tile, wide), lambda i, j, side_ref: (i, j))
    operands = [acts, grad]
    if received is not None:
        specs.append(out_spec)
        operands.append(received)
    return pl.pallas_call(
        half_kernel if received is None else half_add_kernel,
        grid_spec=pltpu.PrefetchScalarGridSpec(
            num_scalar_prefetch=1,
            grid=(inner // (2 * tile), cols // wide),
            in_specs=specs,
            out_specs=out_spec,
        ),
        out_shape=jax.ShapeDtypeStruct((inner // 2, cols), jnp.bfloat16),
        cost_estimate=LIGHT,
        name="half_away" if received is None else "half_kept",
    )(side.reshape(1), *operands)


class Core:
    def __init__(self, acts, grad, sizes):
        masks, core = bit_masks(sizes)
        self.mask, self.sizes = masks[core], sizes
        self.acts, self.grad = acts, grad
        self.away = [half_product(acts, grad, sizes, None)]
        self.received = None
        self.theirs = None

    def send(self):
        self.received = [swap(self.away[0], self.mask, self.sizes)]

    def take(self):
        self.theirs = self.received[0]
        self.received = None
        self.away = []


class Scatter:
    def __init__(self, states, sizes, flip):
        self.sizes = sizes
        masks, core = bit_masks(sizes)
        self.bits = [mask for place, mask in enumerate(masks) if place != core]
        first, second = masks[-1], masks[-2]
        if flip:
            first, second = second, first
        self.todo = [[first], [second]] + far_groups(sizes)[::-1]
        count = 2 ** len(self.bits)
        self.states = [
            state.reshape(count, state.shape[0] // count, state.shape[1]) for state in states
        ]
        self.received = None
        self.prepare()

    def prepare(self):
        group = self.todo[0]
        first = self.bits.index(group[0])
        self.bits = [bit for bit in self.bits if bit not in group]
        slots = 2 ** len(group)
        high = 2**first
        place = small_index(group, self.sizes)
        self.kept = []
        aways = []
        for state in self.states:
            blocks, rows, cols = state.shape
            view = state.reshape(high, slots, blocks // (high * slots), rows, cols)
            parts = [
                lax.dynamic_index_in_dim(view, place ^ index, 1, keepdims=False).reshape(
                    blocks // slots, rows, cols
                )
                for index in range(slots)
            ]
            self.kept.append(parts[0])
            aways.append(parts[1:])
        self.away = [
            jnp.stack([away[index] for away in aways]) for index in range(slots - 1)
        ]
        self.todo = self.todo[1:]
        self.masks = combined(group)[1:]

    def send(self):
        self.received = [swap(away, mask, self.sizes) for away, mask in zip(self.away, self.masks)]

    def take(self):
        last = not self.todo
        self.states = []
        for index, kept in enumerate(self.kept):
            total = kept.astype(jnp.float32)
            for value in self.received:
                total = total + value[index].astype(jnp.float32)
            self.states.append(total.astype(jnp.float32 if last else jnp.bfloat16))
        self.received = None
        self.away = []
        if not last:
            self.prepare()


def split_kernel(flip, side_ref, acts_ref, grad_ref, add_ref, kept_ref, away_ref):
    total = over_rows(acts_ref[...], grad_ref[...]) + add_ref[...].astype(jnp.float32)
    half, rows, cols = kept_ref.shape
    total = total.astype(jnp.bfloat16)
    parts = [[], []]
    for index in range(2 * half):
        bit = (index // 2) % 2 if flip else index % 2
        parts[bit].append(total[index * rows : (index + 1) * rows])

    @pl.when(side_ref[1] == 0)
    def _():
        for index in range(half):
            kept_ref[index] = parts[0][index]
            away_ref[index] = parts[1][index]

    @pl.when(side_ref[1] != 0)
    def _():
        for index in range(half):
            kept_ref[index] = parts[1][index]
            away_ref[index] = parts[0][index]


def split_product(acts, grad, theirs, sizes, flip, start, cols):
    masks, core = bit_masks(sizes)
    devices = sizes[0] * sizes[1]
    rows, inner = acts.shape
    block = inner // devices
    segment = inner // (2 * 2**core)
    tile = math.gcd(segment, 512)
    parts = segment // tile
    wide = math.gcd(cols, 1024)
    shift = start // wide
    first = masks[-2] if flip else masks[-1]
    sides = jnp.stack([small_index([masks[core]], sizes), small_index([first], sizes)])
    half = tile // (2 * block)
    out_spec = pl.BlockSpec((half, block, wide), lambda i, j, side_ref: (i, 0, j))
    out_shape = jax.ShapeDtypeStruct((devices // 4, block, cols), jnp.bfloat16)
    return pl.pallas_call(
        functools.partial(split_kernel, flip),
        grid_spec=pltpu.PrefetchScalarGridSpec(
            num_scalar_prefetch=1,
            grid=(inner // (2 * tile), cols // wide),
            in_specs=[
                pl.BlockSpec(
                    (rows, tile),
                    lambda i, j, side_ref: (
                        0,
                        (i // parts) * 2 * parts + side_ref[0] * parts + i % parts,
                    ),
                ),
                pl.BlockSpec((rows, wide), lambda i, j, side_ref: (0, j + shift)),
                pl.BlockSpec((tile, wide), lambda i, j, side_ref: (i, j + shift)),
            ],
            out_specs=[out_spec, out_spec],
        ),
        out_shape=[out_shape, out_shape],
        cost_estimate=LIGHT,
        name="split_product",
    )(sides, acts, grad, theirs)


def add_split_kernel(side_ref, kept_ref, kept_add_ref, away_ref, away_add_ref, *outs):
    for out, one, two in ((outs[0], kept_ref, kept_add_ref), (outs[1], away_ref, away_add_ref)):
        total = one[:, 0].astype(jnp.float32) + two[:, 0].astype(jnp.float32)
        out[...] = total.astype(jnp.bfloat16)


def add_split(kept, received, bit):
    blocks, rows, cols = kept.shape
    shape = (blocks // 2, 2, rows, cols)
    kept, received = kept.reshape(shape), received.reshape(shape)
    part = math.gcd(blocks // 2, 4)
    stays = pl.BlockSpec((part, 1, rows, cols), lambda i, side_ref: (i, side_ref[0], 0, 0))
    goes = pl.BlockSpec((part, 1, rows, cols), lambda i, side_ref: (i, 1 - side_ref[0], 0, 0))
    out_spec = pl.BlockSpec((part, rows, cols), lambda i, side_ref: (i, 0, 0))
    out_shape = jax.ShapeDtypeStruct((blocks // 2, rows, cols), kept.dtype)
    return pl.pallas_call(
        add_split_kernel,
        grid_spec=pltpu.PrefetchScalarGridSpec(
            num_scalar_prefetch=1,
            grid=(blocks // (2 * part),),
            in_specs=[stays, stays, goes, goes],
            out_specs=[out_spec, out_spec],
        ),
        out_shape=[out_shape, out_shape],
        cost_estimate=LIGHT,
        name="add_split",
    )(bit.reshape(1), kept, received, kept, received)


def add_far_kernel(count, place_ref, *refs):
    outs = refs[2 * count :]
    for slot, out in enumerate(outs):

        @pl.when(pl.program_id(0) == slot)
        def _(out=out):
            start = 0
            for one, two in zip(refs[:count], refs[count : 2 * count]):
                total = one[0].astype(jnp.float32) + two[0].astype(jnp.float32)
                width = total.shape[-1]
                out[:, start : start + width] = total.astype(jnp.bfloat16)
                start += width


def add_far(kept, received, place, slots):
    rows = kept[0].shape[1]
    width = sum(value.shape[2] for value in kept)
    specs = [
        pl.BlockSpec((1, rows, value.shape[2]), lambda i, place_ref: (place_ref[0] ^ i, 0, 0))
        for value in kept
    ]
    return pl.pallas_call(
        functools.partial(add_far_kernel, len(kept)),
        grid_spec=pltpu.PrefetchScalarGridSpec(
            num_scalar_prefetch=1,
            grid=(slots,),
            in_specs=specs + specs,
            out_specs=[pl.BlockSpec((rows, width), lambda i, place_ref: (0, 0))] * slots,
        ),
        out_shape=[jax.ShapeDtypeStruct((rows, width), kept[0].dtype)] * slots,
        cost_estimate=LIGHT,
        name="add_far",
    )(place.reshape(1), *kept, *received)


class Joint:
    def __init__(self, parts, sizes):
        self.sizes = sizes
        masks, core = bit_masks(sizes)
        self.near = masks[-2:]
        self.far = far_groups(sizes)[0]
        self.flips = [flip for exchange, flip, start, cols in parts]
        pairs = [
            split_product(
                exchange.acts, exchange.grad, exchange.theirs, sizes, flip, start, cols
            )
            for exchange, flip, start, cols in parts
        ]
        self.kept = [pair[0] for pair in pairs]
        self.away = [pair[1] for pair in pairs]
        self.masks = [self.near[0] if flip else self.near[1] for flip in self.flips]
        self.received = None
        self.stage = 0

    def send(self):
        self.received = [swap(away, mask, self.sizes) for away, mask in zip(self.away, self.masks)]

    def take(self):
        received, self.received = self.received, None
        self.stage += 1
        if self.stage == 1:
            self.masks = [self.near[1] if flip else self.near[0] for flip in self.flips]
            pairs = [
                add_split(kept, value, small_index([mask], self.sizes))
                for kept, value, mask in zip(self.kept, received, self.masks)
            ]
            self.kept = [pair[0] for pair in pairs]
            self.away = [pair[1] for pair in pairs]
        elif self.stage == 2:
            self.masks = combined(self.far)[1:]
            outs = add_far(
                self.kept, received, small_index(self.far, self.sizes), 2 ** len(self.far)
            )
            self.kept, self.away = outs[0], list(outs[1:])
        else:
            total = self.kept.astype(jnp.float32)
            for value in received:
                total = total + value.astype(jnp.float32)
            self.total = total
            self.away = []

    def result(self):
        return self.total


class Plain:
    def __init__(self, parts, sizes):
        self.chains = []
        for exchange, flip, start, cols in parts:
            kept = half_product(exchange.acts, exchange.grad, sizes, exchange.theirs)
            self.chains.append(Scatter([kept[:, start : start + cols]], sizes, flip))
        self.received = None

    @property
    def away(self):
        return [away for chain in self.chains for away in chain.away]

    @away.setter
    def away(self, values):
        values = list(values)
        for chain in self.chains:
            count = len(chain.away)
            chain.away, values = values[:count], values[count:]

    def send(self):
        for chain in self.chains:
            chain.send()
        self.received = [value for chain in self.chains for value in chain.received]

    def take(self):
        values, self.received = list(self.received), None
        for chain in self.chains:
            count = len(chain.received)
            chain.received, values = values[:count], values[count:]
            chain.take()

    def result(self):
        return jnp.concatenate([chain.states[0][0] for chain in self.chains], axis=1)


def summed(parts, sizes):
    heights = [exchange.acts.shape[1] // (sizes[0] * sizes[1]) for exchange, *unused in parts]
    if len(far_groups(sizes)) == 1 and all(height % 16 == 0 for height in heights):
        return Joint(parts, sizes)
    return Plain(parts, sizes)


class VectorScatter:
    def __init__(self, terms, sizes):
        self.sizes = sizes
        masks, core = bit_masks(sizes)
        self.bits = masks
        self.todo = [masks[core]] + [mask for mask in masks[::-1] if mask != masks[core]]
        self.state = terms
        self.received = None
        self.prepare()

    def prepare(self):
        bit = self.todo[0]
        high = 2 ** self.bits.index(bit)
        self.bits = [other for other in self.bits if other != bit]
        view = self.state.reshape(high, 2, -1, self.state.shape[-1])
        place = small_index([bit], self.sizes)
        away = lax.dynamic_index_in_dim(view, 1 - place, 1, keepdims=False)
        kept = lax.dynamic_index_in_dim(view, place, 1, keepdims=False)
        self.away = [away.reshape(-1, away.shape[-1])]
        self.kept = kept.reshape(-1, kept.shape[-1])
        self.mask = bit
        self.todo = self.todo[1:]

    def send(self):
        self.received = [swap(self.away[0], self.mask, self.sizes)]

    def take(self):
        self.state = self.kept + self.received[0]
        self.received = None
        self.away = []
        if self.todo:
            self.prepare()


def scatter_round(ending, starting, *others):
    ending = [chain for chain in ending if chain.received is not None]
    others = ended(ending, *others)
    going = [chain for chain in starting if chain.away and chain.received is None]
    flat = [value for chain in going for value in chain.away]
    held = list(pinned(*flat, *others))
    for chain in going:
        count = len(chain.away)
        chain.away, held = held[:count], held[count:]
        chain.send()
    return held


def gelu_and_slope(preact):
    square = preact * preact
    bent = jnp.tanh(preact * (0.7978845608028654 + (0.7978845608028654 * 0.044715) * square))
    half = 0.5 + 0.5 * bent
    value = preact * half
    inner = 0.7978845608028654 + (3 * 0.7978845608028654 * 0.044715) * square
    slope = half + value * (1.0 - bent) * inner
    return value.astype(jnp.bfloat16), slope.astype(jnp.bfloat16)


def times(left, right):
    return jnp.dot(left, right, preferred_element_type=jnp.float32)


def grad_pre_kernel(grad_ref, weight_ref, slope_ref, out_ref, bias_ref):
    weight = weight_ref[...]
    total = None
    for start in range(0, grad_ref.shape[0], 256):
        grad_act = against(grad_ref[start : start + 256], weight)
        slope = slope_ref[start : start + 256].astype(jnp.float32)
        grad_pre = (grad_act * slope).astype(jnp.bfloat16)
        out_ref[start : start + 256] = grad_pre
        term = jnp.sum(grad_pre.astype(jnp.float32), axis=0, keepdims=True)
        total = term if total is None else total + term
    bias_ref[...] = total


def grad_two_kernel(grad_ref, weight_ref, out_ref):
    term = against(grad_ref[...], weight_ref[...])

    @pl.when(pl.program_id(0) == 0)
    def _():
        out_ref[...] = term

    @pl.when(pl.program_id(0) != 0)
    def _():
        out_ref[...] += term


def grad_two_of(grad_pre, w_up):
    rows, hidden = grad_pre.shape
    width = w_up.shape[0]
    tile = 1024
    return pl.pallas_call(
        grad_two_kernel,
        grid=(hidden // tile,),
        in_specs=[
            pl.BlockSpec((rows, tile), lambda i: (0, i)),
            pl.BlockSpec((width, tile), lambda i: (0, i)),
        ],
        out_specs=pl.BlockSpec((rows, width), lambda i: (0, 0)),
        out_shape=jax.ShapeDtypeStruct((rows, width), jnp.float32),
        cost_estimate=LIGHT,
        name="grad_two",
    )(grad_pre, w_up)


def grad_pre_of(grad_low, w_down, slope):
    rows, width = grad_low.shape
    hidden = w_down.shape[0]
    tile = 1024
    grad_pre, bias = pl.pallas_call(
        grad_pre_kernel,
        grid=(hidden // tile,),
        in_specs=[
            pl.BlockSpec((rows, width), lambda i: (0, 0)),
            pl.BlockSpec((tile, width), lambda i: (i, 0)),
            pl.BlockSpec((rows, tile), lambda i: (0, i)),
        ],
        out_specs=[
            pl.BlockSpec((rows, tile), lambda i: (0, i)),
            pl.BlockSpec((1, tile), lambda i: (0, i)),
        ],
        out_shape=[
            jax.ShapeDtypeStruct((rows, hidden), jnp.bfloat16),
            jax.ShapeDtypeStruct((1, hidden), jnp.float32),
        ],
        cost_estimate=LIGHT,
        name="grad_pre",
    )(grad_low, w_down, slope)
    return grad_pre, bias.reshape(hidden)


def local(
    sizes,
    frame_input,
    code_embed,
    segment_ids,
    frame_cotangent,
    code_cotangent,
    frame_prenorm,
    frame_query,
    frame_keys,
    frame_values,
    frame_outproj,
    frame_midnorm,
    frame_upproj,
    frame_upbias,
    frame_downproj,
    frame_downbias,
    code_prenorm,
    code_query,
    code_keys,
    code_values,
    code_outproj,
    code_midnorm,
    code_upproj,
    code_upbias,
    code_downproj,
    code_downbias,
):
    low = jnp.bfloat16
    frames = frame_input.shape[0]
    devices = sizes[0] * sizes[1]
    vectors = (
        frame_prenorm,
        frame_midnorm,
        frame_upbias,
        frame_downbias,
        code_prenorm,
        code_midnorm,
        code_upbias,
        code_downbias,
    )
    widths = [vec.shape[0] for vec in vectors]

    def weight(shard, flip):
        return Gather(shard, sizes, flip)

    f_a = weight(jnp.concatenate([frame_query, frame_keys], axis=1)[None], False)
    shard_rows = frame_values.shape[0]
    packed = jnp.concatenate([vec[None] for vec in vectors], axis=1)
    packed = jnp.pad(packed, ((0, 0), (0, shard_rows * 128 - packed.shape[1])))
    packed = packed.reshape(shard_rows, 128)
    f_b = Gather(
        jnp.stack(
            [
                jnp.concatenate([frame_values, packed], axis=1),
                jnp.concatenate([frame_outproj, packed], axis=1),
            ]
        ),
        sizes,
        True,
        128,
    )
    f_u = weight(frame_upproj[None], False)
    f_d = weight(frame_downproj[None], True)
    c_a = weight(jnp.concatenate([code_query, code_keys], axis=1)[None], False)
    c_b = weight(jnp.stack([code_values, code_outproj]), True)
    c_u = weight(code_upproj[None], False)
    c_d = weight(code_downproj[None], True)
    f_attn, f_ff, c_attn, c_ff = [f_a, f_b], [f_u, f_d], [c_a, c_b], [c_u, c_d]

    for unused in range(len(f_a.far) - 1):
        for chains in (f_attn, f_ff, c_attn, c_ff):
            started(chains)
            ended(chains)
    started(f_attn)
    ended(f_attn)
    started(f_attn + f_ff)
    ended(f_attn)
    started(f_attn)
    ended(f_attn + f_ff)
    started(f_attn + f_ff + c_attn)
    ended(f_attn + f_ff + c_attn)
    started(f_ff)
    whole = f_b.tails[0].reshape(devices, -1)[:, : sum(widths)].astype(jnp.float32)
    gains = []
    start = 0
    for width in widths:
        gains.append(whole[:, start : start + width].reshape(devices * width))
        start += width
    frame_gains = tuple(gains[:4])
    code_gains = tuple(gains[4:])
    frame_x = frame_input.astype(jnp.float32)
    f_normed = rms_scale(frame_x, frame_gains[0]).astype(low)
    f_pair = f_a.whole[0]
    f_value, f_out = f_b.whole

    segments = segment_ids[0]
    f_qk = times(f_normed, f_pair).astype(low)
    f_v = times(f_normed, f_value).astype(low)
    f_mixed = frame_attend(f_qk, f_v, segments)
    f_hidden = frame_x + times(f_mixed, f_out)
    f_normed_two = rms_scale(f_hidden, frame_gains[1]).astype(low)
    f_hidden, f_normed_two = ended(f_ff, f_hidden, f_normed_two)
    started(f_ff + c_attn + c_ff)
    code_rows = jnp.swapaxes(code_embed, 0, 1)
    grad_code_y = jnp.swapaxes(code_cotangent, 0, 1)
    code_rows, grad_code_y = ended(f_ff + c_attn, code_rows, grad_code_y)
    started(c_attn)
    (f_up,) = f_u.whole
    (f_down,) = f_d.whole
    f_act, f_slope = gelu_and_slope(times(f_normed_two, f_up) + frame_gains[2])
    rows = CB * frames
    grad_code_y = grad_code_y.reshape(rows, D)
    f_act, f_slope = ended(c_attn + c_ff, f_act, f_slope)
    started(c_attn + c_ff)
    frame_y = f_hidden + (times(f_act, f_down) + frame_gains[3])

    code_x = (code_rows.astype(jnp.float32) + frame_y[None]).reshape(rows, D)
    c_normed = rms_scale(code_x, code_gains[0]).astype(low)
    c_normed, code_x = ended(c_attn + c_ff, c_normed, code_x)
    started(c_ff)
    c_pair = c_a.whole[0]
    c_value, c_out = c_b.whole

    def tokens_of(value):
        return value.reshape(CB, frames, value.shape[-1])

    c_qk = times(c_normed, c_pair).astype(low)
    c_v = times(c_normed, c_value).astype(low)
    c_qk, c_v = ended(c_ff, c_qk, c_v)
    started(c_ff)
    c_mixed = code_attend(tokens_of(c_qk), tokens_of(c_v)).reshape(rows, D)
    c_hidden = code_x + times(c_mixed, c_out)
    c_normed_two = rms_scale(c_hidden, code_gains[1]).astype(low)
    c_hidden, c_normed_two = ended([c_u], c_hidden, c_normed_two)
    (c_up,) = c_u.whole
    c_act, c_slope = gelu_and_slope(times(c_normed_two, c_up) + code_gains[2])
    c_act, c_slope = ended([c_d], c_act, c_slope)
    (c_down,) = c_d.whole

    def both(exchange):
        half = exchange.grad.shape[1] // 2
        return [summed([(exchange, True, 0, half), (exchange, False, half, half)], sizes)]

    def attention_sums(pair, value, outproj):
        parts = [(pair, False, 0, 2 * D), (value, True, 0, D), (outproj, True, 0, D)]
        return [summed(parts, sizes)]

    def norm_back(grad_out, inputs, gain):
        unused, back = jax.vjp(rms_scale, inputs, gain)
        return back(grad_out)

    grad_low = grad_code_y
    c_d_core = Core(c_act, grad_low, sizes)
    c_slope, grad_low = scatter_round([], [c_d_core], c_slope, grad_low)
    c_grad_b_down = jnp.sum(grad_low.astype(jnp.float32), axis=0)
    (c_grad_b_down,) = ended([c_d_core], c_grad_b_down)
    c_d_chain = both(c_d_core)
    c_slope, grad_low = scatter_round([], c_d_chain, c_slope, grad_low)
    grad_pre, c_grad_b_up = grad_pre_of(grad_low, c_down, c_slope)
    c_u_core = Core(c_normed_two, grad_pre, sizes)
    (grad_pre,) = scatter_round(c_d_chain, c_d_chain + [c_u_core], grad_pre)
    grad_two = grad_two_of(grad_pre, c_up)
    (grad_two,) = scatter_round(c_d_chain + [c_u_core], c_d_chain, grad_two)
    c_u_chain = both(c_u_core)
    grad_part, c_grad_mid = norm_back(grad_two, c_hidden, code_gains[1])
    grad_hidden = grad_low.astype(jnp.float32) + grad_part
    grad_attn = grad_hidden.astype(low)
    grad_attn, grad_hidden = scatter_round(c_d_chain, c_u_chain, grad_attn, grad_hidden)
    c_o_core = Core(c_mixed, grad_attn, sizes)
    grad_mixed = against(grad_attn, c_out).astype(low)
    grad_pair, grad_values = code_attend_back(
        tokens_of(c_qk), tokens_of(c_v), tokens_of(grad_mixed)
    )
    grad_pair = grad_pair.reshape(rows, 2 * D)
    grad_values = grad_values.reshape(rows, D)
    grad_pair, grad_values = scatter_round(
        c_u_chain, c_u_chain + [c_o_core], grad_pair, grad_values
    )
    c_p_core = Core(c_normed, grad_pair, sizes)
    c_v_core = Core(c_normed, grad_values, sizes)
    grad_pair, grad_values = scatter_round(
        c_u_chain + [c_o_core], c_u_chain + [c_p_core, c_v_core], grad_pair, grad_values
    )
    grad_normed = against(grad_pair, c_pair) + against(grad_values, c_value)
    grad_part, c_grad_pre = norm_back(grad_normed, code_x, code_gains[0])
    grad_code_x = grad_hidden + grad_part
    grad_frame_y = frame_cotangent.astype(jnp.float32) + jnp.sum(tokens_of(grad_code_x), axis=0)
    grad_code_x, grad_frame_y = ended(
        c_u_chain + [c_p_core, c_v_core], grad_code_x, grad_frame_y
    )
    c_ab = attention_sums(c_p_core, c_v_core, c_o_core)
    (grad_frame_y,) = scatter_round([], c_ab, grad_frame_y)

    grad_low = grad_frame_y.astype(low)
    f_d_core = Core(f_act, grad_low, sizes)
    grad_pre, f_grad_b_up = grad_pre_of(grad_low, f_down, f_slope)
    f_u_core = Core(f_normed_two, grad_pre, sizes)
    (grad_pre,) = scatter_round(c_ab, c_ab + [f_d_core, f_u_core], grad_pre)
    grad_two = grad_two_of(grad_pre, f_up)
    grad_part, f_grad_mid = norm_back(grad_two, f_hidden, frame_gains[1])
    grad_hidden = grad_frame_y + grad_part
    grad_attn = grad_hidden.astype(low)
    grad_attn, grad_hidden = scatter_round(
        c_ab + [f_d_core, f_u_core], c_ab, grad_attn, grad_hidden
    )
    f_d_chain = both(f_d_core)
    grad_attn, grad_hidden = scatter_round(c_ab, f_d_chain, grad_attn, grad_hidden)
    f_u_chain = both(f_u_core)
    f_o_core = Core(f_mixed, grad_attn, sizes)
    grad_mixed = against(grad_attn, f_out).astype(low)
    grad_pair, grad_values = frame_attend_back(f_qk, f_v, grad_mixed, segments)
    grad_pair, grad_values = scatter_round(
        f_d_chain, f_d_chain + f_u_chain + [f_o_core], grad_pair, grad_values
    )
    f_p_core = Core(f_normed, grad_pair, sizes)
    f_v_core = Core(f_normed, grad_values, sizes)
    grad_normed = against(grad_pair, f_pair) + against(grad_values, f_value)
    grad_part, f_grad_pre = norm_back(grad_normed, frame_x, frame_gains[0])
    grad_frame_x = grad_hidden + grad_part
    (grad_frame_x,) = scatter_round(
        f_d_chain + f_u_chain + [f_o_core],
        f_d_chain + f_u_chain + [f_p_core, f_v_core],
        grad_frame_x,
    )
    f_grad_b_down = jnp.sum(grad_low.astype(jnp.float32), axis=0)
    (f_grad_b_down,) = ended(f_u_chain + [f_p_core, f_v_core], f_grad_b_down)
    f_ab = attention_sums(f_p_core, f_v_core, f_o_core)
    terms = jnp.concatenate(
        [
            term.reshape(devices, -1)
            for term in (
                f_grad_pre,
                f_grad_mid,
                f_grad_b_up,
                f_grad_b_down,
                c_grad_pre,
                c_grad_mid,
                c_grad_b_up,
                c_grad_b_down,
            )
        ],
        axis=1,
    )
    row = VectorScatter(terms, sizes)
    grad_frame_x, c_act = scatter_round(f_d_chain, f_ab + f_u_chain + [row], grad_frame_x, c_act)
    code_y = c_hidden + (times(c_act, c_down) + code_gains[3])
    frame_output = frame_y.astype(low)
    (code_y,) = scatter_round(f_ab + [row], f_ab + [row], code_y)
    code_output = jnp.swapaxes(tokens_of(code_y.astype(low)), 0, 1)
    (code_output,) = scatter_round(f_ab + f_u_chain + [row], f_ab + [row], code_output)
    code_embed_grad = jnp.swapaxes(tokens_of(grad_code_x), 0, 1)
    (code_embed_grad,) = scatter_round(f_ab + [row], [row], code_embed_grad)
    everything = c_d_chain + c_u_chain + c_ab + f_d_chain + f_u_chain + f_ab + [row]
    while True:
        started([chain for chain in everything if chain.away and chain.received is None])
        going = [chain for chain in everything if chain.received is not None]
        if not going:
            break
        ended(going)
    sums = row.state[0]
    pieces = []
    start = 0
    for width in widths:
        pieces.append(sums[start : start + width])
        start += width

    def arranged(attn_sums, up_sums, down_sums, vecs):
        total = attn_sums[0].result()
        prenorm, midnorm, upbias, downbias = vecs
        return (
            prenorm,
            total[:, :D],
            total[:, D : 2 * D],
            total[:, 2 * D : 3 * D],
            total[:, 3 * D :],
            midnorm,
            up_sums[0].result(),
            upbias,
            down_sums[0].result(),
            downbias,
        )

    code_outs = arranged(c_ab, c_u_chain, c_d_chain, pieces[4:])
    frame_outs = arranged(f_ab, f_u_chain, f_d_chain, pieces[:4])
    return (frame_output, code_output, grad_frame_x, code_embed_grad) + frame_outs + code_outs


def solution(mesh):
    in_specs = (
        P(("gx", "gy"), None),
        P(("gx", "gy"), None, None),
        P(("gx", "gy"), None),
        P(("gx", "gy"), None),
        P(("gx", "gy"), None, None),
        P(("gx", "gy")),
        P(("gx", "gy"), None),
        P(("gx", "gy"), None),
        P(("gx", "gy"), None),
        P(("gx", "gy"), None),
        P(("gx", "gy")),
        P(("gx", "gy"), None),
        P(("gx", "gy")),
        P(("gx", "gy"), None),
        P(("gx", "gy")),
        P(("gx", "gy")),
        P(("gx", "gy"), None),
        P(("gx", "gy"), None),
        P(("gx", "gy"), None),
        P(("gx", "gy"), None),
        P(("gx", "gy")),
        P(("gx", "gy"), None),
        P(("gx", "gy")),
        P(("gx", "gy"), None),
        P(("gx", "gy")),
    )
    out_specs = (
        P(("gx", "gy"), None),
        P(("gx", "gy"), None, None),
        P(("gx", "gy"), None),
        P(("gx", "gy"), None, None),
        P(("gx", "gy")),
        P(("gx", "gy"), None),
        P(("gx", "gy"), None),
        P(("gx", "gy"), None),
        P(("gx", "gy"), None),
        P(("gx", "gy")),
        P(("gx", "gy"), None),
        P(("gx", "gy")),
        P(("gx", "gy"), None),
        P(("gx", "gy")),
        P(("gx", "gy")),
        P(("gx", "gy"), None),
        P(("gx", "gy"), None),
        P(("gx", "gy"), None),
        P(("gx", "gy"), None),
        P(("gx", "gy")),
        P(("gx", "gy"), None),
        P(("gx", "gy")),
        P(("gx", "gy"), None),
        P(("gx", "gy")),
    )
    sizes = (mesh.shape["gx"], mesh.shape["gy"])
    return jax.shard_map(
        functools.partial(local, sizes), mesh=mesh, in_specs=in_specs, out_specs=out_specs, check_vma=False)
```

time: 3620 us -> 876 us (0.24)
  waiting for transfers between devices: 2780 us -> 215 us
  Pallas kernels: 0 us -> 329 us
  local copies, waits for them, and re-layouts: 297 us -> 17.8 us
  blocking collectives: 212 us -> 0 us
  matrix products: 280 us -> 101 us
  starting transfers between devices: 1.34 us -> 152 us
    reduce_scatter x12 -> x0, waiting for transfers between devices: 2310 us -> none  [the longest x1 360 us: local(): lax.psum_scatter(code_flat[6], ('gx', 'gy'), scatter_dimension=0, tiled=T...]
    all_gather x12 -> x0, waiting for transfers between devices: 459 us -> none  [the longest x1 76 us: local(): lax.all_gather(frame_upproj, ('gx', 'gy'), axis=0, tiled=True)]
    pallas_call x0 -> x70, Pallas kernels: none -> 329 us  [the longest x14 72.1 us: split_product(): pl.pallas_call(functools.partial(split_kernel, flip), grid_spec=pltpu.Pre...]
    ppermute x0 -> x141, waiting for transfers between devices: none -> 215 us  [swap(): lax.ppermute(value, ('gx', 'gy'), [(place, place ^ mask) for place in ran...]
    reshape x32 -> x4, local copies, waits for them, and re-layouts: 175 us -> 0.07 us  [the longest x3 0.06 us: prepare(): view = self.state.reshape(high, 2, -1, self.state.shape[-1])]
    ppermute x0 -> x141, starting transfers between devices: none -> 152 us  [swap(): lax.ppermute(value, ('gx', 'gy'), [(place, place ^ mask) for place in ran...]
    dot_general x36 -> x10, matrix products: 210 us -> 70 us  [times(): return jnp.dot(left, right, preferred_element_type=jnp.float32)]
    all_gather x2 -> x0, blocking collectives: 129 us -> none  [the longest x1 66.1 us: local(): lax.all_gather(frame_upbias, ('gx', 'gy'), axis=0, tiled=True)]
  transfers between devices with their start and end apart: 24 -> 141, of which waited for: 20 -> 42; matrix products, arithmetic and copies ran while one was open for 11% -> 17% of each run, Pallas kernels for 0% -> 28%
where the time goes in v2:
time: 876 us; the launch traced here: 864 us
  Pallas kernels  329 us (38%)
  waiting for transfers between devices  215 us (25%)
  starting transfers between devices  152 us (17%)
  matrix products  101 us (12%)
  other arithmetic  46.6 us (5%)
  local copies, waits for them, and re-layouts  17.8 us (2%)
    ppermute x141, waiting for transfers between devices, swap(): lax.ppermute(value, ('gx', 'gy'), [(place, place ^ mask) for place in ran...  215 us
    ppermute x141, starting transfers between devices, swap(): lax.ppermute(value, ('gx', 'gy'), [(place, place ^ mask) for place in ran...  152 us
    pallas_call x14, Pallas kernels, split_product(): pl.pallas_call(functools.partial(split_kernel, flip), grid_spec=pltpu.Pre...  72.1 us
    dot_general x10, matrix products, times(): return jnp.dot(left, right, preferred_element_type=jnp.float32)  70 us
    pallas_call x10, Pallas kernels, placed_near(): pl.pallas_call(place_near_tail_kernel if tail else place_near_kernel, gri...  60.1 us
    pallas_call x10, Pallas kernels, half_product(): pl.pallas_call(half_kernel if received is None else half_add_kernel, grid...  45.5 us
    pallas_call x14, Pallas kernels, add_split(): pl.pallas_call(add_split_kernel, grid_spec=pltpu.PrefetchScalarGridSpec(n...  34.9 us
    dot_general x6, matrix products, against(): lax.dot_general(left, right, (((1,), (1,)), ((), ())), preferred_element_...  31.4 us
  transfers between devices with their start and end apart: 141, of which 42 were waited for; matrix products, arithmetic and copies ran while one was open for 17% of the time, Pallas kernels for 28%

profile of v2, /device:TPU:0, one launch (start us, length us, event | category | flops | bytes accessed | tf_op | source)
XLA Modules:
  0.0 864.0 jit_solution(18005411722776626621)
XLA Ops:
  14.5 17.1 %collective-permute-done.1.refs_2_ = bf16[1,32,2048]{2,1,0:T(8,128)(2,1)S(1)} collective-permute-done((bf16[1,32,2048]{2,1,0:T(8,128)(2,1)S(1)}, bf16[1,32,2048]{2,1,0:T(8,128)(2,1)S(1)}, u32[]{:S(2)}, u32[]{:S(2)}) %collective-permute-start.1) | collective-permute-done | bytes 131104 | tf_op jit(solution)/shard_map/ppermute | solution.py:303
  63.2 9.8 %collective-permute-done.13.refs_2_ = bf16[1,32,4096]{2,1,0:T(8,128)(2,1)S(1)} collective-permute-done((bf16[1,32,4096]{2,1,0:T(8,128)(2,1)S(1)}, bf16[1,32,4096]{2,1,0:T(8,128)(2,1)S(1)}, u32[]{:S(2)}, u32[]{:S(2)}) %collective-permute-start.13) | collective-permute-done | bytes 262176 | tf_op jit(solution)/shard_map/ppermute | solution.py:303
  73.0 13.1 %collective-permute-start.16 = (bf16[1,128,1024]{2,1,0:T(8,128)(2,1)S(1)}, bf16[1,128,1024]{2,1,0:T(8,128)(2,1)S(1)}, u32[]{:S(2)}, u32[]{:S(2)}) collective-permute-start(bf16[1,128,1024]{2,1,0:T(8,128)(2,1)S(1)} %bitcast.271), channel_id=1, source_target_pairs={{0,8},{1,9},{2,10},{3,11},{4,12},{5,13},{6,14},{7,15},{8,0},{9,1},... | collective-permute-start | bytes 786440 | tf_op jit(solution)/shard_map/ppermute | solution.py:303
  121.0 15.8 %collective-permute-done.28.refs_1_ = bf16[4,128,1024]{2,1,0:T(8,128)(2,1)} collective-permute-done((bf16[4,128,1024]{2,1,0:T(8,128)(2,1)}, bf16[4,128,1024]{2,1,0:T(8,128)(2,1)}, u32[]{:S(2)}, u32[]{:S(2)}) %collective-permute-start.28) | collective-permute-done | bytes 1048608 | tf_op jit(solution)/shard_map/ppermute | solution.py:303
  169.1 7.7 frame_attend.1.acts_ref
  206.6 7.6 place_near.14
  214.3 7.8 place_near.13
  232.3 9.1 %add_convert_fusion.1 = (bf16[256,4096]{1,0:T(8,128)(2,1)}, bf16[256,4096]{1,0:T(8,128)(2,1)S(1)}) fusion(f32[4096]{0:T(1024)S(1)} %get-tuple-element.777, bf16[256,1024]{1,0:T(8,128)(2,1)} %multiply_convert_fusion.2.acts_ref, bf16[1024,4096]{1,0:T(8,128)(2,1)} %bitcast.184), kind=kOutput, calls=%fused_computation.8 | convolution fusion | flops 2164260864 | bytes 13123584 | tf_op jit(solution)/shard_map/dot_general | solution.py:888
  264.9 9.9 %collective-permute-done.67.refs_1_ = bf16[4,128,1024]{2,1,0:T(8,128)(2,1)} collective-permute-done((bf16[4,128,1024]{2,1,0:T(8,128)(2,1)}, bf16[4,128,1024]{2,1,0:T(8,128)(2,1)}, u32[]{:S(2)}, u32[]{:S(2)}) %collective-permute-start.67) | collective-permute-done | bytes 1048608 | tf_op jit(solution)/shard_map/ppermute | solution.py:303
  305.1 14.2 %collective-permute-done.70.refs_3_ = bf16[4,32,4096]{2,1,0:T(8,128)(2,1)} collective-permute-done((bf16[4,32,4096]{2,1,0:T(8,128)(2,1)}, bf16[4,32,4096]{2,1,0:T(8,128)(2,1)}, u32[]{:S(2)}, u32[]{:S(2)}) %collective-permute-start.70) | collective-permute-done | bytes 1048608 | tf_op jit(solution)/shard_map/ppermute | solution.py:303
  345.1 18.2 %add_convert_fusion = (bf16[768,4096]{1,0:T(8,128)(2,1)}, bf16[768,4096]{1,0:T(8,128)(2,1)}) fusion(f32[4096]{0:T(1024)S(1)} %get-tuple-element.776, bf16[768,1024]{1,0:T(8,128)(2,1)S(1)} %multiply_convert_fusion.acts_ref, bf16[1024,4096]{1,0:T(8,128)(2,1)} %bitcast.188), kind=kOutput, calls=%fused_computation | convolution fusion | flops 6492782592 | bytes 22560768 | tf_op jit(solution)/shard_map/dot_general | solution.py:888
  401.7 13.1 %grad_pre.2 = (bf16[768,4096]{1,0:T(8,128)(2,1)}, f32[1,4096]{1,0:T(1,128)}) custom-call(bf16[768,1024]{1,0:T(8,128)(2,1)} %bitcast.175, bf16[4096,1024]{1,0:T(8,128)(2,1)} %bitcast.182, bf16[768,4096]{1,0:T(8,128)(2,1)} %get-tuple-element.489.slope_ref), custom_call_target="tpu_custom_call" | custom-call | flops 1 | bytes 1 | tf_op jit(solution)/shard_map/grad_pre/pallas_call | solution.py:938
  414.8 7.7 half_away.11
  432.3 12.1 %grad_two.2 = f32[768,1024]{1,0:T(8,128)} custom-call(bf16[768,4096]{1,0:T(8,128)(2,1)} %get-tuple-element.503.grad_ref, bf16[1024,4096]{1,0:T(8,128)(2,1)} %bitcast.189), custom_call_target="tpu_custom_call" | custom-call | flops 1 | bytes 1 | tf_op jit(solution)/shard_map/grad_two/pallas_call | solution.py:920
  487.3 11.6 %code_attend_back.1 = (bf16[3,256,2048]{2,1,0:T(8,128)(2,1)}, bf16[3,256,1024]{2,1,0:T(8,128)(2,1)}) custom-call(bf16[3,256,2048]{2,1,0:T(8,128)(2,1)} %bitcast.194, bf16[3,256,1024]{2,1,0:T(8,128)(2,1)} %bitcast.204, bf16[3,256,1024]{2,1,0:T(8,128)(2,1)} %bitcast.267, bf16[1024,128]{1,0:T(8,128)(2,1)} %fusion.15.marks_ref), custom_call_target="tpu_custom_call" | custom-call | flops 1 | bytes 1 | tf_op jit(solution)/shard_map/code_attend_back/pallas_call | solution.py:156
  542.4 8.9 %multiply_reduce_fusion.1 = (f32[1024]{0:T(1024)S(1)}, f32[768]{0:T(1024)S(1)}, f32[768,1024]{1,0:T(8,128)S(1)}) fusion(f32[768,1024]{1,0:T(8,128)} %bitcast.180, f32[768]{0:T(1024)S(1)} %fusion.22, f32[1024]{0:T(1024)S(1)} %mul.221, f32[768,1024]{1,0:T(8,128)} %fusion.34, bf16[768,2048]{1,0:T(8,128)(2,1)} %bitcast.196, bf16[1024,2048]{1,0:T(8,128)(2,1)} %bitcast.244), kind=kOutput, calls=%fused_computation.18 | convolution fusion | flops 3226728704 | bytes 16791552 | tf_op jit(solution)/shard_map/dot_general | solution.py:37
  581.5 7.9 grad_pre.3
  646.0 8.1 collective-permute-done.108
  670.3 12.6 %frame_attend_back.1 = (bf16[256,2048]{1,0:T(8,128)(2,1)}, bf16[256,1024]{1,0:T(8,128)(2,1)}) custom-call(bf16[256,2048]{1,0:T(8,128)(2,1)} %convolution_convert_fusion.1.query_ref.keys_ref, bf16[256,2048]{1,0:T(8,128)(2,1)} %convolution_convert_fusion.1.query_ref.keys_ref, bf16[256,1024]{1,0:T(8,128)(2,1)} %convolution_convert_fusion.5.values_ref, ...), custom_call_target="tpu_custom_call" | custom-call | flops 1 | bytes 1 | tf_op jit(solution)/shard_map/frame_attend_back/pallas_call | solution.py:267
  707.6 11.9 %collective-permute-done.112.refs_2_ = bf16[4,128,512]{2,1,0:T(8,128)(2,1)} collective-permute-done((bf16[4,128,512]{2,1,0:T(8,128)(2,1)}, bf16[4,128,512]{2,1,0:T(8,128)(2,1)}, u32[]{:S(2)}, u32[]{:S(2)}) %collective-permute-start.112) | collective-permute-done | bytes 524320 | tf_op jit(solution)/shard_map/ppermute | solution.py:303
  749.2 8.6 collective-permute-done.122
  787.8 12.1 %add_add_fusion.2 = bf16[768,1024]{1,0:T(8,128)(2,1)} fusion(f32[768,1024]{1,0:T(8,128)S(1)} %copy-done.3, bf16[768,4096]{1,0:T(8,128)(2,1)} %get-tuple-element.677.acts_ref, bf16[4096,1024]{1,0:T(8,128)(2,1)} %bitcast.183, f32[1024]{0:T(1024)} %add.569), kind=kOutput, calls=%fused_computation.16 | convolution fusion | flops 6444810240 | bytes 19402752 | tf_op jit(solution)/shard_map/dot_general | solution.py:888
  801.0 7.7 collective-permute-done.126
  844.1 8.8 %collective-permute-done.136 = bf16[32,4096]{1,0:T(8,128)(2,1)S(1)} collective-permute-done((bf16[32,4096]{1,0:T(8,128)(2,1)}, bf16[32,4096]{1,0:T(8,128)(2,1)S(1)}, u32[]{:S(2)}, u32[]{:S(2)}) %collective-permute-start.136) | collective-permute-done | bytes 262176 | tf_op jit(solution)/shard_map/ppermute | solution.py:303
  (595 shorter events, 600.4 us)
Async XLA Ops:
  39.8 46.8 %collective-permute-start.8 = (bf16[8,32,1152]{2,1,0:T(8,128)(2,1)}, bf16[8,32,1152]{2,1,0:T(8,128)(2,1)S(1)}, u32[]{:S(2)}, u32[]{:S(2)}) collective-permute-start(bf16[8,32,1152]{2,1,0:T(8,128)(2,1)} %bitcast.205), channel_id=1, source_target_pairs={{0,1},{1,0},{2,3},{3,2},{4,5},{5,4},{6,7},{7,6},{8,9},{9,8},{10,11... | collective-permute-start | bytes 1769480 | tf_op jit(solution)/shard_map/ppermute | solution.py:303
  43.3 42.9 %collective-permute-start.7 = (bf16[4,32,2048]{2,1,0:T(8,128)(2,1)}, bf16[4,32,2048]{2,1,0:T(8,128)(2,1)}, u32[]{:S(2)}, u32[]{:S(2)}) collective-permute-start(bf16[4,32,2048]{2,1,0:T(8,128)(2,1)} %bitcast.260), channel_id=1, source_target_pairs={{0,2},{1,3},{2,0},{3,1},{4,6},{5,7},{6,4},{7,5},{8,10},{9,11},{10,... | collective-permute-start | bytes 1572872 | tf_op jit(solution)/shard_map/ppermute | solution.py:303
  61.6 34.6 %collective-permute-start.6 = (bf16[4,32,2048]{2,1,0:T(8,128)(2,1)}, bf16[4,32,2048]{2,1,0:T(8,128)(2,1)}, u32[]{:S(2)}, u32[]{:S(2)}) collective-permute-start(bf16[4,32,2048]{2,1,0:T(8,128)(2,1)} %bitcast.261), channel_id=1, source_target_pairs={{0,1},{1,0},{2,3},{3,2},{4,5},{5,4},{6,7},{7,6},{8,9},{9,8},{10,11... | collective-permute-start | bytes 1572872 | tf_op jit(solution)/shard_map/ppermute | solution.py:303
  117.6 34.5 %collective-permute-start.53 = (bf16[1,32,4096]{2,1,0:T(8,128)(2,1)}, bf16[1,32,4096]{2,1,0:T(8,128)(2,1)S(1)}, u32[]{:S(2)}, u32[]{:S(2)}) collective-permute-start(bf16[1,32,4096]{2,1,0:T(8,128)(2,1)} %bitcast.282), channel_id=1, source_target_pairs={{0,8},{1,9},{2,10},{3,11},{4,12},{5,13},{6,14},{7,15},{8,0},{9,1},... | collective-permute-start | bytes 786440 | tf_op jit(solution)/shard_map/ppermute | solution.py:303
  120.9 42.5 %collective-permute-start.36 = (bf16[4,128,1024]{2,1,0:T(8,128)(2,1)}, bf16[4,128,1024]{2,1,0:T(8,128)(2,1)}, u32[]{:S(2)}, u32[]{:S(2)}) collective-permute-start(bf16[4,128,1024]{2,1,0:T(8,128)(2,1)} %bitcast.239), channel_id=1, source_target_pairs={{0,2},{1,3},{2,0},{3,1},{4,6},{5,7},{6,4},{7,5},{8,10},{9,11},{10,... | collective-permute-start | bytes 3145736 | tf_op jit(solution)/shard_map/ppermute | solution.py:303
  137.8 39.0 %collective-permute-start.43 = (bf16[4,128,1024]{2,1,0:T(8,128)(2,1)}, bf16[4,128,1024]{2,1,0:T(8,128)(2,1)}, u32[]{:S(2)}, u32[]{:S(2)}) collective-permute-start(bf16[4,128,1024]{2,1,0:T(8,128)(2,1)} %bitcast.240), channel_id=1, source_target_pairs={{0,16},{1,17},{2,18},{3,19},{4,20},{5,21},{6,22},{7,23},{8,24},{9,... | collective-permute-start | bytes 3145736 | tf_op jit(solution)/shard_map/ppermute | solution.py:303
  143.6 42.1 %collective-permute-start.35 = (bf16[4,32,4096]{2,1,0:T(8,128)(2,1)}, bf16[4,32,4096]{2,1,0:T(8,128)(2,1)}, u32[]{:S(2)}, u32[]{:S(2)}) collective-permute-start(bf16[4,32,4096]{2,1,0:T(8,128)(2,1)} %collective-permute-done.27.refs_2_), channel_id=1, source_target_pairs={{0,1},{1,0},{2,3},{3,2},{4,5},{5,4},{6,7},{7,6},{8,9},{9,8},{10,11... | collective-permute-start | bytes 3145736 | tf_op jit(solution)/shard_map/ppermute | solution.py:303
  152.1 36.5 %collective-permute-start.37 = (bf16[4,128,1024]{2,1,0:T(8,128)(2,1)}, bf16[4,128,1024]{2,1,0:T(8,128)(2,1)}, u32[]{:S(2)}, u32[]{:S(2)}) collective-permute-start(bf16[4,128,1024]{2,1,0:T(8,128)(2,1)} %collective-permute-done.28.refs_1_), channel_id=1, source_target_pairs={{0,2},{1,3},{2,0},{3,1},{4,6},{5,7},{6,4},{7,5},{8,10},{9,11},{10,... | collective-permute-start | bytes 3145736 | tf_op jit(solution)/shard_map/ppermute | solution.py:303
  163.7 32.6 %collective-permute-start.41 = (bf16[4,32,4096]{2,1,0:T(8,128)(2,1)}, bf16[4,32,4096]{2,1,0:T(8,128)(2,1)}, u32[]{:S(2)}, u32[]{:S(2)}) collective-permute-start(bf16[4,32,4096]{2,1,0:T(8,128)(2,1)} %collective-permute-done.27.refs_2_), channel_id=1, source_target_pairs={{0,16},{1,17},{2,18},{3,19},{4,20},{5,21},{6,22},{7,23},{8,24},{9,... | collective-permute-start | bytes 3145736 | tf_op jit(solution)/shard_map/ppermute | solution.py:303
  196.8 34.5 %collective-permute-start.50 = (bf16[8,32,1024]{2,1,0:T(8,128)(2,1)}, bf16[8,32,1024]{2,1,0:T(8,128)(2,1)}, u32[]{:S(2)}, u32[]{:S(2)}) collective-permute-start(bf16[8,32,1024]{2,1,0:T(8,128)(2,1)} %bitcast.28.refs_0_), channel_id=1, source_target_pairs={{0,2},{1,3},{2,0},{3,1},{4,6},{5,7},{6,4},{7,5},{8,10},{9,11},{10,... | collective-permute-start | bytes 1572872 | tf_op jit(solution)/shard_map/ppermute | solution.py:303
  263.2 41.4 %collective-permute-start.71 = (bf16[4,128,1024]{2,1,0:T(8,128)(2,1)}, bf16[4,128,1024]{2,1,0:T(8,128)(2,1)}, u32[]{:S(2)}, u32[]{:S(2)}) collective-permute-start(bf16[4,128,1024]{2,1,0:T(8,128)(2,1)} %bitcast.39.refs_0_), channel_id=1, source_target_pairs={{0,2},{1,3},{2,0},{3,1},{4,6},{5,7},{6,4},{7,5},{8,10},{9,11},{10,... | collective-permute-start | bytes 3145736 | tf_op jit(solution)/shard_map/ppermute | solution.py:303
  264.3 40.3 %collective-permute-start.69 = (bf16[4,32,4096]{2,1,0:T(8,128)(2,1)}, bf16[4,32,4096]{2,1,0:T(8,128)(2,1)}, u32[]{:S(2)}, u32[]{:S(2)}) collective-permute-start(bf16[4,32,4096]{2,1,0:T(8,128)(2,1)} %bitcast.38.refs_0_), channel_id=1, source_target_pairs={{0,1},{1,0},{2,3},{3,2},{4,5},{5,4},{6,7},{7,6},{8,9},{9,8},{10,11... | collective-permute-start | bytes 3145736 | tf_op jit(solution)/shard_map/ppermute | solution.py:303
  264.6 72.3 %collective-permute-start.68 = (bf16[4,32,4096]{2,1,0:T(8,128)(2,1)}, bf16[4,32,4096]{2,1,0:T(8,128)(2,1)}, u32[]{:S(2)}, u32[]{:S(2)}) collective-permute-start(bf16[4,32,4096]{2,1,0:T(8,128)(2,1)} %bitcast.38.refs_0_), channel_id=1, source_target_pairs={{0,16},{1,17},{2,18},{3,19},{4,20},{5,21},{6,22},{7,23},{8,24},{9,... | collective-permute-start | bytes 3145736 | tf_op jit(solution)/shard_map/ppermute | solution.py:303
  287.7 31.6 %collective-permute-start.70 = (bf16[4,32,4096]{2,1,0:T(8,128)(2,1)}, bf16[4,32,4096]{2,1,0:T(8,128)(2,1)}, u32[]{:S(2)}, u32[]{:S(2)}) collective-permute-start(bf16[4,32,4096]{2,1,0:T(8,128)(2,1)} %collective-permute-done.66.refs_2_), channel_id=1, source_target_pairs={{0,1},{1,0},{2,3},{3,2},{4,5},{5,4},{6,7},{7,6},{8,9},{9,8},{10,11... | collective-permute-start | bytes 3145736 | tf_op jit(solution)/shard_map/ppermute | solution.py:303
  288.0 35.0 %collective-permute-start.72 = (bf16[4,128,1024]{2,1,0:T(8,128)(2,1)}, bf16[4,128,1024]{2,1,0:T(8,128)(2,1)}, u32[]{:S(2)}, u32[]{:S(2)}) collective-permute-start(bf16[4,128,1024]{2,1,0:T(8,128)(2,1)} %collective-permute-done.67.refs_1_), channel_id=1, source_target_pairs={{0,2},{1,3},{2,0},{3,1},{4,6},{5,7},{6,4},{7,5},{8,10},{9,11},{10,... | collective-permute-start | bytes 3145736 | tf_op jit(solution)/shard_map/ppermute | solution.py:303
  304.6 58.7 %collective-permute-start.76 = (bf16[4,128,1024]{2,1,0:T(8,128)(2,1)}, bf16[4,128,1024]{2,1,0:T(8,128)(2,1)}, u32[]{:S(2)}, u32[]{:S(2)}) collective-permute-start(bf16[4,128,1024]{2,1,0:T(8,128)(2,1)} %bitcast.39.refs_0_), channel_id=1, source_target_pairs={{0,16},{1,17},{2,18},{3,19},{4,20},{5,21},{6,22},{7,23},{8,24},{9,... | collective-permute-start | bytes 3145736 | tf_op jit(solution)/shard_map/ppermute | solution.py:303
  304.6 32.3 %collective-permute-start.74 = (bf16[4,32,4096]{2,1,0:T(8,128)(2,1)}, bf16[4,32,4096]{2,1,0:T(8,128)(2,1)}, u32[]{:S(2)}, u32[]{:S(2)}) collective-permute-start(bf16[4,32,4096]{2,1,0:T(8,128)(2,1)} %collective-permute-done.66.refs_2_), channel_id=1, source_target_pairs={{0,16},{1,17},{2,18},{3,19},{4,20},{5,21},{6,22},{7,23},{8,24},{9,... | collective-permute-start | bytes 3145736 | tf_op jit(solution)/shard_map/ppermute | solution.py:303
  528.6 31.1 %collective-permute-start.97 = (bf16[512,2048]{1,0:T(8,128)(2,1)}, bf16[512,2048]{1,0:T(8,128)(2,1)}, u32[]{:S(2)}, u32[]{:S(2)}) collective-permute-start(bf16[512,2048]{1,0:T(8,128)(2,1)} %half_away.13), channel_id=1, source_target_pairs={{0,16},{1,17},{2,18},{3,19},{4,20},{5,21},{6,22},{7,23},{8,24},{9,... | collective-permute-start | bytes 6291464 | tf_op jit(solution)/shard_map/ppermute | solution.py:303
  528.6 31.1 %collective-permute-start.98 = (bf16[512,1024]{1,0:T(8,128)(2,1)}, bf16[512,1024]{1,0:T(8,128)(2,1)}, u32[]{:S(2)}, u32[]{:S(2)}) collective-permute-start(bf16[512,1024]{1,0:T(8,128)(2,1)} %half_away.14), channel_id=1, source_target_pairs={{0,16},{1,17},{2,18},{3,19},{4,20},{5,21},{6,22},{7,23},{8,24},{9,... | collective-permute-start | bytes 3145736 | tf_op jit(solution)/shard_map/ppermute | solution.py:303
  529.1 30.5 %collective-permute-start.94 = (bf16[32,4096]{1,0:T(8,128)(2,1)}, bf16[32,4096]{1,0:T(8,128)(2,1)S(1)}, u32[]{:S(2)}, u32[]{:S(2)}) collective-permute-start(bf16[32,4096]{1,0:T(8,128)(2,1)} %get-tuple-element.549), channel_id=1, source_target_pairs={{0,4},{1,5},{2,6},{3,7},{4,0},{5,1},{6,2},{7,3},{8,12},{9,13},{10,... | collective-permute-start | bytes 786440 | tf_op jit(solution)/shard_map/ppermute | solution.py:303
  688.1 31.4 %collective-permute-start.114 = (bf16[8,32,2048]{2,1,0:T(8,128)(2,1)}, bf16[8,32,2048]{2,1,0:T(8,128)(2,1)}, u32[]{:S(2)}, u32[]{:S(2)}) collective-permute-start(bf16[8,32,2048]{2,1,0:T(8,128)(2,1)} %get-tuple-element.628), channel_id=1, source_target_pairs={{0,2},{1,3},{2,0},{3,1},{4,6},{5,7},{6,4},{7,5},{8,10},{9,11},{10,... | collective-permute-start | bytes 3145736 | tf_op jit(solution)/shard_map/ppermute | solution.py:303
  728.3 42.2 %collective-permute-start.119 = (bf16[512,2048]{1,0:T(8,128)(2,1)}, bf16[512,2048]{1,0:T(8,128)(2,1)}, u32[]{:S(2)}, u32[]{:S(2)}) collective-permute-start(bf16[512,2048]{1,0:T(8,128)(2,1)} %half_away.18), channel_id=1, source_target_pairs={{0,16},{1,17},{2,18},{3,19},{4,20},{5,21},{6,22},{7,23},{8,24},{9,... | collective-permute-start | bytes 6291464 | tf_op jit(solution)/shard_map/ppermute | solution.py:303
  736.3 34.3 %collective-permute-start.120 = (bf16[512,1024]{1,0:T(8,128)(2,1)}, bf16[512,1024]{1,0:T(8,128)(2,1)}, u32[]{:S(2)}, u32[]{:S(2)}) collective-permute-start(bf16[512,1024]{1,0:T(8,128)(2,1)} %half_away.19), channel_id=1, source_target_pairs={{0,16},{1,17},{2,18},{3,19},{4,20},{5,21},{6,22},{7,23},{8,24},{9,... | collective-permute-start | bytes 3145736 | tf_op jit(solution)/shard_map/ppermute | solution.py:303
  787.8 31.5 %collective-permute-start.131 = (bf16[32,4096]{1,0:T(8,128)(2,1)}, bf16[32,4096]{1,0:T(8,128)(2,1)}, u32[]{:S(2)}, u32[]{:S(2)}) collective-permute-start(bf16[32,4096]{1,0:T(8,128)(2,1)} %get-tuple-element.694), channel_id=1, source_target_pairs={{0,4},{1,5},{2,6},{3,7},{4,0},{5,1},{6,2},{7,3},{8,12},{9,13},{10,... | collective-permute-start | bytes 786440 | tf_op jit(solution)/shard_map/ppermute | solution.py:303
  (199 other events, 3714.5 us)

commit v3 on v2

--- a/solution.py
+++ b/solution.py
@@ -332,6 +332,55 @@
     return index
 
 
+def spans(done, pos):
+    high = 2 ** sum(1 for other in done if other < pos)
+    low = 2 ** sum(1 for other in done if other > pos)
+    return high, low
+
+
+def merge_kernel(bit_ref, mine_ref, theirs_ref, *outs):
+    def put(first, second):
+        start = 0
+        for out in outs:
+            width = out.shape[-1]
+            out[0, 0] = first[0, :, start : start + width]
+            out[0, 1] = second[0, :, start : start + width]
+            start += width
+
+    @pl.when(bit_ref[0] == 0)
+    def _():
+        put(mine_ref, theirs_ref)
+
+    @pl.when(bit_ref[0] != 0)
+    def _():
+        put(theirs_ref, mine_ref)
+
+
+def merged(mine, theirs, bit, splits):
+    planes, rows, cols = mine.shape
+    part = rows
+    while part % 2 == 0 and part * cols > 512 * 1024:
+        part //= 2
+    read = pl.BlockSpec((1, part, cols), lambda i, j, bit_ref: (i, j, 0))
+    return pl.pallas_call(
+        merge_kernel,
+        grid_spec=pltpu.PrefetchScalarGridSpec(
+            num_scalar_prefetch=1,
+            grid=(planes, rows // part),
+            in_specs=[read, read],
+            out_specs=[
+                pl.BlockSpec((1, 2, part, width), lambda i, j, bit_ref: (i, 0, j, 0))
+                for width in splits
+            ],
+        ),
+        out_shape=[
+            jax.ShapeDtypeStruct((planes, 2, rows, width), mine.dtype) for width in splits
+        ],
+        cost_estimate=LIGHT,
+        name="merge",
+    )(bit.reshape(1), mine, theirs)
+
+
 def place_far_kernel(place_ref, *refs):
     for index, ref in enumerate(refs[:-1]):
         refs[-1][0, place_ref[0] ^ index] = ref[0]
@@ -354,120 +403,76 @@
     )(place.reshape(1), *pieces)
 
 
-def place_near_kernel(place_ref, *refs):
-    for index, ref in enumerate(refs[:-1]):
-        refs[-1][0, place_ref[1] ^ (index // 4), 0, place_ref[0] ^ (index % 4)] = ref[0]
-
-
-def place_near_tail_kernel(place_ref, *refs):
-    cols = refs[-2].shape[-1]
-    for index, ref in enumerate(refs[:-2]):
-        slot = (0, place_ref[1] ^ (index // 4), 0, place_ref[0] ^ (index % 4))
-        refs[-2][slot] = ref[0, :, :cols]
-        refs[-1][slot] = ref[0, :, cols:]
-
-
-def placed_near(pieces, near_place, core_place, group, high, low, tail):
-    rows, cols = pieces[0].shape[1:]
-    widths = [cols - tail, tail] if tail else [cols]
-    offset = group * high * low
-    outs = pl.pallas_call(
-        place_near_tail_kernel if tail else place_near_kernel,
-        grid_spec=pltpu.PrefetchScalarGridSpec(
-            num_scalar_prefetch=1,
-            grid=(high * low,),
-            in_specs=[pl.BlockSpec((1, rows, cols), lambda i, place_ref: (i + offset, 0, 0))] * 8,
-            out_specs=[
-                pl.BlockSpec(
-                    (1, 2, 1, 4, rows, width),
-                    lambda i, place_ref: (i // low, 0, i % low, 0, 0, 0),
-                )
-                for width in widths
-            ],
-        ),
-        out_shape=[
-            jax.ShapeDtypeStruct((high, 2, low, 4, rows, width), pieces[0].dtype)
-            for width in widths
-        ],
-        cost_estimate=LIGHT,
-        name="place_near",
-    )(jnp.stack([near_place, core_place]), *pieces)
-    return [out.reshape(high * 2 * low * 4 * rows, out.shape[-1]) for out in outs]
-
-
 def pinned(*values):
     return lax.optimization_barrier(values)
 
 
+def gather_order(sizes, flip):
+    masks, core = bit_masks(sizes)
+    count = len(masks)
+    far = [place for place in range(count - 2) if place != core]
+    near = [count - 1, count - 2] if flip else [count - 2, count - 1]
+    return far + near + [core]
+
+
 class Gather:
-    def __init__(self, shard, sizes, flip, tail=0):
+    def __init__(self, shards, sizes, flips, splits):
         self.sizes = sizes
-        self.tail = tail
-        self.groups, self.rows, self.cols = shard.shape
-        self.state = shard
+        self.flips, self.splits = flips, splits
+        masks, core = bit_masks(sizes)
+        self.masks, self.core = masks, core
         self.far = far_groups(sizes)
-        masks, core = bit_masks(sizes)
-        self.near = masks[-2:]
-        self.first, self.second = (2, 1) if not flip else (1, 2)
-        self.core = masks[core]
-        self.high = 2**core
-        self.low = 2 ** (len(masks) - core - 3)
-        self.pieces = None
+        self.states = [shards]
         self.received = None
         self.stage = -len(self.far)
 
-    def flown(self, value, mask):
-        return swap(value, mask, self.sizes)
+    def near_masks(self, second):
+        return [self.masks[-1 if flip != second else -2] for flip in self.flips]
 
     def send(self):
         if self.stage < 0:
-            masks = combined(self.far[self.stage])
-            self.received = [self.flown(self.state, mask) for mask in masks[1:]]
-        elif self.stage == 0:
-            mask = combined(self.near)[self.first]
-            self.received = [self.flown(self.pieces[0], mask)]
-        elif self.stage == 1:
-            mask = combined(self.near)[self.second]
-            self.received = [self.flown(self.pieces[index], mask) for index in (0, self.first)]
+            masks = combined(self.far[self.stage])[1:]
+            self.received = [swap(self.states[0], mask, self.sizes) for mask in masks]
+        elif self.stage < 2:
+            masks = self.near_masks(self.stage == 1)
+            self.received = [
+                swap(state, mask, self.sizes) for state, mask in zip(self.states, masks)
+            ]
         else:
-            self.received = [self.flown(piece, self.core) for piece in self.pieces]
+            mask = self.masks[self.core]
+            self.received = [swap(state, mask, self.sizes) for state in self.states]
 
     def take(self):
+        received, self.received = list(self.received), None
         if self.stage < 0:
+            state = self.states[0]
+            groups, rows, cols = state.shape[0], state.shape[-2], state.shape[-1]
             group = self.far[self.stage]
-            wide = placed_far(
-                [
-                    value.reshape(-1, self.rows, self.cols)
-                    for value in [self.state] + list(self.received)
-                ],
-                small_index(group, self.sizes),
-            )
-            self.state = wide.reshape(-1, self.rows, self.cols)
+            pieces = [value.reshape(-1, rows, cols) for value in [state] + received]
+            wide = placed_far(pieces, small_index(group, self.sizes))
+            self.states = [wide.reshape(groups, -1, rows, cols)]
             if self.stage == -1:
-                self.pieces = [self.state, None, None, None]
-        elif self.stage == 0:
-            self.pieces[self.first] = self.received[0]
-        elif self.stage == 1:
-            self.pieces[self.second] = self.received[0]
-            self.pieces[3] = self.received[1]
+                self.states = [self.states[0][place] for place in range(groups)]
+        elif self.stage < 2:
+            states = []
+            masks = self.near_masks(self.stage == 1)
+            for state, value, mask, flip in zip(self.states, received, masks, self.flips):
+                blocks, rows, cols = state.shape
+                joined = 2 if flip and self.stage == 1 else 1
+                shape = (blocks // joined, joined * rows, cols)
+                bit = small_index([mask], self.sizes)
+                (out,) = merged(state.reshape(shape), value.reshape(shape), bit, [cols])
+                states.append(out.reshape(2 * blocks, rows, cols))
+            self.states = states
         else:
-            near_place = small_index(self.near, self.sizes)
-            core_place = small_index([self.core], self.sizes)
-            outs = [
-                placed_near(
-                    self.pieces + list(self.received),
-                    near_place,
-                    core_place,
-                    group,
-                    self.high,
-                    self.low,
-                    self.tail,
-                )
-                for group in range(self.groups)
-            ]
-            self.whole = [out[0] for out in outs]
-            self.tails = [out[-1] for out in outs]
-        self.received = None
+            self.whole = []
+            for state, value, splits in zip(self.states, received, self.splits):
+                blocks, rows, cols = state.shape
+                high = 2**self.core
+                shape = (high, blocks // high * rows, cols)
+                bit = small_index([self.masks[self.core]], self.sizes)
+                outs = merged(state.reshape(shape), value.reshape(shape), bit, splits)
+                self.whole.append([out.reshape(-1, out.shape[-1]) for out in outs])
         self.stage += 1
 
 
@@ -610,129 +615,150 @@
             self.prepare()
 
 
-def split_kernel(flip, side_ref, acts_ref, grad_ref, add_ref, kept_ref, away_ref):
-    total = over_rows(acts_ref[...], grad_ref[...]) + add_ref[...].astype(jnp.float32)
-    half, rows, cols = kept_ref.shape
-    total = total.astype(jnp.bfloat16)
-    parts = [[], []]
-    for index in range(2 * half):
-        bit = (index // 2) % 2 if flip else index % 2
-        parts[bit].append(total[index * rows : (index + 1) * rows])
-
-    @pl.when(side_ref[1] == 0)
-    def _():
-        for index in range(half):
-            kept_ref[index] = parts[0][index]
-            away_ref[index] = parts[1][index]
-
-    @pl.when(side_ref[1] != 0)
-    def _():
-        for index in range(half):
-            kept_ref[index] = parts[1][index]
-            away_ref[index] = parts[0][index]
-
-
-def split_product(acts, grad, theirs, sizes, flip, start, cols):
+def split_kernel(flips, side_ref, acts_ref, *refs):
+    count = len(flips)
+    acts = acts_ref[...]
+    for place, flip in enumerate(flips):
+        grad_ref, add_ref = refs[2 * place], refs[2 * place + 1]
+        kept_ref, away_ref = refs[2 * (count + place)], refs[2 * (count + place) + 1]
+        total = over_rows(acts, grad_ref[...]) + add_ref[...].astype(jnp.float32)
+        total = total.astype(jnp.bfloat16)
+        half, rows, cols = kept_ref.shape
+        parts = [[], []]
+        for index in range(2 * half):
+            bit = (index // 2) % 2 if flip else index % 2
+            parts[bit].append(total[index * rows : (index + 1) * rows])
+
+        def put(first, second, kept_ref=kept_ref, away_ref=away_ref, half=half):
+            for index in range(half):
+                kept_ref[index] = first[index]
+                away_ref[index] = second[index]
+
+        @pl.when(side_ref[1 + place] == 0)
+        def _(put=put, parts=parts):
+            put(parts[0], parts[1])
+
+        @pl.when(side_ref[1 + place] != 0)
+        def _(put=put, parts=parts):
+            put(parts[1], parts[0])
+
+
+def split_product(acts, grad, theirs, sizes, flips):
     masks, core = bit_masks(sizes)
     devices = sizes[0] * sizes[1]
     rows, inner = acts.shape
+    count = len(flips)
+    cols = grad.shape[1] // count
     block = inner // devices
     segment = inner // (2 * 2**core)
     tile = math.gcd(segment, 512)
     parts = segment // tile
-    wide = math.gcd(cols, 1024)
-    shift = start // wide
-    first = masks[-2] if flip else masks[-1]
-    sides = jnp.stack([small_index([masks[core]], sizes), small_index([first], sizes)])
+    wide = math.gcd(cols, 1024 // count)
+    steps = cols // wide
+    firsts = [masks[-2] if flip else masks[-1] for flip in flips]
+    sides = jnp.stack([small_index([mask], sizes) for mask in [masks[core]] + firsts])
     half = tile // (2 * block)
     out_spec = pl.BlockSpec((half, block, wide), lambda i, j, side_ref: (i, 0, j))
     out_shape = jax.ShapeDtypeStruct((devices // 4, block, cols), jnp.bfloat16)
+    specs = [
+        pl.BlockSpec(
+            (rows, tile),
+            lambda i, j, side_ref: (
+                0,
+                (i // parts) * 2 * parts + side_ref[0] * parts + i % parts,
+            ),
+        )
+    ]
+    for place in range(count):
+        shift = place * steps
+        specs.append(pl.BlockSpec((rows, wide), lambda i, j, side_ref, s=shift: (0, j + s)))
+        specs.append(pl.BlockSpec((tile, wide), lambda i, j, side_ref, s=shift: (i, j + s)))
     return pl.pallas_call(
-        functools.partial(split_kernel, flip),
+        functools.partial(split_kernel, flips),
         grid_spec=pltpu.PrefetchScalarGridSpec(
             num_scalar_prefetch=1,
-            grid=(inner // (2 * tile), cols // wide),
-            in_specs=[
-                pl.BlockSpec(
-                    (rows, tile),
-                    lambda i, j, side_ref: (
-                        0,
-                        (i // parts) * 2 * parts + side_ref[0] * parts + i % parts,
-                    ),
-                ),
-                pl.BlockSpec((rows, wide), lambda i, j, side_ref: (0, j + shift)),
-                pl.BlockSpec((tile, wide), lambda i, j, side_ref: (i, j + shift)),
-            ],
-            out_specs=[out_spec, out_spec],
+            grid=(inner // (2 * tile), steps),
+            in_specs=specs,
+            out_specs=[out_spec] * (2 * count),
         ),
-        out_shape=[out_shape, out_shape],
+        out_shape=[out_shape] * (2 * count),
         cost_estimate=LIGHT,
         name="split_product",
-    )(sides, acts, grad, theirs)
-
-
-def add_split_kernel(side_ref, kept_ref, kept_add_ref, away_ref, away_add_ref, *outs):
-    for out, one, two in ((outs[0], kept_ref, kept_add_ref), (outs[1], away_ref, away_add_ref)):
-        total = one[:, 0].astype(jnp.float32) + two[:, 0].astype(jnp.float32)
-        out[...] = total.astype(jnp.bfloat16)
-
-
-def add_split(kept, received, bit):
-    blocks, rows, cols = kept.shape
-    shape = (blocks // 2, 2, rows, cols)
-    kept, received = kept.reshape(shape), received.reshape(shape)
+    )(sides, acts, *([grad, theirs] * count))
+
+
+def add_split_kernel(side_ref, *refs):
+    count = len(refs) // 6
+    for place in range(count):
+        ins = refs[4 * place : 4 * place + 4]
+        outs = refs[4 * count + 2 * place : 4 * count + 2 * place + 2]
+        for out, one, two in zip(outs, ins[::2], ins[1::2]):
+            out[...] = one[:, 0] + two[:, 0]
+
+
+def add_split(kepts, values, bits):
+    blocks = kepts[0].shape[0]
     part = math.gcd(blocks // 2, 4)
-    stays = pl.BlockSpec((part, 1, rows, cols), lambda i, side_ref: (i, side_ref[0], 0, 0))
-    goes = pl.BlockSpec((part, 1, rows, cols), lambda i, side_ref: (i, 1 - side_ref[0], 0, 0))
-    out_spec = pl.BlockSpec((part, rows, cols), lambda i, side_ref: (i, 0, 0))
-    out_shape = jax.ShapeDtypeStruct((blocks // 2, rows, cols), kept.dtype)
-    return pl.pallas_call(
+    specs, operands, out_specs, out_shapes = [], [], [], []
+    for place, (kept, value) in enumerate(zip(kepts, values)):
+        unused, rows, cols = kept.shape
+        shape = (blocks // 2, 2, rows, cols)
+        block = (part, 1, rows, cols)
+        stays = pl.BlockSpec(block, lambda i, side_ref, p=place: (i, side_ref[p], 0, 0))
+        goes = pl.BlockSpec(block, lambda i, side_ref, p=place: (i, 1 - side_ref[p], 0, 0))
+        specs.extend([stays, stays, goes, goes])
+        operands.extend([kept.reshape(shape), value.reshape(shape)] * 2)
+        out_specs.extend([pl.BlockSpec((part, rows, cols), lambda i, side_ref: (i, 0, 0))] * 2)
+        out_shapes.extend([jax.ShapeDtypeStruct((blocks // 2, rows, cols), kept.dtype)] * 2)
+    outs = pl.pallas_call(
         add_split_kernel,
         grid_spec=pltpu.PrefetchScalarGridSpec(
             num_scalar_prefetch=1,
             grid=(blocks // (2 * part),),
-            in_specs=[stays, stays, goes, goes],
-            out_specs=[out_spec, out_spec],
+            in_specs=specs,
+            out_specs=out_specs,
         ),
-        out_shape=[out_shape, out_shape],
+        out_shape=out_shapes,
         cost_estimate=LIGHT,
         name="add_split",
-    )(bit.reshape(1), kept, received, kept, received)
-
-
-def add_far_kernel(count, place_ref, *refs):
-    outs = refs[2 * count :]
-    for slot, out in enumerate(outs):
-
-        @pl.when(pl.program_id(0) == slot)
+    )(jnp.stack(bits), *operands)
+    return list(outs[::2]), list(outs[1::2])
+
+
+def add_join_kernel(count, place_ref, *refs):
+    for slot, out in enumerate(refs[2 * count :]):
+
+        @pl.when(pl.program_id(1) == slot)
         def _(out=out):
             start = 0
             for one, two in zip(refs[:count], refs[count : 2 * count]):
-                total = one[0].astype(jnp.float32) + two[0].astype(jnp.float32)
+                total = one[0] + two[0]
                 width = total.shape[-1]
-                out[:, start : start + width] = total.astype(jnp.bfloat16)
+                out[0, :, start : start + width] = total
                 start += width
 
 
-def add_far(kept, received, place, slots):
-    rows = kept[0].shape[1]
+def add_join(kept, received, bit):
+    blocks, rows, unused = kept[0].shape
     width = sum(value.shape[2] for value in kept)
     specs = [
-        pl.BlockSpec((1, rows, value.shape[2]), lambda i, place_ref: (place_ref[0] ^ i, 0, 0))
+        pl.BlockSpec(
+            (1, rows, value.shape[2]), lambda i, j, side_ref: (2 * i + (side_ref[0] ^ j), 0, 0)
+        )
         for value in kept
     ]
     return pl.pallas_call(
-        functools.partial(add_far_kernel, len(kept)),
+        functools.partial(add_join_kernel, len(kept)),
         grid_spec=pltpu.PrefetchScalarGridSpec(
             num_scalar_prefetch=1,
-            grid=(slots,),
+            grid=(blocks // 2, 2),
             in_specs=specs + specs,
-            out_specs=[pl.BlockSpec((rows, width), lambda i, place_ref: (0, 0))] * slots,
+            out_specs=[pl.BlockSpec((1, rows, width), lambda i, j, side_ref: (i, 0, 0))] * 2,
         ),
-        out_shape=[jax.ShapeDtypeStruct((rows, width), kept[0].dtype)] * slots,
+        out_shape=[jax.ShapeDtypeStruct((blocks // 2, rows, width), kept[0].dtype)] * 2,
         cost_estimate=LIGHT,
-        name="add_far",
-    )(place.reshape(1), *kept, *received)
+        name="add_join",
+    )(bit.reshape(1), *kept, *received)
 
 
 class Joint:
@@ -741,15 +767,12 @@
         masks, core = bit_masks(sizes)
         self.near = masks[-2:]
         self.far = far_groups(sizes)[0]
-        self.flips = [flip for exchange, flip, start, cols in parts]
-        pairs = [
-            split_product(
-                exchange.acts, exchange.grad, exchange.theirs, sizes, flip, start, cols
-            )
-            for exchange, flip, start, cols in parts
-        ]
-        self.kept = [pair[0] for pair in pairs]
-        self.away = [pair[1] for pair in pairs]
+        self.flips, self.kept, self.away = [], [], []
+        for exchange, flips in parts:
+            outs = split_product(exchange.acts, exchange.grad, exchange.theirs, sizes, flips)
+            self.kept.extend(outs[::2])
+            self.away.extend(outs[1::2])
+            self.flips.extend(flips)
         self.masks = [self.near[0] if flip else self.near[1] for flip in self.flips]
         self.received = None
         self.stage = 0
@@ -762,23 +785,18 @@
         self.stage += 1
         if self.stage == 1:
             self.masks = [self.near[1] if flip else self.near[0] for flip in self.flips]
-            pairs = [
-                add_split(kept, value, small_index([mask], self.sizes))
-                for kept, value, mask in zip(self.kept, received, self.masks)
-            ]
-            self.kept = [pair[0] for pair in pairs]
-            self.away = [pair[1] for pair in pairs]
+            bits = [small_index([mask], self.sizes) for mask in self.masks]
+            self.kept, self.away = add_split(self.kept, received, bits)
         elif self.stage == 2:
-            self.masks = combined(self.far)[1:]
-            outs = add_far(
-                self.kept, received, small_index(self.far, self.sizes), 2 ** len(self.far)
-            )
-            self.kept, self.away = outs[0], list(outs[1:])
+            self.masks = [self.far[1]]
+            kept, away = add_join(self.kept, received, small_index(self.masks, self.sizes))
+            self.kept, self.away = [kept], [away]
+        elif self.stage == 3:
+            self.masks = [self.far[0]]
+            bits = [small_index(self.masks, self.sizes)]
+            self.kept, self.away = add_split(self.kept, received, bits)
         else:
-            total = self.kept.astype(jnp.float32)
-            for value in received:
-                total = total + value.astype(jnp.float32)
-            self.total = total
+            self.total = self.kept[0][0].astype(jnp.float32) + received[0][0].astype(jnp.float32)
             self.away = []
 
     def result(self):
@@ -788,9 +806,9 @@
 class Plain:
     def __init__(self, parts, sizes):
         self.chains = []
-        for exchange, flip, start, cols in parts:
+        for exchange, flips in parts:
             kept = half_product(exchange.acts, exchange.grad, sizes, exchange.theirs)
-            self.chains.append(Scatter([kept[:, start : start + cols]], sizes, flip))
+            self.chains.append(Scatter([kept], sizes, flips[0]))
         self.received = None
 
     @property
@@ -821,8 +839,10 @@
 
 
 def summed(parts, sizes):
-    heights = [exchange.acts.shape[1] // (sizes[0] * sizes[1]) for exchange, *unused in parts]
-    if len(far_groups(sizes)) == 1 and all(height % 16 == 0 for height in heights):
+    heights = [exchange.acts.shape[1] // (sizes[0] * sizes[1]) for exchange, unused in parts]
+    groups = far_groups(sizes)
+    fits = all(height % 16 == 0 for height in heights)
+    if len(groups) == 1 and len(groups[0]) == 2 and fits:
         return Joint(parts, sizes)
     return Plain(parts, sizes)
 
@@ -1000,47 +1020,59 @@
     )
     widths = [vec.shape[0] for vec in vectors]
 
-    def weight(shard, flip):
-        return Gather(shard, sizes, flip)
-
-    f_a = weight(jnp.concatenate([frame_query, frame_keys], axis=1)[None], False)
     shard_rows = frame_values.shape[0]
     packed = jnp.concatenate([vec[None] for vec in vectors], axis=1)
     packed = jnp.pad(packed, ((0, 0), (0, shard_rows * 128 - packed.shape[1])))
     packed = packed.reshape(shard_rows, 128)
-    f_b = Gather(
+    f_ab = Gather(
         jnp.stack(
             [
-                jnp.concatenate([frame_values, packed], axis=1),
-                jnp.concatenate([frame_outproj, packed], axis=1),
+                jnp.concatenate([frame_query, frame_keys, packed], axis=1),
+                jnp.concatenate([frame_values, frame_outproj, packed], axis=1),
             ]
         ),
         sizes,
-        True,
-        128,
-    )
-    f_u = weight(frame_upproj[None], False)
-    f_d = weight(frame_downproj[None], True)
-    c_a = weight(jnp.concatenate([code_query, code_keys], axis=1)[None], False)
-    c_b = weight(jnp.stack([code_values, code_outproj]), True)
-    c_u = weight(code_upproj[None], False)
-    c_d = weight(code_downproj[None], True)
-    f_attn, f_ff, c_attn, c_ff = [f_a, f_b], [f_u, f_d], [c_a, c_b], [c_u, c_d]
-
-    for unused in range(len(f_a.far) - 1):
-        for chains in (f_attn, f_ff, c_attn, c_ff):
-            started(chains)
-            ended(chains)
-    started(f_attn)
-    ended(f_attn)
-    started(f_attn + f_ff)
-    ended(f_attn)
-    started(f_attn)
-    ended(f_attn + f_ff)
-    started(f_attn + f_ff + c_attn)
-    ended(f_attn + f_ff + c_attn)
-    started(f_ff)
-    whole = f_b.tails[0].reshape(devices, -1)[:, : sum(widths)].astype(jnp.float32)
+        (False, True),
+        ([2 * D, 128], [D, D, 128]),
+    )
+    c_ab = Gather(
+        jnp.stack(
+            [
+                jnp.concatenate([code_query, code_keys], axis=1),
+                jnp.concatenate([code_values, code_outproj], axis=1),
+            ]
+        ),
+        sizes,
+        (False, True),
+        ([2 * D], [D, D]),
+    )
+
+    def gathered(shard):
+        return lax.all_gather(shard, ("gx", "gy"), axis=0, tiled=True)
+
+    f_up, f_down = gathered(frame_upproj), gathered(frame_downproj)
+    c_up = gathered(code_upproj)
+    c_d = Gather(code_downproj[None], sizes, (True,), ([D],))
+    for unused in range(len(f_ab.far) - 1):
+        started([f_ab])
+        ended([f_ab])
+        started([c_ab])
+        ended([c_ab])
+        started([c_d])
+        ended([c_d])
+    started([f_ab])
+    ended([f_ab])
+    started([f_ab])
+    code_rows = jnp.swapaxes(code_embed, 0, 1)
+    grad_code_y = jnp.swapaxes(code_cotangent, 0, 1)
+    code_rows, grad_code_y = ended([f_ab], code_rows, grad_code_y)
+    started([f_ab, c_ab])
+    ended([f_ab, c_ab])
+    started([f_ab, c_ab])
+    ended([f_ab, c_ab])
+    f_pair = f_ab.whole[0][0]
+    f_value, f_out, tail = f_ab.whole[1]
+    whole = tail.reshape(devices, -1)[:, : sum(widths)].astype(jnp.float32)
     gains = []
     start = 0
     for width in widths:
@@ -1050,59 +1082,45 @@
     code_gains = tuple(gains[4:])
     frame_x = frame_input.astype(jnp.float32)
     f_normed = rms_scale(frame_x, frame_gains[0]).astype(low)
-    f_pair = f_a.whole[0]
-    f_value, f_out = f_b.whole
-
+    started([c_ab, c_d])
     segments = segment_ids[0]
     f_qk = times(f_normed, f_pair).astype(low)
     f_v = times(f_normed, f_value).astype(low)
     f_mixed = frame_attend(f_qk, f_v, segments)
+    f_qk, f_v, f_mixed = ended([c_ab, c_d], f_qk, f_v, f_mixed)
+    started([c_ab, c_d])
     f_hidden = frame_x + times(f_mixed, f_out)
     f_normed_two = rms_scale(f_hidden, frame_gains[1]).astype(low)
-    f_hidden, f_normed_two = ended(f_ff, f_hidden, f_normed_two)
-    started(f_ff + c_attn + c_ff)
-    code_rows = jnp.swapaxes(code_embed, 0, 1)
-    grad_code_y = jnp.swapaxes(code_cotangent, 0, 1)
-    code_rows, grad_code_y = ended(f_ff + c_attn, code_rows, grad_code_y)
-    started(c_attn)
-    (f_up,) = f_u.whole
-    (f_down,) = f_d.whole
+    f_hidden, f_normed_two = ended([c_ab, c_d], f_hidden, f_normed_two)
+    started([c_d])
     f_act, f_slope = gelu_and_slope(times(f_normed_two, f_up) + frame_gains[2])
     rows = CB * frames
     grad_code_y = grad_code_y.reshape(rows, D)
-    f_act, f_slope = ended(c_attn + c_ff, f_act, f_slope)
-    started(c_attn + c_ff)
     frame_y = f_hidden + (times(f_act, f_down) + frame_gains[3])
+
+    def tokens_of(value):
+        return value.reshape(CB, frames, value.shape[-1])
 
     code_x = (code_rows.astype(jnp.float32) + frame_y[None]).reshape(rows, D)
     c_normed = rms_scale(code_x, code_gains[0]).astype(low)
-    c_normed, code_x = ended(c_attn + c_ff, c_normed, code_x)
-    started(c_ff)
-    c_pair = c_a.whole[0]
-    c_value, c_out = c_b.whole
-
-    def tokens_of(value):
-        return value.reshape(CB, frames, value.shape[-1])
-
+    c_pair = c_ab.whole[0][0]
+    c_value, c_out = c_ab.whole[1]
     c_qk = times(c_normed, c_pair).astype(low)
     c_v = times(c_normed, c_value).astype(low)
-    c_qk, c_v = ended(c_ff, c_qk, c_v)
-    started(c_ff)
     c_mixed = code_attend(tokens_of(c_qk), tokens_of(c_v)).reshape(rows, D)
     c_hidden = code_x + times(c_mixed, c_out)
+    (c_hidden,) = ended([c_d], c_hidden)
+    started([c_d])
     c_normed_two = rms_scale(c_hidden, code_gains[1]).astype(low)
-    c_hidden, c_normed_two = ended([c_u], c_hidden, c_normed_two)
-    (c_up,) = c_u.whole
+    (c_normed_two,) = ended([c_d], c_normed_two)
+    ((c_down,),) = c_d.whole
     c_act, c_slope = gelu_and_slope(times(c_normed_two, c_up) + code_gains[2])
-    c_act, c_slope = ended([c_d], c_act, c_slope)
-    (c_down,) = c_d.whole
 
     def both(exchange):
-        half = exchange.grad.shape[1] // 2
-        return [summed([(exchange, True, 0, half), (exchange, False, half, half)], sizes)]
+        return [summed([(exchange, (True, False))], sizes)]
 
     def attention_sums(pair, value, outproj):
-        parts = [(pair, False, 0, 2 * D), (value, True, 0, D), (outproj, True, 0, D)]
+        parts = [(pair, (False,)), (value, (True,)), (outproj, (True,))]
         return [summed(parts, sizes)]
 
     def norm_back(grad_out, inputs, gain):
@@ -1125,7 +1143,9 @@
     grad_part, c_grad_mid = norm_back(grad_two, c_hidden, code_gains[1])
     grad_hidden = grad_low.astype(jnp.float32) + grad_part
     grad_attn = grad_hidden.astype(low)
-    grad_attn, grad_hidden = scatter_round(c_d_chain, c_u_chain, grad_attn, grad_hidden)
+    grad_attn, grad_hidden = scatter_round(
+        c_d_chain, c_d_chain + c_u_chain, grad_attn, grad_hidden
+    )
     c_o_core = Core(c_mixed, grad_attn, sizes)
     grad_mixed = against(grad_attn, c_out).astype(low)
     grad_pair, grad_values = code_attend_back(
@@ -1134,7 +1154,7 @@
     grad_pair = grad_pair.reshape(rows, 2 * D)
     grad_values = grad_values.reshape(rows, D)
     grad_pair, grad_values = scatter_round(
-        c_u_chain, c_u_chain + [c_o_core], grad_pair, grad_values
+        c_d_chain + c_u_chain, c_u_chain + [c_o_core], grad_pair, grad_values
     )
     c_p_core = Core(c_normed, grad_pair, sizes)
     c_v_core = Core(c_normed, grad_values, sizes)
@@ -1145,46 +1165,49 @@
     grad_part, c_grad_pre = norm_back(grad_normed, code_x, code_gains[0])
     grad_code_x = grad_hidden + grad_part
     grad_frame_y = frame_cotangent.astype(jnp.float32) + jnp.sum(tokens_of(grad_code_x), axis=0)
-    grad_code_x, grad_frame_y = ended(
-        c_u_chain + [c_p_core, c_v_core], grad_code_x, grad_frame_y
-    )
-    c_ab = attention_sums(c_p_core, c_v_core, c_o_core)
-    (grad_frame_y,) = scatter_round([], c_ab, grad_frame_y)
+    grad_code_x, grad_frame_y = scatter_round(
+        c_u_chain + [c_p_core, c_v_core], c_u_chain, grad_code_x, grad_frame_y
+    )
+    c_sums = attention_sums(c_p_core, c_v_core, c_o_core)
+    (grad_frame_y,) = scatter_round(c_u_chain, c_sums, grad_frame_y)
 
     grad_low = grad_frame_y.astype(low)
     f_d_core = Core(f_act, grad_low, sizes)
     grad_pre, f_grad_b_up = grad_pre_of(grad_low, f_down, f_slope)
     f_u_core = Core(f_normed_two, grad_pre, sizes)
-    (grad_pre,) = scatter_round(c_ab, c_ab + [f_d_core, f_u_core], grad_pre)
+    (grad_pre,) = scatter_round(c_sums, c_sums + [f_d_core, f_u_core], grad_pre)
     grad_two = grad_two_of(grad_pre, f_up)
     grad_part, f_grad_mid = norm_back(grad_two, f_hidden, frame_gains[1])
     grad_hidden = grad_frame_y + grad_part
     grad_attn = grad_hidden.astype(low)
     grad_attn, grad_hidden = scatter_round(
-        c_ab + [f_d_core, f_u_core], c_ab, grad_attn, grad_hidden
+        c_sums + [f_d_core, f_u_core], c_sums, grad_attn, grad_hidden
     )
     f_d_chain = both(f_d_core)
-    grad_attn, grad_hidden = scatter_round(c_ab, f_d_chain, grad_attn, grad_hidden)
+    grad_attn, grad_hidden = scatter_round(
+        c_sums, c_sums + f_d_chain, grad_attn, grad_hidden
+    )
     f_u_chain = both(f_u_core)
     f_o_core = Core(f_mixed, grad_attn, sizes)
     grad_mixed = against(grad_attn, f_out).astype(low)
     grad_pair, grad_values = frame_attend_back(f_qk, f_v, grad_mixed, segments)
-    grad_pair, grad_values = scatter_round(
-        f_d_chain, f_d_chain + f_u_chain + [f_o_core], grad_pair, grad_values
+    grad_pair, grad_values, c_act = scatter_round(
+        c_sums + f_d_chain, f_d_chain + f_u_chain + [f_o_core], grad_pair, grad_values, c_act
     )
     f_p_core = Core(f_normed, grad_pair, sizes)
     f_v_core = Core(f_normed, grad_values, sizes)
+    code_y = c_hidden + (times(c_act, c_down) + code_gains[3])
+    code_y, grad_pair, grad_values = scatter_round(
+        f_d_chain + f_u_chain + [f_o_core],
+        f_d_chain + f_u_chain + [f_p_core, f_v_core],
+        code_y,
+        grad_pair,
+        grad_values,
+    )
     grad_normed = against(grad_pair, f_pair) + against(grad_values, f_value)
     grad_part, f_grad_pre = norm_back(grad_normed, frame_x, frame_gains[0])
     grad_frame_x = grad_hidden + grad_part
-    (grad_frame_x,) = scatter_round(
-        f_d_chain + f_u_chain + [f_o_core],
-        f_d_chain + f_u_chain + [f_p_core, f_v_core],
-        grad_frame_x,
-    )
     f_grad_b_down = jnp.sum(grad_low.astype(jnp.float32), axis=0)
-    (f_grad_b_down,) = ended(f_u_chain + [f_p_core, f_v_core], f_grad_b_down)
-    f_ab = attention_sums(f_p_core, f_v_core, f_o_core)
     terms = jnp.concatenate(
         [
             term.reshape(devices, -1)
@@ -1202,15 +1225,21 @@
         axis=1,
     )
     row = VectorScatter(terms, sizes)
-    grad_frame_x, c_act = scatter_round(f_d_chain, f_ab + f_u_chain + [row], grad_frame_x, c_act)
-    code_y = c_hidden + (times(c_act, c_down) + code_gains[3])
+    (grad_frame_x,) = scatter_round(
+        f_d_chain + f_u_chain + [f_p_core, f_v_core],
+        f_d_chain + f_u_chain + [row],
+        grad_frame_x,
+    )
+    f_sums = attention_sums(f_p_core, f_v_core, f_o_core)
+    (code_y,) = scatter_round(
+        f_d_chain + f_u_chain + [row], f_d_chain + f_u_chain + f_sums + [row], code_y
+    )
     frame_output = frame_y.astype(low)
-    (code_y,) = scatter_round(f_ab + [row], f_ab + [row], code_y)
     code_output = jnp.swapaxes(tokens_of(code_y.astype(low)), 0, 1)
-    (code_output,) = scatter_round(f_ab + f_u_chain + [row], f_ab + [row], code_output)
+    (code_output,) = scatter_round(f_u_chain + f_sums + [row], f_sums + [row], code_output)
     code_embed_grad = jnp.swapaxes(tokens_of(grad_code_x), 0, 1)
-    (code_embed_grad,) = scatter_round(f_ab + [row], [row], code_embed_grad)
-    everything = c_d_chain + c_u_chain + c_ab + f_d_chain + f_u_chain + f_ab + [row]
+    (code_embed_grad,) = scatter_round(f_sums + [row], f_sums + [row], code_embed_grad)
+    everything = c_d_chain + c_u_chain + c_sums + f_d_chain + f_u_chain + f_sums + [row]
     while True:
         started([chain for chain in everything if chain.away and chain.received is None])
         going = [chain for chain in everything if chain.received is not None]
@@ -1234,14 +1263,16 @@
             total[:, 2 * D : 3 * D],
             total[:, 3 * D :],
             midnorm,
-            up_sums[0].result(),
+            up_sums,
             upbias,
-            down_sums[0].result(),
+            down_sums,
             downbias,
         )
 
-    code_outs = arranged(c_ab, c_u_chain, c_d_chain, pieces[4:])
-    frame_outs = arranged(f_ab, f_u_chain, f_d_chain, pieces[:4])
+    code_outs = arranged(c_sums, c_u_chain[0].result(), c_d_chain[0].result(), pieces[4:])
+    frame_outs = arranged(
+        f_sums, f_u_chain[0].result(), f_d_chain[0].result(), pieces[:4]
+    )
     return (frame_output, code_output, grad_frame_x, code_embed_grad) + frame_outs + code_outs
 
 

time: 876 us -> 816 us (0.932)
  starting transfers between devices: 152 us -> 99.4 us
  between operations: 2.01 us -> 15.3 us
  matrix products: 101 us -> 87.9 us
  Pallas kernels: 329 us -> 319 us
    ppermute x141 -> x79, starting transfers between devices: 152 us -> 99.3 us  [swap(): lax.ppermute(value, ('gx', 'gy'), [(place, place ^ mask) for place in ran...]
    dot_general x6, matrix products: 31.4 us -> 21.1 us  [against(): lax.dot_general(left, right, (((1,), (1,)), ((), ())), preferred_element_...]
    pallas_call x8 -> x3, Pallas kernels: 16.5 us -> 6.52 us  [placed_far(): pl.pallas_call(place_far_kernel, grid_spec=pltpu.PrefetchScalarGridSpec(n...]
    ppermute x141 -> x79, waiting for transfers between devices: 215 us -> 219 us  [swap(): lax.ppermute(value, ('gx', 'gy'), [(place, place ^ mask) for place in ran...]
    pallas_call x30 -> x31, Pallas kernels: 153 us -> 149 us  [the longest x15 66.2 us: merged(): pl.pallas_call(merge_kernel, grid_spec=pltpu.PrefetchScalarGridSpec(num_s...]
    pallas_call x14 -> x12, Pallas kernels: 34.9 us -> 38.4 us  [add_split(): pl.pallas_call(add_split_kernel, grid_spec=pltpu.PrefetchScalarGridSpec(n...]
  transfers between devices with their start and end apart: 141 -> 82, of which waited for: 42 -> 34; matrix products, arithmetic and copies ran while one was open for 17% -> 14% of each run, Pallas kernels for 28% -> 30%
where the time goes in v3:
time: 816 us; the launch traced here: 806 us
  Pallas kernels  319 us (39%)
  waiting for transfers between devices  221 us (27%)
  starting transfers between devices  99.4 us (12%)
  matrix products  87.9 us (11%)
  other arithmetic  39.2 us (5%)
  local copies, waits for them, and re-layouts  25.2 us (3%)
  between operations  15.3 us (2%)
    ppermute x79, waiting for transfers between devices, swap(): lax.ppermute(value, ('gx', 'gy'), [(place, place ^ mask) for place in ran...  219 us
    ppermute x79, starting transfers between devices, swap(): lax.ppermute(value, ('gx', 'gy'), [(place, place ^ mask) for place in ran...  99.3 us
    dot_general x10, matrix products, times(): return jnp.dot(left, right, preferred_element_type=jnp.float32)  66.8 us
    pallas_call x15, Pallas kernels, merged(): pl.pallas_call(merge_kernel, grid_spec=pltpu.PrefetchScalarGridSpec(num_s...  66.2 us
    pallas_call x10, Pallas kernels, split_product(): pl.pallas_call(functools.partial(split_kernel, flips), grid_spec=pltpu.Pr...  61.9 us
    pallas_call x10, Pallas kernels, half_product(): pl.pallas_call(half_kernel if received is None else half_add_kernel, grid...  45.4 us
    pallas_call x12, Pallas kernels, add_split(): pl.pallas_call(add_split_kernel, grid_spec=pltpu.PrefetchScalarGridSpec(n...  38.4 us
    dot_general x6, matrix products, against(): lax.dot_general(left, right, (((1,), (1,)), ((), ())), preferred_element_...  21.1 us
  transfers between devices with their start and end apart: 82, of which 34 were waited for; matrix products, arithmetic and copies ran while one was open for 14% of the time, Pallas kernels for 30%

profile of v3, /device:TPU:0, one launch (start us, length us, event | category | flops | bytes accessed | tf_op | source)
XLA Modules:
  0.0 806.3 jit_solution(8644945699851018029)
XLA Ops:
  16.4 10.1 %collective-permute-done.refs_1_ = bf16[2,32,2176]{2,1,0:T(8,128)(2,1)S(1)} collective-permute-done((bf16[2,32,2176]{2,1,0:T(8,128)(2,1)S(1)}, bf16[2,32,2176]{2,1,0:T(8,128)(2,1)S(1)}, u32[]{:S(2)}, u32[]{:S(2)}) %collective-permute-start) | collective-permute-done | bytes 278560 | tf_op jit(solution)/shard_map/ppermute | solution.py:303
  26.5 12.7 %collective-permute-done.1.refs_2_ = bf16[2,32,2176]{2,1,0:T(8,128)(2,1)S(1)} collective-permute-done((bf16[2,32,2176]{2,1,0:T(8,128)(2,1)S(1)}, bf16[2,32,2176]{2,1,0:T(8,128)(2,1)S(1)}, u32[]{:S(2)}, u32[]{:S(2)}) %collective-permute-start.1) | collective-permute-done | bytes 278560 | tf_op jit(solution)/shard_map/ppermute | solution.py:303
  46.6 12.1 %collective-permute-done.3.theirs_ref = bf16[4,32,2176]{2,1,0:T(8,128)(2,1)S(1)} collective-permute-done((bf16[4,32,2176]{2,1,0:T(8,128)(2,1)S(1)}, bf16[4,32,2176]{2,1,0:T(8,128)(2,1)S(1)}, u32[]{:S(2)}, u32[]{:S(2)}) %collective-permute-start.3) | collective-permute-done | bytes 557088 | tf_op jit(solution)/shard_map/ppermute | solution.py:303
  73.9 8.9 %collective-permute-start.7 = (bf16[2,32,2048]{2,1,0:T(8,128)(2,1)S(1)}, bf16[2,32,2048]{2,1,0:T(8,128)(2,1)S(1)}, u32[]{:S(2)}, u32[]{:S(2)}) collective-permute-start(bf16[2,32,2048]{2,1,0:T(8,128)(2,1)S(1)} %pad_maximum_fusion.1.refs_0_), channel_id=1, source_target_pairs={{0,4},{1,5},{2,6},{3,7},{4,0},{5,1},{6,2},{7,3},{8,12},{9,13},{10,... | collective-permute-start | bytes 786440 | tf_op jit(solution)/shard_map/ppermute | solution.py:303
  85.4 19.5 %collective-permute-done.7.refs_1_ = bf16[2,32,2048]{2,1,0:T(8,128)(2,1)S(1)} collective-permute-done((bf16[2,32,2048]{2,1,0:T(8,128)(2,1)S(1)}, bf16[2,32,2048]{2,1,0:T(8,128)(2,1)S(1)}, u32[]{:S(2)}, u32[]{:S(2)}) %collective-permute-start.7) | collective-permute-done | bytes 262176 | tf_op jit(solution)/shard_map/ppermute | solution.py:303
  106.3 13.4 %collective-permute-done.9.refs_3_ = bf16[2,32,2048]{2,1,0:T(8,128)(2,1)S(1)} collective-permute-done((bf16[2,32,2048]{2,1,0:T(8,128)(2,1)S(1)}, bf16[2,32,2048]{2,1,0:T(8,128)(2,1)S(1)}, u32[]{:S(2)}, u32[]{:S(2)}) %collective-permute-start.9) | collective-permute-done | bytes 262176 | tf_op jit(solution)/shard_map/ppermute | solution.py:303
  136.6 8.7 %collective-permute-start.16 = (bf16[1,128,1024]{2,1,0:T(8,128)(2,1)S(1)}, bf16[1,128,1024]{2,1,0:T(8,128)(2,1)}, u32[]{:S(2)}, u32[]{:S(2)}) collective-permute-start(bf16[1,128,1024]{2,1,0:T(8,128)(2,1)S(1)} %bitcast.356), channel_id=1, source_target_pairs={{0,4},{1,5},{2,6},{3,7},{4,0},{5,1},{6,2},{7,3},{8,12},{9,13},{10,... | collective-permute-start | bytes 786440 | tf_op jit(solution)/shard_map/ppermute | solution.py:303
  186.6 7.7 frame_attend.1.acts_ref
  221.4 20.2 %collective-permute-done.21.theirs_ref = bf16[4,128,1024]{2,1,0:T(8,128)(2,1)S(1)} collective-permute-done((bf16[4,128,1024]{2,1,0:T(8,128)(2,1)}, bf16[4,128,1024]{2,1,0:T(8,128)(2,1)S(1)}, u32[]{:S(2)}, u32[]{:S(2)}) %collective-permute-start.21) | collective-permute-done | bytes 1048608 | tf_op jit(solution)/shard_map/ppermute | solution.py:303
  255.2 9.2 %add_convert_fusion.1 = (bf16[256,4096]{1,0:T(8,128)(2,1)}, bf16[256,4096]{1,0:T(8,128)(2,1)S(1)}) fusion(f32[4096]{0:T(1024)S(1)} %get-tuple-element.655, bf16[256,1024]{1,0:T(8,128)(2,1)} %multiply_convert_fusion.3.acts_ref, bf16[1024,4096]{1,0:T(8,128)(2,1)} %all-gather.4.cloned.1.call-done.weight_ref), kind=kOutput, calls=%fused_computation.8 | convolution fusion | flops 2164260864 | bytes 13123584 | tf_op jit(solution)/shard_map/dot_general | solution.py:908
  293.9 17.8 %collective-permute-done.22 = bf16[8,128,1024]{2,1,0:T(8,128)(2,1)} collective-permute-done((bf16[8,128,1024]{2,1,0:T(8,128)(2,1)}, bf16[8,128,1024]{2,1,0:T(8,128)(2,1)}, u32[]{:S(2)}, u32[]{:S(2)}) %collective-permute-start.22) | collective-permute-done | bytes 2097184 | tf_op jit(solution)/shard_map/ppermute | solution.py:303
  324.1 16.9 %add_convert_fusion = (bf16[768,4096]{1,0:T(8,128)(2,1)}, bf16[768,4096]{1,0:T(8,128)(2,1)}) fusion(f32[4096]{0:T(1024)S(1)} %get-tuple-element.654, bf16[768,1024]{1,0:T(8,128)(2,1)} %multiply_convert_fusion.acts_ref, bf16[1024,4096]{1,0:T(8,128)(2,1)} %all-gather.8.cloned.1.call-done.weight_ref), kind=kOutput, calls=%fused_computation | convolution fusion | flops 6492782592 | bytes 22560768 | tf_op jit(solution)/shard_map/dot_general | solution.py:908
  356.0 9.6 %split_product.10 = (bf16[8,128,512]{2,1,0:T(8,128)(2,1)}, bf16[8,128,512]{2,1,0:T(8,128)(2,1)}, bf16[8,128,512]{2,1,0:T(8,128)(2,1)}, bf16[8,128,512]{2,1,0:T(8,128)(2,1)}) custom-call(s32[3]{0:T(128)} %add_add_fusion.6.side_ref, bf16[768,4096]{1,0:T(8,128)(2,1)} %get-tuple-element.514.acts_ref, bf16[768,1024]{1,0:T(8,128)(2,1)} %bitcast.226, ...), custom_call_target="tpu_custom_call" | custom-call | flops 1 | bytes 1 | tf_op jit(solution)/shard_map/split_product/pallas_call | solution.py:676
  376.6 13.1 %grad_pre.2 = (bf16[768,4096]{1,0:T(8,128)(2,1)}, f32[1,4096]{1,0:T(1,128)}) custom-call(bf16[768,1024]{1,0:T(8,128)(2,1)} %bitcast.228, bf16[4096,1024]{1,0:T(8,128)(2,1)} %bitcast.231, bf16[768,4096]{1,0:T(8,128)(2,1)} %get-tuple-element.368.slope_ref), custom_call_target="tpu_custom_call" | custom-call | flops 1 | bytes 1 | tf_op jit(solution)/shard_map/grad_pre/pallas_call | solution.py:958
  389.7 7.6 half_away.11
  403.9 12.8 %grad_two.2 = f32[768,1024]{1,0:T(8,128)} custom-call(bf16[768,4096]{1,0:T(8,128)(2,1)} %get-tuple-element.382.grad_ref.refs_0_.refs_2_, bf16[1024,4096]{1,0:T(8,128)(2,1)} %all-gather.8.cloned.1.call-done.weight_ref), custom_call_target="tpu_custom_call" | custom-call | flops 1 | bytes 1 | tf_op jit(solution)/shard_map/grad_two/pallas_call | solution.py:940
  423.8 10.2 %split_product.11 = (bf16[8,32,2048]{2,1,0:T(8,128)(2,1)}, bf16[8,32,2048]{2,1,0:T(8,128)(2,1)}, bf16[8,32,2048]{2,1,0:T(8,128)(2,1)}, bf16[8,32,2048]{2,1,0:T(8,128)(2,1)}) custom-call(s32[3]{0:T(128)} %add_add_fusion.6.side_ref, bf16[768,1024]{1,0:T(8,128)(2,1)} %multiply_convert_fusion.acts_ref, ...), custom_call_target="tpu_custom_call" | custom-call | flops 1 | bytes 1 | tf_op jit(solution)/shard_map/split_product/pallas_call | solution.py:676
  453.9 11.4 %code_attend_back.1 = (bf16[3,256,2048]{2,1,0:T(8,128)(2,1)}, bf16[3,256,1024]{2,1,0:T(8,128)(2,1)}) custom-call(bf16[3,256,2048]{2,1,0:T(8,128)(2,1)} %bitcast.239, bf16[3,256,1024]{2,1,0:T(8,128)(2,1)} %bitcast.261, bf16[3,256,1024]{2,1,0:T(8,128)(2,1)} %bitcast.350, bf16[1024,128]{1,0:T(8,128)(2,1)} %fusion.16.marks_ref), custom_call_target="tpu_custom_call" | custom-call | flops 1 | bytes 1 | tf_op jit(solution)/shard_map/code_attend_back/pallas_call | solution.py:156
  540.5 7.8 grad_pre.3
  599.5 7.7 split_product.16
  615.6 12.4 %frame_attend_back.1 = (bf16[256,2048]{1,0:T(8,128)(2,1)}, bf16[256,1024]{1,0:T(8,128)(2,1)}) custom-call(bf16[256,2048]{1,0:T(8,128)(2,1)} %convolution_convert_fusion.1.query_ref.keys_ref, bf16[256,2048]{1,0:T(8,128)(2,1)} %convolution_convert_fusion.1.query_ref.keys_ref, bf16[256,1024]{1,0:T(8,128)(2,1)} %convolution_convert_fusion.5.values_ref, ...), custom_call_target="tpu_custom_call" | custom-call | flops 1 | bytes 1 | tf_op jit(solution)/shard_map/frame_attend_back/pallas_call | solution.py:267
  637.9 12.3 %add_add_fusion.2 = bf16[768,1024]{1,0:T(8,128)(2,1)} fusion(f32[768,1024]{1,0:T(8,128)S(1)} %copy-done.4, bf16[768,4096]{1,0:T(8,128)(2,1)} %get-tuple-element.514.acts_ref, bf16[4096,1024]{1,0:T(8,128)(2,1)} %bitcast.232, f32[1024]{0:T(1024)S(1)} %add.487), kind=kOutput, calls=%fused_computation.23 | convolution fusion | flops 6444810240 | bytes 19402752 | tf_op jit(solution)/shard_map/dot_general | solution.py:908
  655.8 12.5 %collective-permute-done.53.refs_2_ = bf16[4,128,512]{2,1,0:T(8,128)(2,1)} collective-permute-done((bf16[4,128,512]{2,1,0:T(8,128)(2,1)}, bf16[4,128,512]{2,1,0:T(8,128)(2,1)}, u32[]{:S(2)}, u32[]{:S(2)}) %collective-permute-start.53) | collective-permute-done | bytes 524320 | tf_op jit(solution)/shard_map/ppermute | solution.py:303
  732.4 17.0 %collective-permute-done.70 = f32[8,448]{1,0:T(8,128)S(1)} collective-permute-done((f32[8,448]{1,0:T(8,128)S(1)}, f32[8,448]{1,0:T(8,128)S(1)}, u32[]{:S(2)}, u32[]{:S(2)}) %collective-permute-start.70) | collective-permute-done | bytes 14368 | tf_op jit(solution)/shard_map/ppermute | solution.py:303
  (501 shorter events, 499.5 us)
Async XLA Ops:
  7.2 248.0 %all-gather.4.cloned.1.call-start = ((), (), s32[]{:S(2)}) async-start(), calls=%async_computation | async-start | bytes 8650752 | tf_op jit(solution)/shard_map/all_gather | solution.py:1051
  7.9 256.4 %all-gather.6.cloned.1.call-start = ((), (), s32[]{:S(2)}) async-start(), calls=%async_computation.1 | async-start | bytes 8650752 | tf_op jit(solution)/shard_map/all_gather | solution.py:1051
  8.7 315.5 %all-gather.8.cloned.1.call-start = ((), (), s32[]{:S(2)}) async-start(), calls=%async_computation.2 | async-start | bytes 8650752 | tf_op jit(solution)/shard_map/all_gather | solution.py:1051
  67.8 51.9 %collective-permute-start.6 = (bf16[8,32,2176]{2,1,0:T(8,128)(2,1)}, bf16[8,32,2176]{2,1,0:T(8,128)(2,1)S(1)}, u32[]{:S(2)}, u32[]{:S(2)}) collective-permute-start(bf16[8,32,2176]{2,1,0:T(8,128)(2,1)} %bitcast.262), channel_id=1, source_target_pairs={{0,2},{1,3},{2,0},{3,1},{4,6},{5,7},{6,4},{7,5},{8,10},{9,11},{10,... | collective-permute-start | bytes 3342344 | tf_op jit(solution)/shard_map/ppermute | solution.py:303
  71.3 48.5 %collective-permute-start.5 = (bf16[8,32,2176]{2,1,0:T(8,128)(2,1)}, bf16[8,32,2176]{2,1,0:T(8,128)(2,1)S(1)}, u32[]{:S(2)}, u32[]{:S(2)}) collective-permute-start(bf16[8,32,2176]{2,1,0:T(8,128)(2,1)} %bitcast.264), channel_id=1, source_target_pairs={{0,1},{1,0},{2,3},{3,2},{4,5},{5,4},{6,7},{7,6},{8,9},{9,8},{10,11... | collective-permute-start | bytes 3342344 | tf_op jit(solution)/shard_map/ppermute | solution.py:303
  73.9 31.0 %collective-permute-start.7 = (bf16[2,32,2048]{2,1,0:T(8,128)(2,1)S(1)}, bf16[2,32,2048]{2,1,0:T(8,128)(2,1)S(1)}, u32[]{:S(2)}, u32[]{:S(2)}) collective-permute-start(bf16[2,32,2048]{2,1,0:T(8,128)(2,1)S(1)} %pad_maximum_fusion.1.refs_0_), channel_id=1, source_target_pairs={{0,4},{1,5},{2,6},{3,7},{4,0},{5,1},{6,2},{7,3},{8,12},{9,13},{10,... | collective-permute-start | bytes 786440 | tf_op jit(solution)/shard_map/ppermute | solution.py:303
  84.0 35.7 %collective-permute-start.9 = (bf16[2,32,2048]{2,1,0:T(8,128)(2,1)S(1)}, bf16[2,32,2048]{2,1,0:T(8,128)(2,1)S(1)}, u32[]{:S(2)}, u32[]{:S(2)}) collective-permute-start(bf16[2,32,2048]{2,1,0:T(8,128)(2,1)S(1)} %pad_maximum_fusion.1.refs_0_), channel_id=1, source_target_pairs={{0,12},{1,13},{2,14},{3,15},{4,8},{5,9},{6,10},{7,11},{8,4},{9,5},... | collective-permute-start | bytes 786440 | tf_op jit(solution)/shard_map/ppermute | solution.py:303
  124.7 34.8 %collective-permute-start.11 = (bf16[16,32,2176]{2,1,0:T(8,128)(2,1)}, bf16[16,32,2176]{2,1,0:T(8,128)(2,1)}, u32[]{:S(2)}, u32[]{:S(2)}) collective-permute-start(bf16[16,32,2176]{2,1,0:T(8,128)(2,1)} %bitcast.247), channel_id=1, source_target_pairs={{0,16},{1,17},{2,18},{3,19},{4,20},{5,21},{6,22},{7,23},{8,24},{9,... | collective-permute-start | bytes 6684680 | tf_op jit(solution)/shard_map/ppermute | solution.py:303
  130.6 28.9 %collective-permute-start.10 = (bf16[16,32,2176]{2,1,0:T(8,128)(2,1)}, bf16[16,32,2176]{2,1,0:T(8,128)(2,1)}, u32[]{:S(2)}, u32[]{:S(2)}) collective-permute-start(bf16[16,32,2176]{2,1,0:T(8,128)(2,1)} %bitcast.245), channel_id=1, source_target_pairs={{0,16},{1,17},{2,18},{3,19},{4,20},{5,21},{6,22},{7,23},{8,24},{9,... | collective-permute-start | bytes 6684680 | tf_op jit(solution)/shard_map/ppermute | solution.py:303
  136.6 57.8 %collective-permute-start.16 = (bf16[1,128,1024]{2,1,0:T(8,128)(2,1)S(1)}, bf16[1,128,1024]{2,1,0:T(8,128)(2,1)}, u32[]{:S(2)}, u32[]{:S(2)}) collective-permute-start(bf16[1,128,1024]{2,1,0:T(8,128)(2,1)S(1)} %bitcast.356), channel_id=1, source_target_pairs={{0,4},{1,5},{2,6},{3,7},{4,0},{5,1},{6,2},{7,3},{8,12},{9,13},{10,... | collective-permute-start | bytes 786440 | tf_op jit(solution)/shard_map/ppermute | solution.py:303
  150.5 43.9 %collective-permute-start.17 = (bf16[1,128,1024]{2,1,0:T(8,128)(2,1)S(1)}, bf16[1,128,1024]{2,1,0:T(8,128)(2,1)}, u32[]{:S(2)}, u32[]{:S(2)}) collective-permute-start(bf16[1,128,1024]{2,1,0:T(8,128)(2,1)S(1)} %bitcast.357), channel_id=1, source_target_pairs={{0,8},{1,9},{2,10},{3,11},{4,12},{5,13},{6,14},{7,15},{8,0},{9,1},... | collective-permute-start | bytes 786440 | tf_op jit(solution)/shard_map/ppermute | solution.py:303
  157.9 36.4 %collective-permute-start.18 = (bf16[1,128,1024]{2,1,0:T(8,128)(2,1)S(1)}, bf16[1,128,1024]{2,1,0:T(8,128)(2,1)}, u32[]{:S(2)}, u32[]{:S(2)}) collective-permute-start(bf16[1,128,1024]{2,1,0:T(8,128)(2,1)S(1)} %bitcast.358), channel_id=1, source_target_pairs={{0,12},{1,13},{2,14},{3,15},{4,8},{5,9},{6,10},{7,11},{8,4},{9,5},... | collective-permute-start | bytes 786440 | tf_op jit(solution)/shard_map/ppermute | solution.py:303
  205.0 36.6 %collective-permute-start.20 = (bf16[16,32,2048]{2,1,0:T(8,128)(2,1)}, bf16[16,32,2048]{2,1,0:T(8,128)(2,1)}, u32[]{:S(2)}, u32[]{:S(2)}) collective-permute-start(bf16[16,32,2048]{2,1,0:T(8,128)(2,1)} %bitcast.249), channel_id=1, source_target_pairs={{0,16},{1,17},{2,18},{3,19},{4,20},{5,21},{6,22},{7,23},{8,24},{9,... | collective-permute-start | bytes 6291464 | tf_op jit(solution)/shard_map/ppermute | solution.py:303
  210.9 30.7 %collective-permute-start.19 = (bf16[16,32,2048]{2,1,0:T(8,128)(2,1)}, bf16[16,32,2048]{2,1,0:T(8,128)(2,1)}, u32[]{:S(2)}, u32[]{:S(2)}) collective-permute-start(bf16[16,32,2048]{2,1,0:T(8,128)(2,1)} %bitcast.251), channel_id=1, source_target_pairs={{0,16},{1,17},{2,18},{3,19},{4,20},{5,21},{6,22},{7,23},{8,24},{9,... | collective-permute-start | bytes 6291464 | tf_op jit(solution)/shard_map/ppermute | solution.py:303
  246.3 65.3 %collective-permute-start.22 = (bf16[8,128,1024]{2,1,0:T(8,128)(2,1)}, bf16[8,128,1024]{2,1,0:T(8,128)(2,1)}, u32[]{:S(2)}, u32[]{:S(2)}) collective-permute-start(bf16[8,128,1024]{2,1,0:T(8,128)(2,1)} %bitcast.253), channel_id=1, source_target_pairs={{0,2},{1,3},{2,0},{3,1},{4,6},{5,7},{6,4},{7,5},{8,10},{9,11},{10,... | collective-permute-start | bytes 6291464 | tf_op jit(solution)/shard_map/ppermute | solution.py:303
  365.6 31.8 %collective-permute-start.25 = (bf16[8,128,512]{2,1,0:T(8,128)(2,1)}, bf16[8,128,512]{2,1,0:T(8,128)(2,1)S(1)}, u32[]{:S(2)}, u32[]{:S(2)}) collective-permute-start(bf16[8,128,512]{2,1,0:T(8,128)(2,1)} %get-tuple-element.371), channel_id=1, source_target_pairs={{0,2},{1,3},{2,0},{3,1},{4,6},{5,7},{6,4},{7,5},{8,10},{9,11},{10,... | collective-permute-start | bytes 3145736 | tf_op jit(solution)/shard_map/ppermute | solution.py:303
  366.7 30.6 %collective-permute-start.26 = (bf16[8,128,512]{2,1,0:T(8,128)(2,1)}, bf16[8,128,512]{2,1,0:T(8,128)(2,1)S(1)}, u32[]{:S(2)}, u32[]{:S(2)}) collective-permute-start(bf16[8,128,512]{2,1,0:T(8,128)(2,1)} %get-tuple-element.372), channel_id=1, source_target_pairs={{0,1},{1,0},{2,3},{3,2},{4,5},{5,4},{6,7},{7,6},{8,9},{9,8},{10,11... | collective-permute-start | bytes 3145736 | tf_op jit(solution)/shard_map/ppermute | solution.py:303
  597.4 30.6 %collective-permute-start.51 = (bf16[8,128,512]{2,1,0:T(8,128)(2,1)}, bf16[8,128,512]{2,1,0:T(8,128)(2,1)S(1)}, u32[]{:S(2)}, u32[]{:S(2)}) collective-permute-start(bf16[8,128,512]{2,1,0:T(8,128)(2,1)} %get-tuple-element.488), channel_id=1, source_target_pairs={{0,2},{1,3},{2,0},{3,1},{4,6},{5,7},{6,4},{7,5},{8,10},{9,11},{10,... | collective-permute-start | bytes 3145736 | tf_op jit(solution)/shard_map/ppermute | solution.py:303
  598.4 29.6 %collective-permute-start.52 = (bf16[8,128,512]{2,1,0:T(8,128)(2,1)}, bf16[8,128,512]{2,1,0:T(8,128)(2,1)S(1)}, u32[]{:S(2)}, u32[]{:S(2)}) collective-permute-start(bf16[8,128,512]{2,1,0:T(8,128)(2,1)} %get-tuple-element.489), channel_id=1, source_target_pairs={{0,1},{1,0},{2,3},{3,2},{4,5},{5,4},{6,7},{7,6},{8,9},{9,8},{10,11... | collective-permute-start | bytes 3145736 | tf_op jit(solution)/shard_map/ppermute | solution.py:303
  633.8 34.5 %collective-permute-start.55 = (bf16[8,32,2048]{2,1,0:T(8,128)(2,1)}, bf16[8,32,2048]{2,1,0:T(8,128)(2,1)}, u32[]{:S(2)}, u32[]{:S(2)}) collective-permute-start(bf16[8,32,2048]{2,1,0:T(8,128)(2,1)} %get-tuple-element.511), channel_id=1, source_target_pairs={{0,2},{1,3},{2,0},{3,1},{4,6},{5,7},{6,4},{7,5},{8,10},{9,11},{10,... | collective-permute-start | bytes 3145736 | tf_op jit(solution)/shard_map/ppermute | solution.py:303
  634.8 33.5 %collective-permute-start.56 = (bf16[8,32,2048]{2,1,0:T(8,128)(2,1)}, bf16[8,32,2048]{2,1,0:T(8,128)(2,1)}, u32[]{:S(2)}, u32[]{:S(2)}) collective-permute-start(bf16[8,32,2048]{2,1,0:T(8,128)(2,1)} %get-tuple-element.512), channel_id=1, source_target_pairs={{0,1},{1,0},{2,3},{3,2},{4,5},{5,4},{6,7},{7,6},{8,9},{9,8},{10,11... | collective-permute-start | bytes 3145736 | tf_op jit(solution)/shard_map/ppermute | solution.py:303
  635.4 32.9 %collective-permute-start.57 = (bf16[512,1024]{1,0:T(8,128)(2,1)}, bf16[512,1024]{1,0:T(8,128)(2,1)}, u32[]{:S(2)}, u32[]{:S(2)}) collective-permute-start(bf16[512,1024]{1,0:T(8,128)(2,1)} %half_away.17), channel_id=1, source_target_pairs={{0,16},{1,17},{2,18},{3,19},{4,20},{5,21},{6,22},{7,23},{8,24},{9,... | collective-permute-start | bytes 3145736 | tf_op jit(solution)/shard_map/ppermute | solution.py:303
  635.4 32.9 %collective-permute-start.53 = (bf16[4,128,512]{2,1,0:T(8,128)(2,1)}, bf16[4,128,512]{2,1,0:T(8,128)(2,1)}, u32[]{:S(2)}, u32[]{:S(2)}) collective-permute-start(bf16[4,128,512]{2,1,0:T(8,128)(2,1)} %get-tuple-element.509), channel_id=1, source_target_pairs={{0,1},{1,0},{2,3},{3,2},{4,5},{5,4},{6,7},{7,6},{8,9},{9,8},{10,11... | collective-permute-start | bytes 1572872 | tf_op jit(solution)/shard_map/ppermute | solution.py:303
  636.9 31.4 %collective-permute-start.54 = (bf16[4,128,512]{2,1,0:T(8,128)(2,1)}, bf16[4,128,512]{2,1,0:T(8,128)(2,1)}, u32[]{:S(2)}, u32[]{:S(2)}) collective-permute-start(bf16[4,128,512]{2,1,0:T(8,128)(2,1)} %get-tuple-element.510), channel_id=1, source_target_pairs={{0,2},{1,3},{2,0},{3,1},{4,6},{5,7},{6,4},{7,5},{8,10},{9,11},{10,... | collective-permute-start | bytes 1572872 | tf_op jit(solution)/shard_map/ppermute | solution.py:303
  (152 other events, 1959.0 us)
Sparse Core Ops, SparseCore 0:
  10.9 119.4 all-gather.3
  133.3 90.3 all-gather.5
  226.5 91.9 all-gather.7

commit v4 on v3

--- a/solution.py
+++ b/solution.py
@@ -698,7 +698,7 @@
 
 def add_split(kepts, values, bits):
     blocks = kepts[0].shape[0]
-    part = math.gcd(blocks // 2, 4)
+    part = math.gcd(blocks // 2, 2)
     specs, operands, out_specs, out_shapes = [], [], [], []
     for place, (kept, value) in enumerate(zip(kepts, values)):
         unused, rows, cols = kept.shape
@@ -1112,9 +1112,9 @@
     (c_hidden,) = ended([c_d], c_hidden)
     started([c_d])
     c_normed_two = rms_scale(c_hidden, code_gains[1]).astype(low)
-    (c_normed_two,) = ended([c_d], c_normed_two)
+    c_act, c_slope = gelu_and_slope(times(c_normed_two, c_up) + code_gains[2])
+    c_act, c_slope = ended([c_d], c_act, c_slope)
     ((c_down,),) = c_d.whole
-    c_act, c_slope = gelu_and_slope(times(c_normed_two, c_up) + code_gains[2])
 
     def both(exchange):
         return [summed([(exchange, (True, False))], sizes)]

time: 816 us -> 814 us (level)
  transfers between devices with their start and end apart: 82 -> 82, of which waited for: 34 -> 33; matrix products, arithmetic and copies ran while one was open for 14% -> 16% of each run, Pallas kernels for 30% -> 30%
where the time goes in v4:
time: 814 us; the launch traced here: 804 us
  Pallas kernels  317 us (39%)
  waiting for transfers between devices  215 us (26%)
  starting transfers between devices  104 us (13%)
  matrix products  87.9 us (11%)
  other arithmetic  39.2 us (5%)
  local copies, waits for them, and re-layouts  25.2 us (3%)
  between operations  15.2 us (2%)
    ppermute x79, waiting for transfers between devices, swap(): lax.ppermute(value, ('gx', 'gy'), [(place, place ^ mask) for place in ran...  213 us
    ppermute x79, starting transfers between devices, swap(): lax.ppermute(value, ('gx', 'gy'), [(place, place ^ mask) for place in ran...  104 us
    dot_general x10, matrix products, times(): return jnp.dot(left, right, preferred_element_type=jnp.float32)  66.8 us
    pallas_call x15, Pallas kernels, merged(): pl.pallas_call(merge_kernel, grid_spec=pltpu.PrefetchScalarGridSpec(num_s...  66.2 us
    pallas_call x10, Pallas kernels, split_product(): pl.pallas_call(functools.partial(split_kernel, flips), grid_spec=pltpu.Pr...  61.7 us
    pallas_call x10, Pallas kernels, half_product(): pl.pallas_call(half_kernel if received is None else half_add_kernel, grid...  45.4 us
    pallas_call x12, Pallas kernels, add_split(): pl.pallas_call(add_split_kernel, grid_spec=pltpu.PrefetchScalarGridSpec(n...  37.1 us
    dot_general x6, matrix products, against(): lax.dot_general(left, right, (((1,), (1,)), ((), ())), preferred_element_...  21.1 us
  transfers between devices with their start and end apart: 82, of which 33 were waited for; matrix products, arithmetic and copies ran while one was open for 16% of the time, Pallas kernels for 30%

profile of v4, /device:TPU:0, one launch (start us, length us, event | category | flops | bytes accessed | tf_op | source)
XLA Modules:
  0.0 803.7 jit_solution(1259508092112319917)
XLA Ops:
  17.0 10.2 %collective-permute-done.refs_1_ = bf16[2,32,2176]{2,1,0:T(8,128)(2,1)S(1)} collective-permute-done((bf16[2,32,2176]{2,1,0:T(8,128)(2,1)S(1)}, bf16[2,32,2176]{2,1,0:T(8,128)(2,1)S(1)}, u32[]{:S(2)}, u32[]{:S(2)}) %collective-permute-start) | collective-permute-done | bytes 278560 | tf_op jit(solution)/shard_map/ppermute | solution.py:303
  27.2 12.7 %collective-permute-done.1.refs_2_ = bf16[2,32,2176]{2,1,0:T(8,128)(2,1)S(1)} collective-permute-done((bf16[2,32,2176]{2,1,0:T(8,128)(2,1)S(1)}, bf16[2,32,2176]{2,1,0:T(8,128)(2,1)S(1)}, u32[]{:S(2)}, u32[]{:S(2)}) %collective-permute-start.1) | collective-permute-done | bytes 278560 | tf_op jit(solution)/shard_map/ppermute | solution.py:303
  47.3 12.1 %collective-permute-done.3.theirs_ref = bf16[4,32,2176]{2,1,0:T(8,128)(2,1)S(1)} collective-permute-done((bf16[4,32,2176]{2,1,0:T(8,128)(2,1)S(1)}, bf16[4,32,2176]{2,1,0:T(8,128)(2,1)S(1)}, u32[]{:S(2)}, u32[]{:S(2)}) %collective-permute-start.3) | collective-permute-done | bytes 557088 | tf_op jit(solution)/shard_map/ppermute | solution.py:303
  74.6 8.9 %collective-permute-start.7 = (bf16[2,32,2048]{2,1,0:T(8,128)(2,1)S(1)}, bf16[2,32,2048]{2,1,0:T(8,128)(2,1)S(1)}, u32[]{:S(2)}, u32[]{:S(2)}) collective-permute-start(bf16[2,32,2048]{2,1,0:T(8,128)(2,1)S(1)} %pad_maximum_fusion.1.refs_0_), channel_id=1, source_target_pairs={{0,4},{1,5},{2,6},{3,7},{4,0},{5,1},{6,2},{7,3},{8,12},{9,13},{10,... | collective-permute-start | bytes 786440 | tf_op jit(solution)/shard_map/ppermute | solution.py:303
  86.1 19.5 %collective-permute-done.7.refs_1_ = bf16[2,32,2048]{2,1,0:T(8,128)(2,1)S(1)} collective-permute-done((bf16[2,32,2048]{2,1,0:T(8,128)(2,1)S(1)}, bf16[2,32,2048]{2,1,0:T(8,128)(2,1)S(1)}, u32[]{:S(2)}, u32[]{:S(2)}) %collective-permute-start.7) | collective-permute-done | bytes 262176 | tf_op jit(solution)/shard_map/ppermute | solution.py:303
  107.0 13.4 %collective-permute-done.9.refs_3_ = bf16[2,32,2048]{2,1,0:T(8,128)(2,1)S(1)} collective-permute-done((bf16[2,32,2048]{2,1,0:T(8,128)(2,1)S(1)}, bf16[2,32,2048]{2,1,0:T(8,128)(2,1)S(1)}, u32[]{:S(2)}, u32[]{:S(2)}) %collective-permute-start.9) | collective-permute-done | bytes 262176 | tf_op jit(solution)/shard_map/ppermute | solution.py:303
  137.3 8.7 %collective-permute-start.16 = (bf16[1,128,1024]{2,1,0:T(8,128)(2,1)S(1)}, bf16[1,128,1024]{2,1,0:T(8,128)(2,1)}, u32[]{:S(2)}, u32[]{:S(2)}) collective-permute-start(bf16[1,128,1024]{2,1,0:T(8,128)(2,1)S(1)} %bitcast.356), channel_id=1, source_target_pairs={{0,4},{1,5},{2,6},{3,7},{4,0},{5,1},{6,2},{7,3},{8,12},{9,13},{10,... | collective-permute-start | bytes 786440 | tf_op jit(solution)/shard_map/ppermute | solution.py:303
  187.3 7.7 frame_attend.1.acts_ref
  222.0 20.1 %collective-permute-done.21.theirs_ref = bf16[4,128,1024]{2,1,0:T(8,128)(2,1)S(1)} collective-permute-done((bf16[4,128,1024]{2,1,0:T(8,128)(2,1)}, bf16[4,128,1024]{2,1,0:T(8,128)(2,1)S(1)}, u32[]{:S(2)}, u32[]{:S(2)}) %collective-permute-start.21) | collective-permute-done | bytes 1048608 | tf_op jit(solution)/shard_map/ppermute | solution.py:303
  255.8 9.2 %add_convert_fusion.1 = (bf16[256,4096]{1,0:T(8,128)(2,1)}, bf16[256,4096]{1,0:T(8,128)(2,1)S(1)}) fusion(f32[4096]{0:T(1024)S(1)} %get-tuple-element.657, bf16[256,1024]{1,0:T(8,128)(2,1)} %multiply_convert_fusion.3.acts_ref, bf16[1024,4096]{1,0:T(8,128)(2,1)} %all-gather.4.cloned.1.call-done.weight_ref), kind=kOutput, calls=%fused_computation.8 | convolution fusion | flops 2164260864 | bytes 13123584 | tf_op jit(solution)/shard_map/dot_general | solution.py:908
  294.4 17.6 %collective-permute-done.22 = bf16[8,128,1024]{2,1,0:T(8,128)(2,1)} collective-permute-done((bf16[8,128,1024]{2,1,0:T(8,128)(2,1)}, bf16[8,128,1024]{2,1,0:T(8,128)(2,1)}, u32[]{:S(2)}, u32[]{:S(2)}) %collective-permute-start.22) | collective-permute-done | bytes 2097184 | tf_op jit(solution)/shard_map/ppermute | solution.py:303
  319.1 16.9 %add_convert_fusion = (bf16[768,4096]{1,0:T(8,128)(2,1)}, bf16[768,4096]{1,0:T(8,128)(2,1)}) fusion(f32[4096]{0:T(1024)S(1)} %get-tuple-element.656, bf16[768,1024]{1,0:T(8,128)(2,1)} %multiply_convert_fusion.acts_ref, bf16[1024,4096]{1,0:T(8,128)(2,1)} %all-gather.8.cloned.1.call-done.weight_ref), kind=kOutput, calls=%fused_computation | convolution fusion | flops 6492782592 | bytes 22560768 | tf_op jit(solution)/shard_map/dot_general | solution.py:908
  350.9 9.6 %split_product.10 = (bf16[8,128,512]{2,1,0:T(8,128)(2,1)}, bf16[8,128,512]{2,1,0:T(8,128)(2,1)}, bf16[8,128,512]{2,1,0:T(8,128)(2,1)}, bf16[8,128,512]{2,1,0:T(8,128)(2,1)}) custom-call(s32[3]{0:T(128)} %add_add_fusion.6.side_ref, bf16[768,4096]{1,0:T(8,128)(2,1)} %get-tuple-element.516.acts_ref, bf16[768,1024]{1,0:T(8,128)(2,1)} %bitcast.226, ...), custom_call_target="tpu_custom_call" | custom-call | flops 1 | bytes 1 | tf_op jit(solution)/shard_map/split_product/pallas_call | solution.py:676
  371.6 13.1 %grad_pre.2 = (bf16[768,4096]{1,0:T(8,128)(2,1)}, f32[1,4096]{1,0:T(1,128)}) custom-call(bf16[768,1024]{1,0:T(8,128)(2,1)} %bitcast.228, bf16[4096,1024]{1,0:T(8,128)(2,1)} %bitcast.231, bf16[768,4096]{1,0:T(8,128)(2,1)} %get-tuple-element.370.slope_ref), custom_call_target="tpu_custom_call" | custom-call | flops 1 | bytes 1 | tf_op jit(solution)/shard_map/grad_pre/pallas_call | solution.py:958
  399.0 12.8 %grad_two.2 = f32[768,1024]{1,0:T(8,128)} custom-call(bf16[768,4096]{1,0:T(8,128)(2,1)} %get-tuple-element.384.grad_ref.refs_0_.refs_2_, bf16[1024,4096]{1,0:T(8,128)(2,1)} %all-gather.8.cloned.1.call-done.weight_ref), custom_call_target="tpu_custom_call" | custom-call | flops 1 | bytes 1 | tf_op jit(solution)/shard_map/grad_two/pallas_call | solution.py:940
  421.3 10.0 %split_product.11 = (bf16[8,32,2048]{2,1,0:T(8,128)(2,1)}, bf16[8,32,2048]{2,1,0:T(8,128)(2,1)}, bf16[8,32,2048]{2,1,0:T(8,128)(2,1)}, bf16[8,32,2048]{2,1,0:T(8,128)(2,1)}) custom-call(s32[3]{0:T(128)} %add_add_fusion.6.side_ref, bf16[768,1024]{1,0:T(8,128)(2,1)} %multiply_convert_fusion.acts_ref, ...), custom_call_target="tpu_custom_call" | custom-call | flops 1 | bytes 1 | tf_op jit(solution)/shard_map/split_product/pallas_call | solution.py:676
  452.6 11.4 %code_attend_back.1 = (bf16[3,256,2048]{2,1,0:T(8,128)(2,1)}, bf16[3,256,1024]{2,1,0:T(8,128)(2,1)}) custom-call(bf16[3,256,2048]{2,1,0:T(8,128)(2,1)} %bitcast.239, bf16[3,256,1024]{2,1,0:T(8,128)(2,1)} %bitcast.261, bf16[3,256,1024]{2,1,0:T(8,128)(2,1)} %bitcast.350, bf16[1024,128]{1,0:T(8,128)(2,1)} %fusion.16.marks_ref), custom_call_target="tpu_custom_call" | custom-call | flops 1 | bytes 1 | tf_op jit(solution)/shard_map/code_attend_back/pallas_call | solution.py:156
  539.4 7.8 grad_pre.3
  612.0 12.4 %frame_attend_back.1 = (bf16[256,2048]{1,0:T(8,128)(2,1)}, bf16[256,1024]{1,0:T(8,128)(2,1)}) custom-call(bf16[256,2048]{1,0:T(8,128)(2,1)} %convolution_convert_fusion.1.query_ref.keys_ref, bf16[256,2048]{1,0:T(8,128)(2,1)} %convolution_convert_fusion.1.query_ref.keys_ref, bf16[256,1024]{1,0:T(8,128)(2,1)} %convolution_convert_fusion.5.values_ref, ...), custom_call_target="tpu_custom_call" | custom-call | flops 1 | bytes 1 | tf_op jit(solution)/shard_map/frame_attend_back/pallas_call | solution.py:267
  634.0 12.3 %add_add_fusion.2 = bf16[768,1024]{1,0:T(8,128)(2,1)} fusion(f32[768,1024]{1,0:T(8,128)S(1)} %copy-done.4, bf16[768,4096]{1,0:T(8,128)(2,1)} %get-tuple-element.516.acts_ref, bf16[4096,1024]{1,0:T(8,128)(2,1)} %bitcast.232, f32[1024]{0:T(1024)S(1)} %add.487), kind=kOutput, calls=%fused_computation.23 | convolution fusion | flops 6444810240 | bytes 19402752 | tf_op jit(solution)/shard_map/dot_general | solution.py:908
  652.0 12.5 %collective-permute-done.53.refs_2_ = bf16[4,128,512]{2,1,0:T(8,128)(2,1)} collective-permute-done((bf16[4,128,512]{2,1,0:T(8,128)(2,1)}, bf16[4,128,512]{2,1,0:T(8,128)(2,1)}, u32[]{:S(2)}, u32[]{:S(2)}) %collective-permute-start.53) | collective-permute-done | bytes 524320 | tf_op jit(solution)/shard_map/ppermute | solution.py:303
  685.0 8.1 %collective-permute-done.58 = bf16[2,128,1024]{2,1,0:T(8,128)(2,1)S(1)} collective-permute-done((bf16[2,128,1024]{2,1,0:T(8,128)(2,1)}, bf16[2,128,1024]{2,1,0:T(8,128)(2,1)S(1)}, u32[]{:S(2)}, u32[]{:S(2)}) %collective-permute-start.58) | collective-permute-done | bytes 524320 | tf_op jit(solution)/shard_map/ppermute | solution.py:303
  727.5 17.5 %collective-permute-done.70 = f32[8,448]{1,0:T(8,128)S(1)} collective-permute-done((f32[8,448]{1,0:T(8,128)S(1)}, f32[8,448]{1,0:T(8,128)S(1)}, u32[]{:S(2)}, u32[]{:S(2)}) %collective-permute-start.70) | collective-permute-done | bytes 14368 | tf_op jit(solution)/shard_map/ppermute | solution.py:303
  784.5 9.3 %collective-permute-done.77 = bf16[1,32,4096]{2,1,0:T(8,128)(2,1)S(1)} collective-permute-done((bf16[1,32,4096]{2,1,0:T(8,128)(2,1)}, bf16[1,32,4096]{2,1,0:T(8,128)(2,1)S(1)}, u32[]{:S(2)}, u32[]{:S(2)}) %collective-permute-start.77) | collective-permute-done | bytes 262176 | tf_op jit(solution)/shard_map/ppermute | solution.py:303
  (501 shorter events, 494.7 us)
Async XLA Ops:
  7.2 248.6 %all-gather.4.cloned.1.call-start = ((), (), s32[]{:S(2)}) async-start(), calls=%async_computation | async-start | bytes 8650752 | tf_op jit(solution)/shard_map/all_gather | solution.py:1051
  7.9 257.0 %all-gather.6.cloned.1.call-start = ((), (), s32[]{:S(2)}) async-start(), calls=%async_computation.1 | async-start | bytes 8650752 | tf_op jit(solution)/shard_map/all_gather | solution.py:1051
  8.7 310.4 %all-gather.8.cloned.1.call-start = ((), (), s32[]{:S(2)}) async-start(), calls=%async_computation.2 | async-start | bytes 8650752 | tf_op jit(solution)/shard_map/all_gather | solution.py:1051
  68.5 51.9 %collective-permute-start.6 = (bf16[8,32,2176]{2,1,0:T(8,128)(2,1)}, bf16[8,32,2176]{2,1,0:T(8,128)(2,1)S(1)}, u32[]{:S(2)}, u32[]{:S(2)}) collective-permute-start(bf16[8,32,2176]{2,1,0:T(8,128)(2,1)} %bitcast.262), channel_id=1, source_target_pairs={{0,2},{1,3},{2,0},{3,1},{4,6},{5,7},{6,4},{7,5},{8,10},{9,11},{10,... | collective-permute-start | bytes 3342344 | tf_op jit(solution)/shard_map/ppermute | solution.py:303
  72.0 48.5 %collective-permute-start.5 = (bf16[8,32,2176]{2,1,0:T(8,128)(2,1)}, bf16[8,32,2176]{2,1,0:T(8,128)(2,1)S(1)}, u32[]{:S(2)}, u32[]{:S(2)}) collective-permute-start(bf16[8,32,2176]{2,1,0:T(8,128)(2,1)} %bitcast.264), channel_id=1, source_target_pairs={{0,1},{1,0},{2,3},{3,2},{4,5},{5,4},{6,7},{7,6},{8,9},{9,8},{10,11... | collective-permute-start | bytes 3342344 | tf_op jit(solution)/shard_map/ppermute | solution.py:303
  74.6 31.0 %collective-permute-start.7 = (bf16[2,32,2048]{2,1,0:T(8,128)(2,1)S(1)}, bf16[2,32,2048]{2,1,0:T(8,128)(2,1)S(1)}, u32[]{:S(2)}, u32[]{:S(2)}) collective-permute-start(bf16[2,32,2048]{2,1,0:T(8,128)(2,1)S(1)} %pad_maximum_fusion.1.refs_0_), channel_id=1, source_target_pairs={{0,4},{1,5},{2,6},{3,7},{4,0},{5,1},{6,2},{7,3},{8,12},{9,13},{10,... | collective-permute-start | bytes 786440 | tf_op jit(solution)/shard_map/ppermute | solution.py:303
  84.7 35.7 %collective-permute-start.9 = (bf16[2,32,2048]{2,1,0:T(8,128)(2,1)S(1)}, bf16[2,32,2048]{2,1,0:T(8,128)(2,1)S(1)}, u32[]{:S(2)}, u32[]{:S(2)}) collective-permute-start(bf16[2,32,2048]{2,1,0:T(8,128)(2,1)S(1)} %pad_maximum_fusion.1.refs_0_), channel_id=1, source_target_pairs={{0,12},{1,13},{2,14},{3,15},{4,8},{5,9},{6,10},{7,11},{8,4},{9,5},... | collective-permute-start | bytes 786440 | tf_op jit(solution)/shard_map/ppermute | solution.py:303
  125.4 34.8 %collective-permute-start.11 = (bf16[16,32,2176]{2,1,0:T(8,128)(2,1)}, bf16[16,32,2176]{2,1,0:T(8,128)(2,1)}, u32[]{:S(2)}, u32[]{:S(2)}) collective-permute-start(bf16[16,32,2176]{2,1,0:T(8,128)(2,1)} %bitcast.247), channel_id=1, source_target_pairs={{0,16},{1,17},{2,18},{3,19},{4,20},{5,21},{6,22},{7,23},{8,24},{9,... | collective-permute-start | bytes 6684680 | tf_op jit(solution)/shard_map/ppermute | solution.py:303
  131.3 28.8 %collective-permute-start.10 = (bf16[16,32,2176]{2,1,0:T(8,128)(2,1)}, bf16[16,32,2176]{2,1,0:T(8,128)(2,1)}, u32[]{:S(2)}, u32[]{:S(2)}) collective-permute-start(bf16[16,32,2176]{2,1,0:T(8,128)(2,1)} %bitcast.245), channel_id=1, source_target_pairs={{0,16},{1,17},{2,18},{3,19},{4,20},{5,21},{6,22},{7,23},{8,24},{9,... | collective-permute-start | bytes 6684680 | tf_op jit(solution)/shard_map/ppermute | solution.py:303
  137.3 57.7 %collective-permute-start.16 = (bf16[1,128,1024]{2,1,0:T(8,128)(2,1)S(1)}, bf16[1,128,1024]{2,1,0:T(8,128)(2,1)}, u32[]{:S(2)}, u32[]{:S(2)}) collective-permute-start(bf16[1,128,1024]{2,1,0:T(8,128)(2,1)S(1)} %bitcast.356), channel_id=1, source_target_pairs={{0,4},{1,5},{2,6},{3,7},{4,0},{5,1},{6,2},{7,3},{8,12},{9,13},{10,... | collective-permute-start | bytes 786440 | tf_op jit(solution)/shard_map/ppermute | solution.py:303
  151.1 43.9 %collective-permute-start.17 = (bf16[1,128,1024]{2,1,0:T(8,128)(2,1)S(1)}, bf16[1,128,1024]{2,1,0:T(8,128)(2,1)}, u32[]{:S(2)}, u32[]{:S(2)}) collective-permute-start(bf16[1,128,1024]{2,1,0:T(8,128)(2,1)S(1)} %bitcast.357), channel_id=1, source_target_pairs={{0,8},{1,9},{2,10},{3,11},{4,12},{5,13},{6,14},{7,15},{8,0},{9,1},... | collective-permute-start | bytes 786440 | tf_op jit(solution)/shard_map/ppermute | solution.py:303
  158.6 36.4 %collective-permute-start.18 = (bf16[1,128,1024]{2,1,0:T(8,128)(2,1)S(1)}, bf16[1,128,1024]{2,1,0:T(8,128)(2,1)}, u32[]{:S(2)}, u32[]{:S(2)}) collective-permute-start(bf16[1,128,1024]{2,1,0:T(8,128)(2,1)S(1)} %bitcast.358), channel_id=1, source_target_pairs={{0,12},{1,13},{2,14},{3,15},{4,8},{5,9},{6,10},{7,11},{8,4},{9,5},... | collective-permute-start | bytes 786440 | tf_op jit(solution)/shard_map/ppermute | solution.py:303
  173.8 28.0 %collective-permute-start.14 = (bf16[8,32,2048]{2,1,0:T(8,128)(2,1)}, bf16[8,32,2048]{2,1,0:T(8,128)(2,1)}, u32[]{:S(2)}, u32[]{:S(2)}) collective-permute-start(bf16[8,32,2048]{2,1,0:T(8,128)(2,1)} %bitcast.302), channel_id=1, source_target_pairs={{0,1},{1,0},{2,3},{3,2},{4,5},{5,4},{6,7},{7,6},{8,9},{9,8},{10,11... | collective-permute-start | bytes 3145736 | tf_op jit(solution)/shard_map/ppermute | solution.py:303
  205.6 36.5 %collective-permute-start.20 = (bf16[16,32,2048]{2,1,0:T(8,128)(2,1)}, bf16[16,32,2048]{2,1,0:T(8,128)(2,1)}, u32[]{:S(2)}, u32[]{:S(2)}) collective-permute-start(bf16[16,32,2048]{2,1,0:T(8,128)(2,1)} %bitcast.249), channel_id=1, source_target_pairs={{0,16},{1,17},{2,18},{3,19},{4,20},{5,21},{6,22},{7,23},{8,24},{9,... | collective-permute-start | bytes 6291464 | tf_op jit(solution)/shard_map/ppermute | solution.py:303
  211.5 30.6 %collective-permute-start.19 = (bf16[16,32,2048]{2,1,0:T(8,128)(2,1)}, bf16[16,32,2048]{2,1,0:T(8,128)(2,1)}, u32[]{:S(2)}, u32[]{:S(2)}) collective-permute-start(bf16[16,32,2048]{2,1,0:T(8,128)(2,1)} %bitcast.251), channel_id=1, source_target_pairs={{0,16},{1,17},{2,18},{3,19},{4,20},{5,21},{6,22},{7,23},{8,24},{9,... | collective-permute-start | bytes 6291464 | tf_op jit(solution)/shard_map/ppermute | solution.py:303
  246.9 65.1 %collective-permute-start.22 = (bf16[8,128,1024]{2,1,0:T(8,128)(2,1)}, bf16[8,128,1024]{2,1,0:T(8,128)(2,1)}, u32[]{:S(2)}, u32[]{:S(2)}) collective-permute-start(bf16[8,128,1024]{2,1,0:T(8,128)(2,1)} %bitcast.253), channel_id=1, source_target_pairs={{0,2},{1,3},{2,0},{3,1},{4,6},{5,7},{6,4},{7,5},{8,10},{9,11},{10,... | collective-permute-start | bytes 6291464 | tf_op jit(solution)/shard_map/ppermute | solution.py:303
  360.6 31.8 %collective-permute-start.25 = (bf16[8,128,512]{2,1,0:T(8,128)(2,1)}, bf16[8,128,512]{2,1,0:T(8,128)(2,1)S(1)}, u32[]{:S(2)}, u32[]{:S(2)}) collective-permute-start(bf16[8,128,512]{2,1,0:T(8,128)(2,1)} %get-tuple-element.373), channel_id=1, source_target_pairs={{0,2},{1,3},{2,0},{3,1},{4,6},{5,7},{6,4},{7,5},{8,10},{9,11},{10,... | collective-permute-start | bytes 3145736 | tf_op jit(solution)/shard_map/ppermute | solution.py:303
  361.7 30.6 %collective-permute-start.26 = (bf16[8,128,512]{2,1,0:T(8,128)(2,1)}, bf16[8,128,512]{2,1,0:T(8,128)(2,1)S(1)}, u32[]{:S(2)}, u32[]{:S(2)}) collective-permute-start(bf16[8,128,512]{2,1,0:T(8,128)(2,1)} %get-tuple-element.374), channel_id=1, source_target_pairs={{0,1},{1,0},{2,3},{3,2},{4,5},{5,4},{6,7},{7,6},{8,9},{9,8},{10,11... | collective-permute-start | bytes 3145736 | tf_op jit(solution)/shard_map/ppermute | solution.py:303
  595.8 28.5 %collective-permute-start.51 = (bf16[8,128,512]{2,1,0:T(8,128)(2,1)}, bf16[8,128,512]{2,1,0:T(8,128)(2,1)S(1)}, u32[]{:S(2)}, u32[]{:S(2)}) collective-permute-start(bf16[8,128,512]{2,1,0:T(8,128)(2,1)} %get-tuple-element.490), channel_id=1, source_target_pairs={{0,2},{1,3},{2,0},{3,1},{4,6},{5,7},{6,4},{7,5},{8,10},{9,11},{10,... | collective-permute-start | bytes 3145736 | tf_op jit(solution)/shard_map/ppermute | solution.py:303
  629.9 34.5 %collective-permute-start.55 = (bf16[8,32,2048]{2,1,0:T(8,128)(2,1)}, bf16[8,32,2048]{2,1,0:T(8,128)(2,1)}, u32[]{:S(2)}, u32[]{:S(2)}) collective-permute-start(bf16[8,32,2048]{2,1,0:T(8,128)(2,1)} %get-tuple-element.513), channel_id=1, source_target_pairs={{0,2},{1,3},{2,0},{3,1},{4,6},{5,7},{6,4},{7,5},{8,10},{9,11},{10,... | collective-permute-start | bytes 3145736 | tf_op jit(solution)/shard_map/ppermute | solution.py:303
  630.9 33.5 %collective-permute-start.56 = (bf16[8,32,2048]{2,1,0:T(8,128)(2,1)}, bf16[8,32,2048]{2,1,0:T(8,128)(2,1)}, u32[]{:S(2)}, u32[]{:S(2)}) collective-permute-start(bf16[8,32,2048]{2,1,0:T(8,128)(2,1)} %get-tuple-element.514), channel_id=1, source_target_pairs={{0,1},{1,0},{2,3},{3,2},{4,5},{5,4},{6,7},{7,6},{8,9},{9,8},{10,11... | collective-permute-start | bytes 3145736 | tf_op jit(solution)/shard_map/ppermute | solution.py:303
  631.7 32.8 %collective-permute-start.57 = (bf16[512,1024]{1,0:T(8,128)(2,1)}, bf16[512,1024]{1,0:T(8,128)(2,1)}, u32[]{:S(2)}, u32[]{:S(2)}) collective-permute-start(bf16[512,1024]{1,0:T(8,128)(2,1)} %half_away.17), channel_id=1, source_target_pairs={{0,16},{1,17},{2,18},{3,19},{4,20},{5,21},{6,22},{7,23},{8,24},{9,... | collective-permute-start | bytes 3145736 | tf_op jit(solution)/shard_map/ppermute | solution.py:303
  631.7 32.8 %collective-permute-start.53 = (bf16[4,128,512]{2,1,0:T(8,128)(2,1)}, bf16[4,128,512]{2,1,0:T(8,128)(2,1)}, u32[]{:S(2)}, u32[]{:S(2)}) collective-permute-start(bf16[4,128,512]{2,1,0:T(8,128)(2,1)} %get-tuple-element.511), channel_id=1, source_target_pairs={{0,1},{1,0},{2,3},{3,2},{4,5},{5,4},{6,7},{7,6},{8,9},{9,8},{10,11... | collective-permute-start | bytes 1572872 | tf_op jit(solution)/shard_map/ppermute | solution.py:303
  633.0 31.5 %collective-permute-start.54 = (bf16[4,128,512]{2,1,0:T(8,128)(2,1)}, bf16[4,128,512]{2,1,0:T(8,128)(2,1)}, u32[]{:S(2)}, u32[]{:S(2)}) collective-permute-start(bf16[4,128,512]{2,1,0:T(8,128)(2,1)} %get-tuple-element.512), channel_id=1, source_target_pairs={{0,2},{1,3},{2,0},{3,1},{4,6},{5,7},{6,4},{7,5},{8,10},{9,11},{10,... | collective-permute-start | bytes 1572872 | tf_op jit(solution)/shard_map/ppermute | solution.py:303
  (152 other events, 1968.0 us)
Sparse Core Ops, SparseCore 0:
  10.9 120.1 all-gather.3
  133.9 90.2 all-gather.5
  227.1 91.9 all-gather.7

commit v5 on v4

--- a/solution.py
+++ b/solution.py
@@ -1131,7 +1131,7 @@
     c_d_core = Core(c_act, grad_low, sizes)
     c_slope, grad_low = scatter_round([], [c_d_core], c_slope, grad_low)
     c_grad_b_down = jnp.sum(grad_low.astype(jnp.float32), axis=0)
-    (c_grad_b_down,) = ended([c_d_core], c_grad_b_down)
+    c_grad_b_down, c_down = ended([c_d_core], c_grad_b_down, c_down)
     c_d_chain = both(c_d_core)
     c_slope, grad_low = scatter_round([], c_d_chain, c_slope, grad_low)
     grad_pre, c_grad_b_up = grad_pre_of(grad_low, c_down, c_slope)

time: 814 us -> 811 us (level)
  starting transfers between devices: 104 us -> 80.4 us
  waiting for transfers between devices: 215 us -> 232 us
    ppermute x79, starting transfers between devices: 104 us -> 80.3 us  [swap(): lax.ppermute(value, ('gx', 'gy'), [(place, place ^ mask) for place in ran...]
    ppermute x79, waiting for transfers between devices: 213 us -> 223 us  [swap(): lax.ppermute(value, ('gx', 'gy'), [(place, place ^ mask) for place in ran...]
  transfers between devices with their start and end apart: 82 -> 82, of which waited for: 33 -> 35; matrix products, arithmetic and copies ran while one was open for 16% -> 17% of each run, Pallas kernels for 30% -> 29%
where the time goes in v5:
time: 811 us; the launch traced here: 801 us
  Pallas kernels  316 us (39%)
  waiting for transfers between devices  232 us (29%)
  matrix products  89 us (11%)
  starting transfers between devices  80.4 us (10%)
  other arithmetic  45.7 us (6%)
  local copies, waits for them, and re-layouts  21.9 us (3%)
  between operations  15.2 us (2%)
    ppermute x79, waiting for transfers between devices, swap(): lax.ppermute(value, ('gx', 'gy'), [(place, place ^ mask) for place in ran...  223 us
    ppermute x79, starting transfers between devices, swap(): lax.ppermute(value, ('gx', 'gy'), [(place, place ^ mask) for place in ran...  80.3 us
    dot_general x10, matrix products, times(): return jnp.dot(left, right, preferred_element_type=jnp.float32)  66.8 us
    pallas_call x15, Pallas kernels, merged(): pl.pallas_call(merge_kernel, grid_spec=pltpu.PrefetchScalarGridSpec(num_s...  66.1 us
    pallas_call x10, Pallas kernels, split_product(): pl.pallas_call(functools.partial(split_kernel, flips), grid_spec=pltpu.Pr...  62 us
    pallas_call x10, Pallas kernels, half_product(): pl.pallas_call(half_kernel if received is None else half_add_kernel, grid...  45.4 us
    pallas_call x12, Pallas kernels, add_split(): pl.pallas_call(add_split_kernel, grid_spec=pltpu.PrefetchScalarGridSpec(n...  36.5 us
    dot_general x6, matrix products, against(): lax.dot_general(left, right, (((1,), (1,)), ((), ())), preferred_element_...  22.2 us
  transfers between devices with their start and end apart: 82, of which 35 were waited for; matrix products, arithmetic and copies ran while one was open for 17% of the time, Pallas kernels for 29%

profile of v5, /device:TPU:0, one launch (start us, length us, event | category | flops | bytes accessed | tf_op | source)
XLA Modules:
  0.0 800.9 jit_solution(3943710917989358245)
XLA Ops:
  24.1 21.6 %collective-permute-done.1.refs_2_ = bf16[2,32,2176]{2,1,0:T(8,128)(2,1)S(1)} collective-permute-done((bf16[2,32,2176]{2,1,0:T(8,128)(2,1)S(1)}, bf16[2,32,2176]{2,1,0:T(8,128)(2,1)S(1)}, u32[]{:S(2)}, u32[]{:S(2)}) %collective-permute-start.1) | collective-permute-done | bytes 278560 | tf_op jit(solution)/shard_map/ppermute | solution.py:303
  53.2 14.6 %collective-permute-done.4.theirs_ref = bf16[4,32,2176]{2,1,0:T(8,128)(2,1)S(1)} collective-permute-done((bf16[4,32,2176]{2,1,0:T(8,128)(2,1)S(1)}, bf16[4,32,2176]{2,1,0:T(8,128)(2,1)S(1)}, u32[]{:S(2)}, u32[]{:S(2)}) %collective-permute-start.4) | collective-permute-done | bytes 557088 | tf_op jit(solution)/shard_map/ppermute | solution.py:303
  82.2 12.1 %collective-permute-done.9.refs_3_ = bf16[2,32,2048]{2,1,0:T(8,128)(2,1)S(1)} collective-permute-done((bf16[2,32,2048]{2,1,0:T(8,128)(2,1)S(1)}, bf16[2,32,2048]{2,1,0:T(8,128)(2,1)S(1)}, u32[]{:S(2)}, u32[]{:S(2)}) %collective-permute-start.9) | collective-permute-done | bytes 262176 | tf_op jit(solution)/shard_map/ppermute | solution.py:303
  94.3 26.7 %collective-permute-done.8.refs_2_ = bf16[2,32,2048]{2,1,0:T(8,128)(2,1)S(1)} collective-permute-done((bf16[2,32,2048]{2,1,0:T(8,128)(2,1)S(1)}, bf16[2,32,2048]{2,1,0:T(8,128)(2,1)S(1)}, u32[]{:S(2)}, u32[]{:S(2)}) %collective-permute-start.8) | collective-permute-done | bytes 262176 | tf_op jit(solution)/shard_map/ppermute | solution.py:303
  141.2 8.6 %collective-permute-done.13.theirs_ref = bf16[4,32,2048]{2,1,0:T(8,128)(2,1)S(1)} collective-permute-done((bf16[4,32,2048]{2,1,0:T(8,128)(2,1)S(1)}, bf16[4,32,2048]{2,1,0:T(8,128)(2,1)S(1)}, u32[]{:S(2)}, u32[]{:S(2)}) %collective-permute-start.13) | collective-permute-done | bytes 524320 | tf_op jit(solution)/shard_map/ppermute | solution.py:303
  179.5 7.8 frame_attend.1.acts_ref
  211.6 21.6 %collective-permute-done.21.theirs_ref = bf16[4,128,1024]{2,1,0:T(8,128)(2,1)S(1)} collective-permute-done((bf16[4,128,1024]{2,1,0:T(8,128)(2,1)}, bf16[4,128,1024]{2,1,0:T(8,128)(2,1)S(1)}, u32[]{:S(2)}, u32[]{:S(2)}) %collective-permute-start.21) | collective-permute-done | bytes 1048608 | tf_op jit(solution)/shard_map/ppermute | solution.py:303
  246.8 9.2 %add_convert_fusion.1 = (bf16[256,4096]{1,0:T(8,128)(2,1)}, bf16[256,4096]{1,0:T(8,128)(2,1)S(1)}) fusion(f32[4096]{0:T(1024)S(1)} %get-tuple-element.659, bf16[256,1024]{1,0:T(8,128)(2,1)} %multiply_convert_fusion.3.acts_ref, bf16[1024,4096]{1,0:T(8,128)(2,1)} %all-gather.4.cloned.1.call-done.weight_ref), kind=kOutput, calls=%fused_computation.8 | convolution fusion | flops 2164260864 | bytes 13123584 | tf_op jit(solution)/shard_map/dot_general | solution.py:908
  285.5 17.0 %collective-permute-done.22 = bf16[8,128,1024]{2,1,0:T(8,128)(2,1)} collective-permute-done((bf16[8,128,1024]{2,1,0:T(8,128)(2,1)}, bf16[8,128,1024]{2,1,0:T(8,128)(2,1)}, u32[]{:S(2)}, u32[]{:S(2)}) %collective-permute-start.22) | collective-permute-done | bytes 2097184 | tf_op jit(solution)/shard_map/ppermute | solution.py:303
  316.1 16.9 %add_convert_fusion = (bf16[768,4096]{1,0:T(8,128)(2,1)}, bf16[768,4096]{1,0:T(8,128)(2,1)}) fusion(f32[4096]{0:T(1024)S(1)} %get-tuple-element.658, bf16[768,1024]{1,0:T(8,128)(2,1)} %multiply_convert_fusion.acts_ref, bf16[1024,4096]{1,0:T(8,128)(2,1)} %all-gather.8.cloned.1.call-done.weight_ref), kind=kOutput, calls=%fused_computation | convolution fusion | flops 6492782592 | bytes 22560768 | tf_op jit(solution)/shard_map/dot_general | solution.py:908
  348.6 9.6 %split_product.10 = (bf16[8,128,512]{2,1,0:T(8,128)(2,1)}, bf16[8,128,512]{2,1,0:T(8,128)(2,1)}, bf16[8,128,512]{2,1,0:T(8,128)(2,1)}, bf16[8,128,512]{2,1,0:T(8,128)(2,1)}) custom-call(s32[3]{0:T(128)} %add_add_fusion.6.side_ref, bf16[768,4096]{1,0:T(8,128)(2,1)} %get-tuple-element.518.acts_ref, bf16[768,1024]{1,0:T(8,128)(2,1)} %bitcast.226, ...), custom_call_target="tpu_custom_call" | custom-call | flops 1 | bytes 1 | tf_op jit(solution)/shard_map/split_product/pallas_call | solution.py:676
  361.2 13.2 %grad_pre.2 = (bf16[768,4096]{1,0:T(8,128)(2,1)}, f32[1,4096]{1,0:T(1,128)}) custom-call(bf16[768,1024]{1,0:T(8,128)(2,1)} %bitcast.228, bf16[4096,1024]{1,0:T(8,128)(2,1)} %bitcast.231, bf16[768,4096]{1,0:T(8,128)(2,1)} %get-tuple-element.372.slope_ref), custom_call_target="tpu_custom_call" | custom-call | flops 1 | bytes 1 | tf_op jit(solution)/shard_map/grad_pre/pallas_call | solution.py:958
  374.4 7.6 half_away.11
  391.6 12.5 %grad_two.2 = f32[768,1024]{1,0:T(8,128)} custom-call(bf16[768,4096]{1,0:T(8,128)(2,1)} %get-tuple-element.386.grad_ref.refs_0_.refs_2_, bf16[1024,4096]{1,0:T(8,128)(2,1)} %all-gather.8.cloned.1.call-done.weight_ref), custom_call_target="tpu_custom_call" | custom-call | flops 1 | bytes 1 | tf_op jit(solution)/shard_map/grad_two/pallas_call | solution.py:940
  406.5 10.2 %split_product.11 = (bf16[8,32,2048]{2,1,0:T(8,128)(2,1)}, bf16[8,32,2048]{2,1,0:T(8,128)(2,1)}, bf16[8,32,2048]{2,1,0:T(8,128)(2,1)}, bf16[8,32,2048]{2,1,0:T(8,128)(2,1)}) custom-call(s32[3]{0:T(128)} %add_add_fusion.6.side_ref, bf16[768,1024]{1,0:T(8,128)(2,1)} %multiply_convert_fusion.acts_ref, ...), custom_call_target="tpu_custom_call" | custom-call | flops 1 | bytes 1 | tf_op jit(solution)/shard_map/split_product/pallas_call | solution.py:676
  427.7 9.0 %collective-permute-done.30 = bf16[2,128,1024]{2,1,0:T(8,128)(2,1)} collective-permute-done((bf16[2,128,1024]{2,1,0:T(8,128)(2,1)S(1)}, bf16[2,128,1024]{2,1,0:T(8,128)(2,1)}, u32[]{:S(2)}, u32[]{:S(2)}) %collective-permute-start.30) | collective-permute-done | bytes 524320 | tf_op jit(solution)/shard_map/ppermute | solution.py:303
  452.1 11.4 %code_attend_back.1 = (bf16[3,256,2048]{2,1,0:T(8,128)(2,1)}, bf16[3,256,1024]{2,1,0:T(8,128)(2,1)}) custom-call(bf16[3,256,2048]{2,1,0:T(8,128)(2,1)} %bitcast.239, bf16[3,256,1024]{2,1,0:T(8,128)(2,1)} %bitcast.261, bf16[3,256,1024]{2,1,0:T(8,128)(2,1)} %bitcast.334, bf16[1024,128]{1,0:T(8,128)(2,1)} %fusion.16.marks_ref), custom_call_target="tpu_custom_call" | custom-call | flops 1 | bytes 1 | tf_op jit(solution)/shard_map/code_attend_back/pallas_call | solution.py:156
  537.2 7.9 grad_pre.3
  596.0 7.5 split_product.16
  611.0 12.4 %frame_attend_back.1 = (bf16[256,2048]{1,0:T(8,128)(2,1)}, bf16[256,1024]{1,0:T(8,128)(2,1)}) custom-call(bf16[256,2048]{1,0:T(8,128)(2,1)} %convolution_convert_fusion.1.query_ref.keys_ref, bf16[256,2048]{1,0:T(8,128)(2,1)} %convolution_convert_fusion.1.query_ref.keys_ref, bf16[256,1024]{1,0:T(8,128)(2,1)} %convolution_convert_fusion.5.values_ref, ...), custom_call_target="tpu_custom_call" | custom-call | flops 1 | bytes 1 | tf_op jit(solution)/shard_map/frame_attend_back/pallas_call | solution.py:267
  631.6 12.3 %add_add_fusion.2 = bf16[768,1024]{1,0:T(8,128)(2,1)} fusion(f32[768,1024]{1,0:T(8,128)S(1)} %copy-done.3, bf16[768,4096]{1,0:T(8,128)(2,1)} %get-tuple-element.518.acts_ref, bf16[4096,1024]{1,0:T(8,128)(2,1)} %bitcast.232, f32[1024]{0:T(1024)S(1)} %add.487), kind=kOutput, calls=%fused_computation.23 | convolution fusion | flops 6444810240 | bytes 19402752 | tf_op jit(solution)/shard_map/dot_general | solution.py:908
  649.5 12.2 %collective-permute-done.55 = bf16[8,32,2048]{2,1,0:T(8,128)(2,1)} collective-permute-done((bf16[8,32,2048]{2,1,0:T(8,128)(2,1)}, bf16[8,32,2048]{2,1,0:T(8,128)(2,1)}, u32[]{:S(2)}, u32[]{:S(2)}) %collective-permute-start.55) | collective-permute-done | bytes 1048608 | tf_op jit(solution)/shard_map/ppermute | solution.py:303
  725.7 16.7 %collective-permute-done.70 = f32[8,448]{1,0:T(8,128)S(1)} collective-permute-done((f32[8,448]{1,0:T(8,128)S(1)}, f32[8,448]{1,0:T(8,128)S(1)}, u32[]{:S(2)}, u32[]{:S(2)}) %collective-permute-start.70) | collective-permute-done | bytes 14368 | tf_op jit(solution)/shard_map/ppermute | solution.py:303
  783.5 7.5 collective-permute-done.77
  (485 shorter events, 479.6 us)
Async XLA Ops:
  7.2 239.6 %all-gather.4.cloned.1.call-start = ((), (), s32[]{:S(2)}) async-start(), calls=%async_computation | async-start | bytes 8650752 | tf_op jit(solution)/shard_map/all_gather | solution.py:1051
  7.9 248.0 %all-gather.6.cloned.1.call-start = ((), (), s32[]{:S(2)}) async-start(), calls=%async_computation.1 | async-start | bytes 8650752 | tf_op jit(solution)/shard_map/all_gather | solution.py:1051
  8.7 307.4 %all-gather.8.cloned.1.call-start = ((), (), s32[]{:S(2)}) async-start(), calls=%async_computation.2 | async-start | bytes 8650752 | tf_op jit(solution)/shard_map/all_gather | solution.py:1051
  16.4 29.3 %collective-permute-start.1 = (bf16[2,32,2176]{2,1,0:T(8,128)(2,1)S(1)}, bf16[2,32,2176]{2,1,0:T(8,128)(2,1)S(1)}, u32[]{:S(2)}, u32[]{:S(2)}) collective-permute-start(bf16[2,32,2176]{2,1,0:T(8,128)(2,1)S(1)} %pad_maximum_fusion.refs_0_), channel_id=1, source_target_pairs={{0,8},{1,9},{2,10},{3,11},{4,12},{5,13},{6,14},{7,15},{8,0},{9,1},... | collective-permute-start | bytes 835592 | tf_op jit(solution)/shard_map/ppermute | solution.py:303
  16.4 29.3 %collective-permute-start = (bf16[2,32,2176]{2,1,0:T(8,128)(2,1)S(1)}, bf16[2,32,2176]{2,1,0:T(8,128)(2,1)S(1)}, u32[]{:S(2)}, u32[]{:S(2)}) collective-permute-start(bf16[2,32,2176]{2,1,0:T(8,128)(2,1)S(1)} %pad_maximum_fusion.refs_0_), channel_id=1, source_target_pairs={{0,4},{1,5},{2,6},{3,7},{4,0},{5,1},{6,2},{7,3},{8,12},{9,13},{10,... | collective-permute-start | bytes 835592 | tf_op jit(solution)/shard_map/ppermute | solution.py:303
  72.1 48.9 %collective-permute-start.6 = (bf16[8,32,2176]{2,1,0:T(8,128)(2,1)}, bf16[8,32,2176]{2,1,0:T(8,128)(2,1)S(1)}, u32[]{:S(2)}, u32[]{:S(2)}) collective-permute-start(bf16[8,32,2176]{2,1,0:T(8,128)(2,1)} %bitcast.262), channel_id=1, source_target_pairs={{0,2},{1,3},{2,0},{3,1},{4,6},{5,7},{6,4},{7,5},{8,10},{9,11},{10,... | collective-permute-start | bytes 3342344 | tf_op jit(solution)/shard_map/ppermute | solution.py:303
  77.0 44.0 %collective-permute-start.5 = (bf16[8,32,2176]{2,1,0:T(8,128)(2,1)}, bf16[8,32,2176]{2,1,0:T(8,128)(2,1)S(1)}, u32[]{:S(2)}, u32[]{:S(2)}) collective-permute-start(bf16[8,32,2176]{2,1,0:T(8,128)(2,1)} %bitcast.264), channel_id=1, source_target_pairs={{0,1},{1,0},{2,3},{3,2},{4,5},{5,4},{6,7},{7,6},{8,9},{9,8},{10,11... | collective-permute-start | bytes 3342344 | tf_op jit(solution)/shard_map/ppermute | solution.py:303
  81.2 39.8 %collective-permute-start.8 = (bf16[2,32,2048]{2,1,0:T(8,128)(2,1)S(1)}, bf16[2,32,2048]{2,1,0:T(8,128)(2,1)S(1)}, u32[]{:S(2)}, u32[]{:S(2)}) collective-permute-start(bf16[2,32,2048]{2,1,0:T(8,128)(2,1)S(1)} %pad_maximum_fusion.1.refs_0_), channel_id=1, source_target_pairs={{0,8},{1,9},{2,10},{3,11},{4,12},{5,13},{6,14},{7,15},{8,0},{9,1},... | collective-permute-start | bytes 786440 | tf_op jit(solution)/shard_map/ppermute | solution.py:303
  81.2 39.8 %collective-permute-start.7 = (bf16[2,32,2048]{2,1,0:T(8,128)(2,1)S(1)}, bf16[2,32,2048]{2,1,0:T(8,128)(2,1)S(1)}, u32[]{:S(2)}, u32[]{:S(2)}) collective-permute-start(bf16[2,32,2048]{2,1,0:T(8,128)(2,1)S(1)} %pad_maximum_fusion.1.refs_0_), channel_id=1, source_target_pairs={{0,4},{1,5},{2,6},{3,7},{4,0},{5,1},{6,2},{7,3},{8,12},{9,13},{10,... | collective-permute-start | bytes 786440 | tf_op jit(solution)/shard_map/ppermute | solution.py:303
  138.8 48.6 %collective-permute-start.18 = (bf16[1,128,1024]{2,1,0:T(8,128)(2,1)S(1)}, bf16[1,128,1024]{2,1,0:T(8,128)(2,1)S(1)}, u32[]{:S(2)}, u32[]{:S(2)}) collective-permute-start(bf16[1,128,1024]{2,1,0:T(8,128)(2,1)S(1)} %bitcast.340), channel_id=1, source_target_pairs={{0,12},{1,13},{2,14},{3,15},{4,8},{5,9},{6,10},{7,11},{8,4},{9,5},... | collective-permute-start | bytes 786440 | tf_op jit(solution)/shard_map/ppermute | solution.py:303
  149.8 37.6 %collective-permute-start.17 = (bf16[1,128,1024]{2,1,0:T(8,128)(2,1)S(1)}, bf16[1,128,1024]{2,1,0:T(8,128)(2,1)}, u32[]{:S(2)}, u32[]{:S(2)}) collective-permute-start(bf16[1,128,1024]{2,1,0:T(8,128)(2,1)S(1)} %bitcast.341), channel_id=1, source_target_pairs={{0,8},{1,9},{2,10},{3,11},{4,12},{5,13},{6,14},{7,15},{8,0},{9,1},... | collective-permute-start | bytes 786440 | tf_op jit(solution)/shard_map/ppermute | solution.py:303
  151.0 36.4 %collective-permute-start.16 = (bf16[1,128,1024]{2,1,0:T(8,128)(2,1)S(1)}, bf16[1,128,1024]{2,1,0:T(8,128)(2,1)}, u32[]{:S(2)}, u32[]{:S(2)}) collective-permute-start(bf16[1,128,1024]{2,1,0:T(8,128)(2,1)S(1)} %bitcast.342), channel_id=1, source_target_pairs={{0,4},{1,5},{2,6},{3,7},{4,0},{5,1},{6,2},{7,3},{8,12},{9,13},{10,... | collective-permute-start | bytes 786440 | tf_op jit(solution)/shard_map/ppermute | solution.py:303
  158.6 28.8 %collective-permute-start.15 = (bf16[8,32,2048]{2,1,0:T(8,128)(2,1)}, bf16[8,32,2048]{2,1,0:T(8,128)(2,1)S(1)}, u32[]{:S(2)}, u32[]{:S(2)}) collective-permute-start(bf16[8,32,2048]{2,1,0:T(8,128)(2,1)} %bitcast.294), channel_id=1, source_target_pairs={{0,2},{1,3},{2,0},{3,1},{4,6},{5,7},{6,4},{7,5},{8,10},{9,11},{10,... | collective-permute-start | bytes 3145736 | tf_op jit(solution)/shard_map/ppermute | solution.py:303
  160.1 32.4 %collective-permute-start.14 = (bf16[8,32,2048]{2,1,0:T(8,128)(2,1)}, bf16[8,32,2048]{2,1,0:T(8,128)(2,1)S(1)}, u32[]{:S(2)}, u32[]{:S(2)}) collective-permute-start(bf16[8,32,2048]{2,1,0:T(8,128)(2,1)} %bitcast.292), channel_id=1, source_target_pairs={{0,1},{1,0},{2,3},{3,2},{4,5},{5,4},{6,7},{7,6},{8,9},{9,8},{10,11... | collective-permute-start | bytes 3145736 | tf_op jit(solution)/shard_map/ppermute | solution.py:303
  203.2 29.9 %collective-permute-start.20 = (bf16[16,32,2048]{2,1,0:T(8,128)(2,1)}, bf16[16,32,2048]{2,1,0:T(8,128)(2,1)}, u32[]{:S(2)}, u32[]{:S(2)}) collective-permute-start(bf16[16,32,2048]{2,1,0:T(8,128)(2,1)} %bitcast.249), channel_id=1, source_target_pairs={{0,16},{1,17},{2,18},{3,19},{4,20},{5,21},{6,22},{7,23},{8,24},{9,... | collective-permute-start | bytes 6291464 | tf_op jit(solution)/shard_map/ppermute | solution.py:303
  203.2 29.9 %collective-permute-start.19 = (bf16[16,32,2048]{2,1,0:T(8,128)(2,1)}, bf16[16,32,2048]{2,1,0:T(8,128)(2,1)}, u32[]{:S(2)}, u32[]{:S(2)}) collective-permute-start(bf16[16,32,2048]{2,1,0:T(8,128)(2,1)} %bitcast.251), channel_id=1, source_target_pairs={{0,16},{1,17},{2,18},{3,19},{4,20},{5,21},{6,22},{7,23},{8,24},{9,... | collective-permute-start | bytes 6291464 | tf_op jit(solution)/shard_map/ppermute | solution.py:303
  206.0 27.2 %collective-permute-start.21 = (bf16[4,128,1024]{2,1,0:T(8,128)(2,1)}, bf16[4,128,1024]{2,1,0:T(8,128)(2,1)S(1)}, u32[]{:S(2)}, u32[]{:S(2)}) collective-permute-start(bf16[4,128,1024]{2,1,0:T(8,128)(2,1)} %bitcast.296), channel_id=1, source_target_pairs={{0,1},{1,0},{2,3},{3,2},{4,5},{5,4},{6,7},{7,6},{8,9},{9,8},{10,11... | collective-permute-start | bytes 3145736 | tf_op jit(solution)/shard_map/ppermute | solution.py:303
  237.9 64.6 %collective-permute-start.22 = (bf16[8,128,1024]{2,1,0:T(8,128)(2,1)}, bf16[8,128,1024]{2,1,0:T(8,128)(2,1)}, u32[]{:S(2)}, u32[]{:S(2)}) collective-permute-start(bf16[8,128,1024]{2,1,0:T(8,128)(2,1)} %bitcast.253), channel_id=1, source_target_pairs={{0,2},{1,3},{2,0},{3,1},{4,6},{5,7},{6,4},{7,5},{8,10},{9,11},{10,... | collective-permute-start | bytes 6291464 | tf_op jit(solution)/shard_map/ppermute | solution.py:303
  525.8 26.8 %collective-permute-start.41 = (bf16[8,32,2048]{2,1,0:T(8,128)(2,1)}, bf16[8,32,2048]{2,1,0:T(8,128)(2,1)}, u32[]{:S(2)}, u32[]{:S(2)}) collective-permute-start(bf16[8,32,2048]{2,1,0:T(8,128)(2,1)} %get-tuple-element.451), channel_id=1, source_target_pairs={{0,1},{1,0},{2,3},{3,2},{4,5},{5,4},{6,7},{7,6},{8,9},{9,8},{10,11... | collective-permute-start | bytes 3145736 | tf_op jit(solution)/shard_map/ppermute | solution.py:303
  593.9 29.6 %collective-permute-start.51 = (bf16[8,128,512]{2,1,0:T(8,128)(2,1)}, bf16[8,128,512]{2,1,0:T(8,128)(2,1)}, u32[]{:S(2)}, u32[]{:S(2)}) collective-permute-start(bf16[8,128,512]{2,1,0:T(8,128)(2,1)} %get-tuple-element.492), channel_id=1, source_target_pairs={{0,2},{1,3},{2,0},{3,1},{4,6},{5,7},{6,4},{7,5},{8,10},{9,11},{10,... | collective-permute-start | bytes 3145736 | tf_op jit(solution)/shard_map/ppermute | solution.py:303
  595.2 28.3 %collective-permute-start.52 = (bf16[8,128,512]{2,1,0:T(8,128)(2,1)}, bf16[8,128,512]{2,1,0:T(8,128)(2,1)}, u32[]{:S(2)}, u32[]{:S(2)}) collective-permute-start(bf16[8,128,512]{2,1,0:T(8,128)(2,1)} %get-tuple-element.493), channel_id=1, source_target_pairs={{0,1},{1,0},{2,3},{3,2},{4,5},{5,4},{6,7},{7,6},{8,9},{9,8},{10,11... | collective-permute-start | bytes 3145736 | tf_op jit(solution)/shard_map/ppermute | solution.py:303
  629.0 32.7 %collective-permute-start.55 = (bf16[8,32,2048]{2,1,0:T(8,128)(2,1)}, bf16[8,32,2048]{2,1,0:T(8,128)(2,1)}, u32[]{:S(2)}, u32[]{:S(2)}) collective-permute-start(bf16[8,32,2048]{2,1,0:T(8,128)(2,1)} %get-tuple-element.515), channel_id=1, source_target_pairs={{0,2},{1,3},{2,0},{3,1},{4,6},{5,7},{6,4},{7,5},{8,10},{9,11},{10,... | collective-permute-start | bytes 3145736 | tf_op jit(solution)/shard_map/ppermute | solution.py:303
  629.9 31.8 %collective-permute-start.56 = (bf16[8,32,2048]{2,1,0:T(8,128)(2,1)}, bf16[8,32,2048]{2,1,0:T(8,128)(2,1)}, u32[]{:S(2)}, u32[]{:S(2)}) collective-permute-start(bf16[8,32,2048]{2,1,0:T(8,128)(2,1)} %get-tuple-element.516), channel_id=1, source_target_pairs={{0,1},{1,0},{2,3},{3,2},{4,5},{5,4},{6,7},{7,6},{8,9},{9,8},{10,11... | collective-permute-start | bytes 3145736 | tf_op jit(solution)/shard_map/ppermute | solution.py:303
  631.5 30.1 %collective-permute-start.57 = (bf16[512,1024]{1,0:T(8,128)(2,1)}, bf16[512,1024]{1,0:T(8,128)(2,1)}, u32[]{:S(2)}, u32[]{:S(2)}) collective-permute-start(bf16[512,1024]{1,0:T(8,128)(2,1)} %half_away.17), channel_id=1, source_target_pairs={{0,16},{1,17},{2,18},{3,19},{4,20},{5,21},{6,22},{7,23},{8,24},{9,... | collective-permute-start | bytes 3145736 | tf_op jit(solution)/shard_map/ppermute | solution.py:303
  (144 other events, 1891.2 us)
Sparse Core Ops, SparseCore 0:
  10.9 111.0 all-gather.3
  124.8 92.0 all-gather.5
  219.8 96.2 all-gather.7
